TPU v7x, 512 devices: a whole 4x4x16 slice. The times are simulated.
512 devices in a mesh: ctx: 32 (over x, z_hi, core), head: 16 (over y, z_lo).
Axes of the slice: x: 4, y: 4, z: 16 (z_hi: 4, z_lo: 4; z = z_hi * 4 + z_lo), core: 2. Of those that a mesh axis runs over, the one named last changes fastest.
Arguments:
- query_states: bfloat16 [16384, 4096], P(('ctx', 'head')), may hold values from -6 to 6
- key_states: bfloat16 [16384, 2048], P(('ctx', 'head')), may hold values from -6 to 6
- value_states: bfloat16 [16384, 2048], P(('ctx', 'head')), may hold values from -6 to 6
- grad_out: bfloat16 [16384, 4096], P(('ctx', 'head')), may hold values from -6 to 6
- pack_table: int32 [8, 4], replicated, may hold values from 0 to 16384, as said below
Outputs:
- grad_query: bfloat16 [16384, 4096], P(('ctx', 'head'))
- grad_key: bfloat16 [16384, 2048], P(('ctx', 'head'))
- grad_value: bfloat16 [16384, 2048], P(('ctx', 'head'))
Inputs may be any that keep to these rules, and one draw needn't show every extreme that they name: `pack_table`: one row a pack, in order of the stream: start, prompt end (the chosen response's start), rejected response's start, end. The packs tile 0 to 16384 without gaps; inner pack boundaries lie within 512 of the multiples of 2048. Each response has 128 to 512 tokens; some response has exactly 512, and with two or more packs some chosen and some rejected response both do.
All inputs are finite; a program needn't handle non-finite values.
Results may differ from a plain program's by a relative error of at most 0.006.
Values may be sent and summed in bfloat16 or wider, within the bound.
No kernel may reach another device: no remote copies, remote signals or barrier semaphores. Data moves between devices by JAX's collectives and lax.ppermute only.
A program may use at most 64 MiB of HBM per device.

v0:
```python
import jax
import jax.numpy as jnp
from jax import lax
from jax.sharding import PartitionSpec as P

HEAD_DIM = 128
WINDOW = 4096
RESP_MOST = 512
PACK_MEAN = 2048


soft_cap = 50.0
score_scale = 1.0 / 12.0


def shifted(value, axis, by):
    peers = lax.axis_size(axis)
    pairs = [(i, i + by) for i in range(peers) if 0 <= i + by < peers]
    return lax.ppermute(value, axis, pairs)


def shifted_2(block, axis, distance):
    devices = range(lax.axis_size(axis))
    route = [((i - distance) % len(devices), i) for i in devices]
    return lax.ppermute(block, axis, route)


def token_info(positions, pack_table):
    pack_count = pack_table.shape[0]
    inside = (positions[:, None] >= pack_table[None, :, 0]).astype(jnp.int32)
    pack_id = jnp.sum(inside, axis=1) - 1
    selected = (pack_id[:, None] == jnp.arange(pack_count, dtype=jnp.int32)[None, :]).astype(
        jnp.int32
    )
    bounds = jnp.sum(selected[:, :, None] * pack_table[None, :, :], axis=1)
    token_role = (positions >= bounds[:, 1]).astype(jnp.int32) + (positions >= bounds[:, 2]).astype(
        jnp.int32
    )
    logical = (
        jnp.where(token_role == 2, positions - bounds[:, 2] + bounds[:, 1], positions)
        - bounds[:, 0]
    )
    return (pack_id, token_role, logical)


def allowed(query_info, key_info):
    same_pack = query_info[0][:, None] == key_info[0][None, :]
    distance = query_info[2][:, None] - key_info[2][None, :]
    inside = (distance >= 0) & (distance < WINDOW)
    crossing = query_info[1][:, None] + key_info[1][None, :] == 3
    return same_pack & inside & jnp.logical_not(crossing)


def capped_of(query_heads, key_block):
    raw_score = (
        jnp.einsum("qgd,kd->gqk", query_heads, key_block, preferred_element_type=jnp.float32)
        * score_scale
    )
    return soft_cap * jnp.tanh(raw_score / soft_cap)


def local(query_states, key_states, value_states, grad_out, pack_table):
    queries, keys_here, values_here, grads_here = (
        lax.all_to_all(query_states, "head", split_axis=1, concat_axis=0, tiled=True),
        lax.all_to_all(key_states, "head", split_axis=1, concat_axis=0, tiled=True),
        lax.all_to_all(value_states, "head", split_axis=1, concat_axis=0, tiled=True),
        lax.all_to_all(grad_out, "head", split_axis=1, concat_axis=0, tiled=True),
    )
    rows_here = keys_here.shape[0]
    per_group = queries.shape[1] // HEAD_DIM
    ctx_count = lax.axis_size("ctx")
    ctx_index = lax.axis_index("ctx")
    span = min(WINDOW + RESP_MOST, PACK_MEAN + PACK_MEAN // 2)
    reach = min(ctx_count - 1, (span + rows_here - 2) // rows_here)
    query_heads = queries.reshape(rows_here, per_group, HEAD_DIM)
    grad_heads = grads_here.reshape(rows_here, per_group, HEAD_DIM)
    stacked = jnp.stack([keys_here, values_here])
    local_rows = jnp.arange(rows_here, dtype=jnp.int32)
    query_info = token_info(ctx_index * rows_here + local_rows, pack_table)
    blocks = [stacked]
    current = stacked
    for offset in range(1, reach + 1):
        current = shifted(current, "ctx", 1)
        blocks.append(current)
    visibles = []
    row_total = jnp.zeros((per_group, rows_here), jnp.float32)
    weighted = jnp.zeros((rows_here, per_group, HEAD_DIM), jnp.float32)
    for offset in range(reach + 1):
        key_info = token_info((ctx_index - offset) * rows_here + local_rows, pack_table)
        visible = allowed(query_info, key_info)
        visibles.append(visible)
        capped = capped_of(query_heads, blocks[offset][0])
        expo = jnp.where(visible[None], jnp.exp(capped), 0.0)
        row_total = row_total + jnp.sum(expo, axis=2)
        weighted = weighted + jnp.einsum(
            "gqk,kd->qgd",
            expo.astype(jnp.bfloat16),
            blocks[offset][1],
            preferred_element_type=jnp.float32,
        )
    attn_out = weighted / jnp.transpose(row_total)[:, :, None]
    row_delta = jnp.sum(grad_heads.astype(jnp.float32) * attn_out, axis=2)
    delta_heads = jnp.transpose(row_delta)[:, :, None]
    grad_query_acc = jnp.zeros((rows_here, per_group, HEAD_DIM), jnp.float32)
    partials = []
    for offset in range(reach + 1):
        key_block = blocks[offset][0]
        value_block = blocks[offset][1]
        capped = capped_of(query_heads, key_block)
        prob = jnp.where(visibles[offset][None], jnp.exp(capped), 0.0) / row_total[:, :, None]
        dprob = jnp.einsum(
            "qgd,kd->gqk", grad_heads, value_block, preferred_element_type=jnp.float32
        )
        ratio = capped / soft_cap
        dscore = (prob * (dprob - delta_heads) * (1.0 - ratio * ratio) * score_scale).astype(
            jnp.bfloat16
        )
        grad_query_acc = grad_query_acc + jnp.einsum(
            "gqk,kd->qgd", dscore, key_block, preferred_element_type=jnp.float32
        )
        part_key = jnp.einsum(
            "gqk,qgd->kd", dscore, query_heads, preferred_element_type=jnp.float32
        )
        part_value = jnp.einsum(
            "gqk,qgd->kd", prob.astype(jnp.bfloat16), grad_heads, preferred_element_type=jnp.float32
        )
        partials.append(jnp.stack([part_key, part_value]))
    carried = partials[0]
    for offset in range(1, reach + 1):
        carried = shifted_2(carried, "ctx", 1)
        carried = carried + partials[offset]
    summed = shifted_2(carried.astype(jnp.bfloat16), "ctx", -reach).astype(carried.dtype)
    grad_query = grad_query_acc.reshape(rows_here, per_group * HEAD_DIM).astype(jnp.bfloat16)
    grad_key = summed[0].astype(jnp.bfloat16)
    grad_value = summed[1].astype(jnp.bfloat16)
    result = (
        lax.all_to_all(grad_query, "head", split_axis=0, concat_axis=1, tiled=True),
        lax.all_to_all(grad_key, "head", split_axis=0, concat_axis=1, tiled=True),
        lax.all_to_all(grad_value, "head", split_axis=0, concat_axis=1, tiled=True),
    )
    return (result[0], result[1], result[2])


def solution(mesh):
    return jax.shard_map(
        local,
        mesh=mesh,
        in_specs=(
            P(("ctx", "head"), None),
            P(("ctx", "head"), None),
            P(("ctx", "head"), None),
            P(("ctx", "head"), None),
            P(),
        ),
        out_specs=(P(("ctx", "head"), None), P(("ctx", "head"), None), P(("ctx", "head"), None)),
        check_vma=False,
    )
```

profile of v0, /device:TPU:4, one launch (start us, length us, event | category | flops | bytes accessed | tf_op | source)
XLA Modules:
  0.0 380.2 jit_solution(8894933694529405906)
XLA Ops:
  2.2 8.6 %all-to-all-start = ((bf16[32,16,128]{2,0,1:T(8,128)(2,1)}), bf16[32,16,128]{2,0,1:T(8,128)(2,1)S(1)}, u32[]{:S(2)}, u32[]{:S(2)}) async-start(bf16[32,16,128]{2,0,1:T(8,128)(2,1)} %copy_bitcast_fusion.5), calls=%async_computation | async-start | bytes 262144 | tf_op jit(solution)/shard_map/all_to_all | solution.py:65
  14.5 4.8 %all-to-all-done = bf16[32,16,128]{2,0,1:T(8,128)(2,1)S(1)} async-done(((bf16[32,16,128]{2,0,1:T(8,128)(2,1)}), bf16[32,16,128]{2,0,1:T(8,128)(2,1)S(1)}, u32[]{:S(2)}, u32[]{:S(2)}) %all-to-all-start) | async-done | bytes 131104 | tf_op jit(solution)/shard_map/all_to_all | solution.py:65
  19.3 3.5 all-to-all-start.2
  24.5 6.6 %all-to-all-done.2 = bf16[32,16,128]{2,0,1:T(8,128)(2,1)S(1)} async-done(((bf16[32,16,128]{2,0,1:T(8,128)(2,1)}), bf16[32,16,128]{2,0,1:T(8,128)(2,1)S(1)}, u32[]{:S(2)}, u32[]{:S(2)}) %all-to-all-start.2) | async-done | bytes 131104 | tf_op jit(solution)/shard_map/all_to_all | solution.py:66
  31.1 3.5 all-to-all-start.1
  35.5 8.3 %all-to-all-done.1 = bf16[32,16,256]{2,0,1:T(8,128)(2,1)S(1)} async-done(((bf16[32,16,256]{2,0,1:T(8,128)(2,1)}), bf16[32,16,256]{2,0,1:T(8,128)(2,1)S(1)}, u32[]{:S(2)}, u32[]{:S(2)}) %all-to-all-start.1) | async-done | bytes 262176 | tf_op jit(solution)/shard_map/all_to_all | solution.py:64
  43.8 3.5 all-to-all-start.3
  47.3 2.9 fusion.64
  50.2 1.9 collective-permute-start
  53.4 9.7 %collective-permute-done = bf16[2,512,128]{2,1,0:T(8,128)(2,1)S(1)} collective-permute-done((bf16[2,512,128]{2,1,0:T(8,128)(2,1)S(1)}, bf16[2,512,128]{2,1,0:T(8,128)(2,1)S(1)}, u32[]{:S(2)}, u32[]{:S(2)}) %collective-permute-start) | collective-permute-done | bytes 262176 | tf_op jit(solution)/shard_map/ppermute | solution.py:19
  63.0 9.9 %collective-permute-start.1 = (bf16[2,512,128]{2,1,0:T(8,128)(2,1)S(1)}, bf16[2,512,128]{2,1,0:T(8,128)(2,1)}, u32[]{:S(2)}, u32[]{:S(2)}) collective-permute-start(bf16[2,512,128]{2,1,0:T(8,128)(2,1)S(1)} %collective-permute-done), channel_id=1, source_target_pairs={{0,16},{16,32},{32,48},{48,64},{64,80},{80,96},{96,112},{112,128},... | collective-permute-start | bytes 786440 | tf_op jit(solution)/shard_map/ppermute | solution.py:19
  76.6 4.3 %collective-permute-done.1 = bf16[2,512,128]{2,1,0:T(8,128)(2,1)} collective-permute-done((bf16[2,512,128]{2,1,0:T(8,128)(2,1)S(1)}, bf16[2,512,128]{2,1,0:T(8,128)(2,1)}, u32[]{:S(2)}, u32[]{:S(2)}) %collective-permute-start.1) | collective-permute-done | bytes 262176 | tf_op jit(solution)/shard_map/ppermute | solution.py:19
  80.9 12.0 %collective-permute-start.2 = (bf16[2,512,128]{2,1,0:T(8,128)(2,1)}, bf16[2,512,128]{2,1,0:T(8,128)(2,1)S(1)}, u32[]{:S(2)}, u32[]{:S(2)}) collective-permute-start(bf16[2,512,128]{2,1,0:T(8,128)(2,1)} %collective-permute-done.1), channel_id=1, source_target_pairs={{0,16},{16,32},{32,48},{48,64},{64,80},{80,96},{96,112},{112,128},... | collective-permute-start | bytes 786440 | tf_op jit(solution)/shard_map/ppermute | solution.py:19
  96.4 10.9 %collective-permute-start.3 = (bf16[2,512,128]{2,1,0:T(8,128)(2,1)S(1)}, bf16[2,512,128]{2,1,0:T(8,128)(2,1)S(1)}, u32[]{:S(2)}, u32[]{:S(2)}) collective-permute-start(bf16[2,512,128]{2,1,0:T(8,128)(2,1)S(1)} %collective-permute-done.2), channel_id=1, source_target_pairs={{0,16},{16,32},{32,48},{48,64},{64,80},{80,96},{96,112},{112,128},... | collective-permute-start | bytes 786440 | tf_op jit(solution)/shard_map/ppermute | solution.py:19
  109.0 10.7 %collective-permute-start.4 = (bf16[2,512,128]{2,1,0:T(8,128)(2,1)S(1)}, bf16[2,512,128]{2,1,0:T(8,128)(2,1)S(1)}, u32[]{:S(2)}, u32[]{:S(2)}) collective-permute-start(bf16[2,512,128]{2,1,0:T(8,128)(2,1)S(1)} %collective-permute-done.3), channel_id=1, source_target_pairs={{0,16},{16,32},{32,48},{48,64},{64,80},{80,96},{96,112},{112,128},... | collective-permute-start | bytes 786440 | tf_op jit(solution)/shard_map/ppermute | solution.py:19
  121.5 11.2 %collective-permute-start.5 = (bf16[2,512,128]{2,1,0:T(8,128)(2,1)S(1)}, bf16[2,512,128]{2,1,0:T(8,128)(2,1)S(1)}, u32[]{:S(2)}, u32[]{:S(2)}) collective-permute-start(bf16[2,512,128]{2,1,0:T(8,128)(2,1)S(1)} %collective-permute-done.4), channel_id=1, source_target_pairs={{0,16},{16,32},{32,48},{48,64},{64,80},{80,96},{96,112},{112,128},... | collective-permute-start | bytes 786440 | tf_op jit(solution)/shard_map/ppermute | solution.py:19
  139.0 13.1 %collective-permute-start.6 = (f32[2,512,128]{2,1,0:T(8,128)S(1)}, f32[2,512,128]{2,1,0:T(8,128)S(1)}, u32[]{:S(2)}, u32[]{:S(2)}) collective-permute-start(f32[2,512,128]{2,1,0:T(8,128)S(1)} %pad_maximum_fusion), channel_id=1, source_target_pairs={{496,0},{0,16},{16,32},{32,48},{48,64},{64,80},{80,96},{96,112},{1... | collective-permute-start | bytes 1572872 | tf_op jit(solution)/shard_map/ppermute | solution.py:25
  153.3 2.1 fusion.13
  165.8 30.7 %collective-permute-start.7 = (f32[2,512,128]{2,1,0:T(8,128)S(1)}, f32[2,512,128]{2,1,0:T(8,128)S(1)}, u32[]{:S(2)}, u32[]{:S(2)}) collective-permute-start(f32[2,512,128]{2,1,0:T(8,128)S(1)} %maximum_add_fusion), channel_id=1, source_target_pairs={{496,0},{0,16},{16,32},{32,48},{48,64},{64,80},{80,96},{96,112},{1... | collective-permute-start | bytes 1572872 | tf_op jit(solution)/shard_map/ppermute | solution.py:25
  197.9 23.5 %collective-permute-start.8 = (f32[2,512,128]{2,1,0:T(8,128)S(1)}, f32[2,512,128]{2,1,0:T(8,128)S(1)}, u32[]{:S(2)}, u32[]{:S(2)}) collective-permute-start(f32[2,512,128]{2,1,0:T(8,128)S(1)} %maximum_add_fusion.1), channel_id=1, source_target_pairs={{496,0},{0,16},{16,32},{32,48},{48,64},{64,80},{80,96},{96,112},{1... | collective-permute-start | bytes 1572872 | tf_op jit(solution)/shard_map/ppermute | solution.py:25
  222.6 8.8 %collective-permute-done.8 = f32[2,512,128]{2,1,0:T(8,128)S(1)} collective-permute-done((f32[2,512,128]{2,1,0:T(8,128)S(1)}, f32[2,512,128]{2,1,0:T(8,128)S(1)}, u32[]{:S(2)}, u32[]{:S(2)}) %collective-permute-start.8) | collective-permute-done | bytes 524320 | tf_op jit(solution)/shard_map/ppermute | solution.py:25
  231.5 9.7 %collective-permute-start.9 = (f32[2,512,128]{2,1,0:T(8,128)S(1)}, f32[2,512,128]{2,1,0:T(8,128)S(1)}, u32[]{:S(2)}, u32[]{:S(2)}) collective-permute-start(f32[2,512,128]{2,1,0:T(8,128)S(1)} %maximum_add_fusion.2), channel_id=1, source_target_pairs={{496,0},{0,16},{16,32},{32,48},{48,64},{64,80},{80,96},{96,112},{1... | collective-permute-start | bytes 1572872 | tf_op jit(solution)/shard_map/ppermute | solution.py:25
  242.3 17.4 %collective-permute-done.9 = f32[2,512,128]{2,1,0:T(8,128)S(1)} collective-permute-done((f32[2,512,128]{2,1,0:T(8,128)S(1)}, f32[2,512,128]{2,1,0:T(8,128)S(1)}, u32[]{:S(2)}, u32[]{:S(2)}) %collective-permute-start.9) | collective-permute-done | bytes 524320 | tf_op jit(solution)/shard_map/ppermute | solution.py:25
  259.7 1.9 collective-permute-start.10
  263.3 23.3 %all-to-all-start.4 = ((bf16[16,32,256]{2,1,0:T(8,128)(2,1)}), bf16[16,32,256]{2,1,0:T(8,128)(2,1)S(1)}, u32[]{:S(2)}, u32[]{:S(2)}) async-start(bf16[16,32,256]{2,1,0:T(8,128)(2,1)} %convert_element_type.355), calls=%async_computation.4 | async-start | bytes 524288 | tf_op jit(solution)/shard_map/all_to_all | solution.py:137
  286.6 2.5 convolution_bitcast_fusion.16
  289.2 1.9 collective-permute-start.11
  292.3 30.2 %collective-permute-done.11 = f32[2,512,128]{2,1,0:T(8,128)S(1)} collective-permute-done((f32[2,512,128]{2,1,0:T(8,128)S(1)}, f32[2,512,128]{2,1,0:T(8,128)S(1)}, u32[]{:S(2)}, u32[]{:S(2)}) %collective-permute-start.11) | collective-permute-done | bytes 524320 | tf_op jit(solution)/shard_map/ppermute | solution.py:25
  324.5 16.9 %collective-permute-done.12 = bf16[2,512,128]{2,1,0:T(8,128)(2,1)S(1)} collective-permute-done((bf16[2,512,128]{2,1,0:T(8,128)(2,1)S(1)}, bf16[2,512,128]{2,1,0:T(8,128)(2,1)S(1)}, u32[]{:S(2)}, u32[]{:S(2)}) %collective-permute-start.12) | collective-permute-done | bytes 262176 | tf_op jit(solution)/shard_map/ppermute | solution.py:25
  342.1 25.6 %all_to_all.118 = bf16[16,32,128]{2,1,0:T(8,128)(2,1)S(1)} all-to-all(bf16[16,32,128]{2,1,0:T(8,128)(2,1)S(1)} %bitcast.486), channel_id=1, replica_groups=mesh['ctx'=32,'head'=16] {'head'}, dimensions={0} | all-to-all | bytes 262144 | tf_op jit(solution)/shard_map/all_to_all | solution.py:139
  367.7 3.5 all-to-all-start.5
  372.6 7.0 %all-to-all-done.5 = bf16[16,32,128]{2,1,0:T(8,128)(2,1)S(1)} async-done(((bf16[16,32,128]{2,1,0:T(8,128)(2,1)}), bf16[16,32,128]{2,1,0:T(8,128)(2,1)S(1)}, u32[]{:S(2)}, u32[]{:S(2)}) %all-to-all-start.5) | async-done | bytes 131104 | tf_op jit(solution)/shard_map/all_to_all | solution.py:138
  (126 shorter events, 48.2 us)
Async XLA Ops:
  0.6 0.9 copy-start
  1.5 33.1 %copy-start.1 = (bf16[32,4096]{1,0:T(8,128)(2,1)S(1)}, bf16[32,4096]{1,0:T(8,128)(2,1)}, u32[]{:S(2)}) copy-start(bf16[32,4096]{1,0:T(8,128)(2,1)} %param.8) | copy-start | bytes 786436
  2.2 17.0 %all-to-all-start = ((bf16[32,16,128]{2,0,1:T(8,128)(2,1)}), bf16[32,16,128]{2,0,1:T(8,128)(2,1)S(1)}, u32[]{:S(2)}, u32[]{:S(2)}) async-start(bf16[32,16,128]{2,0,1:T(8,128)(2,1)} %copy_bitcast_fusion.5), calls=%async_computation | async-start | bytes 262144 | tf_op jit(solution)/shard_map/all_to_all | solution.py:65
  19.3 11.9 %all-to-all-start.2 = ((bf16[32,16,128]{2,0,1:T(8,128)(2,1)}), bf16[32,16,128]{2,0,1:T(8,128)(2,1)S(1)}, u32[]{:S(2)}, u32[]{:S(2)}) async-start(bf16[32,16,128]{2,0,1:T(8,128)(2,1)} %copy_bitcast_fusion.4), calls=%async_computation.2 | async-start | bytes 262144 | tf_op jit(solution)/shard_map/all_to_all | solution.py:66
  31.1 12.6 %all-to-all-start.1 = ((bf16[32,16,256]{2,0,1:T(8,128)(2,1)}), bf16[32,16,256]{2,0,1:T(8,128)(2,1)S(1)}, u32[]{:S(2)}, u32[]{:S(2)}) async-start(bf16[32,16,256]{2,0,1:T(8,128)(2,1)} %bitcast.476), calls=%async_computation.1 | async-start | bytes 524288 | tf_op jit(solution)/shard_map/all_to_all | solution.py:64
  43.8 29.3 %all-to-all-start.3 = ((bf16[32,16,256]{2,0,1:T(8,128)(2,1)}), bf16[32,16,256]{2,0,1:T(8,128)(2,1)S(1)}, u32[]{:S(2)}, u32[]{:S(2)}) async-start(bf16[32,16,256]{2,0,1:T(8,128)(2,1)} %bitcast.475), calls=%async_computation.3 | async-start | bytes 524288 | tf_op jit(solution)/shard_map/all_to_all | solution.py:67
  50.2 108.9 %copy-start.2 = (pred[512,512]{0,1:T(8,128)(4,1)}, pred[512,512]{0,1:T(8,128)(4,1)S(1)}, u32[]{:S(2)}) copy-start(pred[512,512]{0,1:T(8,128)(4,1)S(1)} %get-tuple-element.42) | copy-start | bytes 786436
  50.2 12.8 %collective-permute-start = (bf16[2,512,128]{2,1,0:T(8,128)(2,1)S(1)}, bf16[2,512,128]{2,1,0:T(8,128)(2,1)S(1)}, u32[]{:S(2)}, u32[]{:S(2)}) collective-permute-start(bf16[2,512,128]{2,1,0:T(8,128)(2,1)S(1)} %pad_maximum_fusion.1), channel_id=1, source_target_pairs={{0,16},{16,32},{32,48},{48,64},{64,80},{80,96},{96,112},{112,128},... | collective-permute-start | bytes 786440 | tf_op jit(solution)/shard_map/ppermute | solution.py:19
  63.0 12.7 %copy-start.4 = (bf16[2,512,128]{2,1,0:T(8,128)(2,1)}, bf16[2,512,128]{2,1,0:T(8,128)(2,1)S(1)}, u32[]{:S(2)}) copy-start(bf16[2,512,128]{2,1,0:T(8,128)(2,1)S(1)} %collective-permute-done) | copy-start | bytes 786436
  63.0 17.9 %collective-permute-start.1 = (bf16[2,512,128]{2,1,0:T(8,128)(2,1)S(1)}, bf16[2,512,128]{2,1,0:T(8,128)(2,1)}, u32[]{:S(2)}, u32[]{:S(2)}) collective-permute-start(bf16[2,512,128]{2,1,0:T(8,128)(2,1)S(1)} %collective-permute-done), channel_id=1, source_target_pairs={{0,16},{16,32},{32,48},{48,64},{64,80},{80,96},{96,112},{112,128},... | collective-permute-start | bytes 786440 | tf_op jit(solution)/shard_map/ppermute | solution.py:19
  80.9 15.5 %collective-permute-start.2 = (bf16[2,512,128]{2,1,0:T(8,128)(2,1)}, bf16[2,512,128]{2,1,0:T(8,128)(2,1)S(1)}, u32[]{:S(2)}, u32[]{:S(2)}) collective-permute-start(bf16[2,512,128]{2,1,0:T(8,128)(2,1)} %collective-permute-done.1), channel_id=1, source_target_pairs={{0,16},{16,32},{32,48},{48,64},{64,80},{80,96},{96,112},{112,128},... | collective-permute-start | bytes 786440 | tf_op jit(solution)/shard_map/ppermute | solution.py:19
  96.4 12.6 %collective-permute-start.3 = (bf16[2,512,128]{2,1,0:T(8,128)(2,1)S(1)}, bf16[2,512,128]{2,1,0:T(8,128)(2,1)S(1)}, u32[]{:S(2)}, u32[]{:S(2)}) collective-permute-start(bf16[2,512,128]{2,1,0:T(8,128)(2,1)S(1)} %collective-permute-done.2), channel_id=1, source_target_pairs={{0,16},{16,32},{32,48},{48,64},{64,80},{80,96},{96,112},{112,128},... | collective-permute-start | bytes 786440 | tf_op jit(solution)/shard_map/ppermute | solution.py:19
  109.0 12.5 %collective-permute-start.4 = (bf16[2,512,128]{2,1,0:T(8,128)(2,1)S(1)}, bf16[2,512,128]{2,1,0:T(8,128)(2,1)S(1)}, u32[]{:S(2)}, u32[]{:S(2)}) collective-permute-start(bf16[2,512,128]{2,1,0:T(8,128)(2,1)S(1)} %collective-permute-done.3), channel_id=1, source_target_pairs={{0,16},{16,32},{32,48},{48,64},{64,80},{80,96},{96,112},{112,128},... | collective-permute-start | bytes 786440 | tf_op jit(solution)/shard_map/ppermute | solution.py:19
  121.5 12.8 %collective-permute-start.5 = (bf16[2,512,128]{2,1,0:T(8,128)(2,1)S(1)}, bf16[2,512,128]{2,1,0:T(8,128)(2,1)S(1)}, u32[]{:S(2)}, u32[]{:S(2)}) collective-permute-start(bf16[2,512,128]{2,1,0:T(8,128)(2,1)S(1)} %collective-permute-done.4), channel_id=1, source_target_pairs={{0,16},{16,32},{32,48},{48,64},{64,80},{80,96},{96,112},{112,128},... | collective-permute-start | bytes 786440 | tf_op jit(solution)/shard_map/ppermute | solution.py:19
  133.5 24.4 %copy-start.6 = (f32[512,512,2]{1,0,2:T(8,128)}, f32[512,512,2]{1,0,2:T(8,128)S(1)}, u32[]{:S(2)}) copy-start(f32[512,512,2]{1,0,2:T(8,128)S(1)} %get-tuple-element.66) | copy-start | bytes 6291460
  135.2 23.9 %copy-start.7 = (f32[512,512,2]{1,0,2:T(8,128)}, f32[512,512,2]{1,0,2:T(8,128)S(1)}, u32[]{:S(2)}) copy-start(f32[512,512,2]{1,0,2:T(8,128)S(1)} %get-tuple-element.64) | copy-start | bytes 6291460
  138.0 14.1 %copy-start.5 = (bf16[2,512,128]{2,1,0:T(8,128)(2,1)S(1)}, bf16[2,512,128]{2,1,0:T(8,128)(2,1)}, u32[]{:S(2)}) copy-start(bf16[2,512,128]{2,1,0:T(8,128)(2,1)} %copy-done.4) | copy-start | bytes 786436
  139.0 26.7 %collective-permute-start.6 = (f32[2,512,128]{2,1,0:T(8,128)S(1)}, f32[2,512,128]{2,1,0:T(8,128)S(1)}, u32[]{:S(2)}, u32[]{:S(2)}) collective-permute-start(f32[2,512,128]{2,1,0:T(8,128)S(1)} %pad_maximum_fusion), channel_id=1, source_target_pairs={{496,0},{0,16},{16,32},{32,48},{48,64},{64,80},{80,96},{96,112},{1... | collective-permute-start | bytes 1572872 | tf_op jit(solution)/shard_map/ppermute | solution.py:25
  165.8 32.0 %collective-permute-start.7 = (f32[2,512,128]{2,1,0:T(8,128)S(1)}, f32[2,512,128]{2,1,0:T(8,128)S(1)}, u32[]{:S(2)}, u32[]{:S(2)}) collective-permute-start(f32[2,512,128]{2,1,0:T(8,128)S(1)} %maximum_add_fusion), channel_id=1, source_target_pairs={{496,0},{0,16},{16,32},{32,48},{48,64},{64,80},{80,96},{96,112},{1... | collective-permute-start | bytes 1572872 | tf_op jit(solution)/shard_map/ppermute | solution.py:25
  197.9 33.5 %collective-permute-start.8 = (f32[2,512,128]{2,1,0:T(8,128)S(1)}, f32[2,512,128]{2,1,0:T(8,128)S(1)}, u32[]{:S(2)}, u32[]{:S(2)}) collective-permute-start(f32[2,512,128]{2,1,0:T(8,128)S(1)} %maximum_add_fusion.1), channel_id=1, source_target_pairs={{496,0},{0,16},{16,32},{32,48},{48,64},{64,80},{80,96},{96,112},{1... | collective-permute-start | bytes 1572872 | tf_op jit(solution)/shard_map/ppermute | solution.py:25
  231.5 28.2 %collective-permute-start.9 = (f32[2,512,128]{2,1,0:T(8,128)S(1)}, f32[2,512,128]{2,1,0:T(8,128)S(1)}, u32[]{:S(2)}, u32[]{:S(2)}) collective-permute-start(f32[2,512,128]{2,1,0:T(8,128)S(1)} %maximum_add_fusion.2), channel_id=1, source_target_pairs={{496,0},{0,16},{16,32},{32,48},{48,64},{64,80},{80,96},{96,112},{1... | collective-permute-start | bytes 1572872 | tf_op jit(solution)/shard_map/ppermute | solution.py:25
  259.7 29.4 %collective-permute-start.10 = (f32[2,512,128]{2,1,0:T(8,128)S(1)}, f32[2,512,128]{2,1,0:T(8,128)S(1)}, u32[]{:S(2)}, u32[]{:S(2)}) collective-permute-start(f32[2,512,128]{2,1,0:T(8,128)S(1)} %maximum_add_fusion.3), channel_id=1, source_target_pairs={{496,0},{0,16},{16,32},{32,48},{48,64},{64,80},{80,96},{96,112},{1... | collective-permute-start | bytes 1572872 | tf_op jit(solution)/shard_map/ppermute | solution.py:25
  263.3 78.8 %all-to-all-start.4 = ((bf16[16,32,256]{2,1,0:T(8,128)(2,1)}), bf16[16,32,256]{2,1,0:T(8,128)(2,1)S(1)}, u32[]{:S(2)}, u32[]{:S(2)}) async-start(bf16[16,32,256]{2,1,0:T(8,128)(2,1)} %convert_element_type.355), calls=%async_computation.4 | async-start | bytes 524288 | tf_op jit(solution)/shard_map/all_to_all | solution.py:137
  286.6 4.5 %copy-start.3 = (pred[512,512]{0,1:T(8,128)(4,1)S(1)}, pred[512,512]{0,1:T(8,128)(4,1)}, u32[]{:S(2)}) copy-start(pred[512,512]{0,1:T(8,128)(4,1)} %copy-done.2) | copy-start | bytes 786436
  286.6 4.5 %copy-start.8 = (f32[512,512,2]{1,0,2:T(8,128)S(1)}, f32[512,512,2]{1,0,2:T(8,128)}, u32[]{:S(2)}) copy-start(f32[512,512,2]{1,0,2:T(8,128)} %copy-done.7) | copy-start | bytes 6291460
  289.2 33.3 %collective-permute-start.11 = (f32[2,512,128]{2,1,0:T(8,128)S(1)}, f32[2,512,128]{2,1,0:T(8,128)S(1)}, u32[]{:S(2)}, u32[]{:S(2)}) collective-permute-start(f32[2,512,128]{2,1,0:T(8,128)S(1)} %maximum_add_fusion.4), channel_id=1, source_target_pairs={{496,0},{0,16},{16,32},{32,48},{48,64},{64,80},{80,96},{96,112},{1... | collective-permute-start | bytes 1572872 | tf_op jit(solution)/shard_map/ppermute | solution.py:25
  322.6 18.9 %collective-permute-start.12 = (bf16[2,512,128]{2,1,0:T(8,128)(2,1)S(1)}, bf16[2,512,128]{2,1,0:T(8,128)(2,1)S(1)}, u32[]{:S(2)}, u32[]{:S(2)}) collective-permute-start(bf16[2,512,128]{2,1,0:T(8,128)(2,1)S(1)} %fusion.86), channel_id=1, source_target_pairs={{96,0},{112,16},{128,32},{144,48},{160,64},{176,80},{192,96},{208,... | collective-permute-start | bytes 786440 | tf_op jit(solution)/shard_map/ppermute | solution.py:25
  367.7 11.9 %all-to-all-start.5 = ((bf16[16,32,128]{2,1,0:T(8,128)(2,1)}), bf16[16,32,128]{2,1,0:T(8,128)(2,1)S(1)}, u32[]{:S(2)}, u32[]{:S(2)}) async-start(bf16[16,32,128]{2,1,0:T(8,128)(2,1)} %bitcast.138), calls=%async_computation.5 | async-start | bytes 262144 | tf_op jit(solution)/shard_map/all_to_all | solution.py:138
where the time goes:
time: 381 us; the launch traced here: 380 us
  starting transfers between devices  185 us (49%)
  waiting for transfers between devices  114 us (30%)
  matrix products  37.2 us (10%)
  blocking collectives  25.6 us (7%)
  local copies, waits for them, and re-layouts  10.5 us (3%)
  other arithmetic  5.66 us (1%)
    ppermute x7, starting transfers between devices, shifted_2(): return lax.ppermute(block, axis, route)  82.7 us
    ppermute x7, waiting for transfers between devices, shifted_2(): return lax.ppermute(block, axis, route)  73.4 us
    ppermute x6, starting transfers between devices, shifted(): return lax.ppermute(value, axis, pairs)  56.6 us
    all_to_all x1, blocking collectives, local(): lax.all_to_all(grad_value, 'head', split_axis=0, concat_axis=1, tiled=True)  25.6 us
    all_to_all x1, starting transfers between devices, local(): lax.all_to_all(grad_query, 'head', split_axis=0, concat_axis=1, tiled=True)  23.3 us
    ppermute x6, waiting for transfers between devices, shifted(): return lax.ppermute(value, axis, pairs)  14.2 us
    dot_general x7, matrix products, local(): jnp.einsum('qgd,kd->gqk', grad_heads, value_block, preferred_element_type...  9.36 us
    all_to_all x1, starting transfers between devices, local(): lax.all_to_all(key_states, 'head', split_axis=1, concat_axis=0, tiled=True)  8.64 us
  transfers between devices with their start and end apart: 19, of which 13 were waited for; matrix products, arithmetic and copies ran while one was open for 12% of the time, Pallas kernels for 0%

commit v1 on v0

v1 whole, which is shorter than its diff:
```python
import jax
import jax.numpy as jnp
from jax import lax
from jax.experimental import pallas as pl
from jax.experimental.pallas import tpu as pltpu
from jax.sharding import Mesh, PartitionSpec as P

HEAD_DIM = 128
WINDOW = 4096
SOFT_CAP = 50.0
SCORE_SCALE = 1.0 / 12.0

X, ZH, CORE, Y, ZL = 4, 4, 2, 4, 4
HEADS = ZH * ZL
SLAB = 4096
RUN = 128
HALO = 3
SLOTS = 2 * (HALO + ZH)
KB = 256
BLOCKS = SLOTS * 512 // KB
MOST = 14
PACK_STEP = 1 << 15


def token_codes(positions, pack_table):
    starts = pack_table[:, 0]
    pack_id = jnp.sum((positions[:, None] >= starts[None, :]).astype(jnp.int32), axis=1) - 1
    chosen = pack_id[:, None] == jnp.arange(pack_table.shape[0], dtype=jnp.int32)[None, :]
    bounds = jnp.sum(jnp.where(chosen[:, :, None], pack_table[None, :, :], 0), axis=1)
    role = (positions >= bounds[:, 1]).astype(jnp.int32) + (positions >= bounds[:, 2]).astype(
        jnp.int32
    )
    logical = (
        jnp.where(role == 2, positions - bounds[:, 2] + bounds[:, 1], positions) - bounds[:, 0]
    )
    return pack_id * PACK_STEP + logical, role, bounds[:, 0]


def attend(
    where_ref, query_code_ref, key_code_ref, qg_ref,
    own0, own1, own2, own3, own_other, halo0, halo1, halo2, halo3, halo_other,
    dq_ref, mine_ref, other_ref,
    keys, values, keys_t, values_t, ratios, expos, sums,
):
    y = where_ref[8]
    core = where_ref[9]
    f32, b16 = jnp.float32, jnp.bfloat16

    def place(slot, row, piece):
        block = slot * 2 + row // 2
        at = pl.multiple_of((row % 2) * RUN, RUN)
        keys[block, pl.ds(at, RUN), :] = piece[:, :HEAD_DIM]
        values[block, pl.ds(at, RUN), :] = piece[:, HEAD_DIM:]

    for dy, (own, halo) in enumerate(((own0, halo0), (own1, halo1), (own2, halo2), (own3, halo3))):
        row = (y + dy) % Y
        for c in range(ZH):
            place(2 * (HALO + c) + core, row, own[c * RUN : (c + 1) * RUN, :])
            place(2 * (HALO + c) + 1 - core, row, own_other[dy, c * RUN : (c + 1) * RUN, :])
        for c in range(HALO):
            place(2 * c + core, row, halo[c * RUN : (c + 1) * RUN, :])
            place(2 * c + 1 - core, row, halo_other[dy, c * RUN : (c + 1) * RUN, :])

    def prepare(block, carry):
        keys_t[block] = keys[block].T
        values_t[block] = values[block].T
        return carry

    lax.fori_loop(where_ref[0], BLOCKS, prepare, 0)

    def clear(block, carry):
        sums[block] = jnp.zeros((KB, 2 * HEAD_DIM), f32)
        return carry

    lax.fori_loop(0, BLOCKS, clear, 0)

    for c in range(ZH):
        rows = slice(c * RUN, (c + 1) * RUN)
        low = where_ref[c]
        high = where_ref[4 + c]
        query = jnp.concatenate([qg_ref[rows, 0:128], qg_ref[rows, 128:256]], axis=0)
        grad = jnp.concatenate([qg_ref[rows, 256:384], qg_ref[rows, 384:512]], axis=0)
        query_t = query.T
        grad_t = grad.T
        query_code = query_code_ref[c : c + 1, :]

        def forward(block, carry):
            total, weighted = carry
            raw = jnp.dot(keys[block], query_t, preferred_element_type=f32)
            ratio = jnp.tanh(raw * (SCORE_SCALE / SOFT_CAP))
            expo = jnp.exp(ratio * SOFT_CAP)
            gap = query_code - key_code_ref[pl.ds(pl.multiple_of(block * KB, KB), KB), :]
            seen = (gap >= 0) & (gap < 8 * WINDOW) & ((gap & 7) != 1)
            expo = jnp.concatenate(
                [jnp.where(seen, expo[:, :RUN], 0.0), jnp.where(seen, expo[:, RUN:], 0.0)], axis=1
            )
            ratios[block - low] = ratio
            expos[block - low] = expo
            total = total + jnp.sum(expo, axis=0, keepdims=True)
            weighted = weighted + jnp.dot(
                values_t[block], expo.astype(b16), preferred_element_type=f32
            )
            return total, weighted

        total, weighted = lax.fori_loop(
            low, high + 1, forward,
            (jnp.zeros((1, 2 * RUN), f32), jnp.zeros((HEAD_DIM, 2 * RUN), f32)),
        )
        scale = 1.0 / total
        delta = jnp.sum(grad_t.astype(f32) * weighted, axis=0, keepdims=True) * scale

        def backward(block, dq_t):
            ratio = ratios[block - low]
            prob = expos[block - low] * scale
            dprob = jnp.dot(values[block], grad_t, preferred_element_type=f32)
            dscore = prob * (dprob - delta) * ((1.0 - ratio * ratio) * SCORE_SCALE)
            dscore = dscore.astype(b16)
            dq_t = dq_t + jnp.dot(keys_t[block], dscore, preferred_element_type=f32)
            dk = jnp.dot(dscore, query, preferred_element_type=f32)
            dv = jnp.dot(prob.astype(b16), grad, preferred_element_type=f32)
            sums[block] = sums[block] + jnp.concatenate([dk, dv], axis=1)
            return dq_t

        dq_t = lax.fori_loop(low, high + 1, backward, jnp.zeros((HEAD_DIM, 2 * RUN), f32))
        dq_ref[rows, 0:128] = dq_t[:, :RUN].T.astype(b16)
        dq_ref[rows, 128:256] = dq_t[:, RUN:].T.astype(b16)

    for dy in range(Y):
        row = (y + dy) % Y
        at = pl.multiple_of((row % 2) * RUN, RUN)
        for c in range(HALO + ZH):
            mine_ref[dy, c * RUN : (c + 1) * RUN, :] = sums[
                (2 * c + core) * 2 + row // 2, pl.ds(at, RUN), :
            ]
            other_ref[dy, c * RUN : (c + 1) * RUN, :] = sums[
                (2 * c + 1 - core) * 2 + row // 2, pl.ds(at, RUN), :
            ].astype(b16)


def call_attend(where, query_code, key_code, qg, pieces):
    vmem = pl.BlockSpec(memory_space=pltpu.VMEM)
    rows = (HALO + ZH) * RUN
    return pl.pallas_call(
        attend,
        out_shape=(
            jax.ShapeDtypeStruct((ZH * RUN, 256), jnp.bfloat16),
            jax.ShapeDtypeStruct((Y, rows, 256), jnp.float32),
            jax.ShapeDtypeStruct((Y, rows, 256), jnp.bfloat16),
        ),
        in_specs=[pl.BlockSpec(memory_space=pltpu.SMEM)] + [vmem] * 13,
        out_specs=(vmem, vmem, vmem),
        scratch_shapes=[
            pltpu.VMEM((BLOCKS, KB, HEAD_DIM), jnp.bfloat16),
            pltpu.VMEM((BLOCKS, KB, HEAD_DIM), jnp.bfloat16),
            pltpu.VMEM((BLOCKS, HEAD_DIM, KB), jnp.bfloat16),
            pltpu.VMEM((BLOCKS, HEAD_DIM, KB), jnp.bfloat16),
            pltpu.VMEM((MOST, KB, 2 * RUN), jnp.float32),
            pltpu.VMEM((MOST, KB, 2 * RUN), jnp.float32),
            pltpu.VMEM((BLOCKS, KB, 2 * HEAD_DIM), jnp.float32),
        ],
        compiler_params=pltpu.CompilerParams(vmem_limit_bytes=56 << 20),
        name="attend",
    )(where, query_code, key_code, qg, *pieces)


def tables(x, core, y, pack_table):
    first = x * SLAB - HALO * 1024
    code, role, _ = token_codes(first + jnp.arange(SLOTS * 512, dtype=jnp.int32), pack_table)
    key_code = jnp.broadcast_to((8 * code + role)[:, None], (SLOTS * 512, RUN))
    runs = jnp.arange(ZH, dtype=jnp.int32)
    begin = x * SLAB + runs * 1024 + core * 512 + y * RUN
    position = (begin[:, None] + jnp.arange(RUN, dtype=jnp.int32)[None, :]).reshape(-1)
    code, role, start = token_codes(position, pack_table)
    query_code = (8 * code + 4 - role).reshape(ZH, RUN)
    high = (begin - first) // KB
    low = (start.reshape(ZH, RUN)[:, 0] - first) // KB
    low = jnp.maximum(jnp.maximum(low, high - (MOST - 1)), 0)
    where = jnp.concatenate([low, high, jnp.stack([y, core])])
    return where, query_code, key_code


def ring(size, by):
    return [(i, (i + by) % size) for i in range(size)]


def local(query_states, key_states, value_states, grad_out, pack_table):
    b16, f32 = jnp.bfloat16, jnp.float32
    x, core, y = lax.axis_index("x"), lax.axis_index("core"), lax.axis_index("y")
    z = ("zh", "zl")
    tokens = query_states.shape[0]

    def by_head(value):
        return jnp.transpose(value.reshape(tokens, HEADS, -1), (1, 0, 2))

    kv = jnp.concatenate([by_head(key_states), by_head(value_states)], axis=2)
    kv = lax.all_to_all(kv, z, split_axis=0, concat_axis=0, tiled=True).reshape(ZH * RUN, 256)
    qg = jnp.concatenate([by_head(query_states), by_head(grad_out)], axis=2)
    qg = lax.all_to_all(qg, z, split_axis=0, concat_axis=0, tiled=True).reshape(ZH * RUN, 512)
    where, query_code, key_code = tables(x, core, y, pack_table)

    halo = lax.ppermute(kv[RUN:], "x", [(i, i + 1) for i in range(X - 1)])
    own = [kv] + [lax.ppermute(kv, "y", ring(Y, -dy)) for dy in range(1, Y)]
    halos = [halo] + [lax.ppermute(halo, "y", ring(Y, -dy)) for dy in range(1, Y)]
    own_other = lax.ppermute(jnp.stack(own), "core", ring(CORE, 1))
    halo_other = lax.ppermute(jnp.stack(halos), "core", ring(CORE, 1))
    dq, mine, other = call_attend(
        where, query_code, key_code, qg, (*own, own_other, *halos, halo_other)
    )

    dq = lax.all_to_all(dq.reshape(HEADS, tokens, 256), z, split_axis=0, concat_axis=0, tiled=True)
    grad_query = jnp.transpose(dq, (1, 0, 2)).reshape(tokens, HEADS * 256)

    part = mine + lax.ppermute(other, "core", ring(CORE, 1)).astype(f32)
    total = part[0]
    for dy in range(1, Y):
        total = total + lax.ppermute(part[dy].astype(b16), "y", ring(Y, dy)).astype(f32)
    back = lax.ppermute(
        total[: HALO * RUN].astype(b16), "x", [(i + 1, i) for i in range(X - 1)]
    ).astype(f32)
    total = total[HALO * RUN :] + jnp.pad(back, ((RUN, 0), (0, 0)))
    dkv = lax.all_to_all(
        total.astype(b16).reshape(HEADS, tokens, 256), z, split_axis=0, concat_axis=0, tiled=True
    )
    dkv = jnp.transpose(dkv, (1, 0, 2))
    grad_key = dkv[:, :, :HEAD_DIM].reshape(tokens, HEADS * HEAD_DIM)
    grad_value = dkv[:, :, HEAD_DIM:].reshape(tokens, HEADS * HEAD_DIM)
    return grad_query, grad_key, grad_value


def solution(mesh):
    axes = ("x", "zh", "core", "y", "zl")
    fine = Mesh(mesh.devices.reshape(X, ZH, CORE, Y, ZL), axes)
    spread = P(axes, None)
    return jax.shard_map(
        local,
        mesh=fine,
        in_specs=(spread, spread, spread, spread, P()),
        out_specs=(spread, spread, spread),
        check_vma=False,
    )
```

time: 381 us -> 197 us (0.52)
  the two profiles are of different devices: /device:TPU:4 before, /device:TPU:44 now
where the time goes in v1:
time: 197 us; the launch traced here: 196 us
  starting transfers between devices  85.4 us (43%)
  waiting for transfers between devices  56.2 us (29%)
  Pallas kernels  28.9 us (15%)
  other arithmetic  13 us (7%)
  local copies, waits for them, and re-layouts  11.6 us (6%)
    pallas_call x1, Pallas kernels, call_attend(): pl.pallas_call(attend, out_shape=(jax.ShapeDtypeStruct((ZH * RUN, 256), j...  28.9 us
    all_to_all x1, waiting for transfers between devices, local(): lax.all_to_all(total.astype(b16).reshape(HEADS, tokens, 256), z, split_ax...  16.8 us
    all_to_all x1, starting transfers between devices, local(): lax.all_to_all(kv, z, split_axis=0, concat_axis=0, tiled=True)  15.2 us
    all_to_all x1, waiting for transfers between devices, local(): lax.all_to_all(kv, z, split_axis=0, concat_axis=0, tiled=True)  13.3 us
    all_to_all x1, starting transfers between devices, local(): lax.all_to_all(dq.reshape(HEADS, tokens, 256), z, split_axis=0, concat_ax...  12 us
    all_to_all x1, starting transfers between devices, local(): lax.all_to_all(total.astype(b16).reshape(HEADS, tokens, 256), z, split_ax...  10.7 us
    ppermute x3, starting transfers between devices, local(): own = [kv] + [lax.ppermute(kv, 'y', ring(Y, -dy)) for dy in range(1, Y)]  10.6 us
    ppermute x3, starting transfers between devices, local(): lax.ppermute(part[dy].astype(b16), 'y', ring(Y, dy)).astype(f32)  10.6 us
  transfers between devices with their start and end apart: 18, of which 11 were waited for; matrix products, arithmetic and copies ran while one was open for 5% of the time, Pallas kernels for 0%

profile of v1, /device:TPU:44, one launch (start us, length us, event | category | flops | bytes accessed | tf_op | source)
XLA Modules:
  0.0 196.0 jit_solution(8615839355211903183)
XLA Ops:
  3.2 15.2 %all-to-all-start.1 = ((bf16[16,32,256]{2,1,0:T(8,128)(2,1)}), bf16[16,32,256]{2,1,0:T(8,128)(2,1)S(1)}, u32[]{:S(2)}, u32[]{:S(2)}) async-start(bf16[16,32,256]{2,1,0:T(8,128)(2,1)} %pad_maximum_fusion.3), calls=%async_computation.1 | async-start | bytes 524288 | tf_op jit(solution)/shard_map/all_to_all | solution.py:196
  23.1 13.3 %all-to-all-done.1 = bf16[16,32,256]{2,1,0:T(8,128)(2,1)S(1)} async-done(((bf16[16,32,256]{2,1,0:T(8,128)(2,1)}), bf16[16,32,256]{2,1,0:T(8,128)(2,1)S(1)}, u32[]{:S(2)}, u32[]{:S(2)}) %all-to-all-start.1) | async-done | bytes 262176 | tf_op jit(solution)/shard_map/all_to_all | solution.py:196
  36.4 6.2 %all-to-all-start = ((bf16[16,32,512]{2,1,0:T(8,128)(2,1)}), bf16[16,32,512]{2,1,0:T(8,128)(2,1)S(1)}, u32[]{:S(2)}, u32[]{:S(2)}) async-start(bf16[16,32,512]{2,1,0:T(8,128)(2,1)} %pad_maximum_fusion.2), calls=%async_computation | async-start | bytes 1048576 | tf_op jit(solution)/shard_map/all_to_all | solution.py:198
  42.8 3.5 %collective-permute-start.2 = (bf16[512,256]{1,0:T(8,128)(2,1)S(1)}, bf16[512,256]{1,0:T(8,128)(2,1)S(1)}, u32[]{:S(2)}, u32[]{:S(2)}) collective-permute-start(bf16[512,256]{1,0:T(8,128)(2,1)S(1)} %bitcast.84), channel_id=1, source_target_pairs={{0,4},{4,8},{8,12},{12,0},{1,5},{5,9},{9,13},{13,1},{2,6},{6,10},{... | collective-permute-start | bytes 786440 | tf_op jit(solution)/shard_map/ppermute | solution.py:202
  46.3 2.8 %collective-permute-start.1 = (bf16[512,256]{1,0:T(8,128)(2,1)S(1)}, bf16[512,256]{1,0:T(8,128)(2,1)S(1)}, u32[]{:S(2)}, u32[]{:S(2)}) collective-permute-start(bf16[512,256]{1,0:T(8,128)(2,1)S(1)} %bitcast.85), channel_id=1, source_target_pairs={{0,8},{4,12},{8,0},{12,4},{1,9},{5,13},{9,1},{13,5},{2,10},{6,14},... | collective-permute-start | bytes 786440 | tf_op jit(solution)/shard_map/ppermute | solution.py:202
  49.1 4.3 %collective-permute-start = (bf16[512,256]{1,0:T(8,128)(2,1)S(1)}, bf16[512,256]{1,0:T(8,128)(2,1)S(1)}, u32[]{:S(2)}, u32[]{:S(2)}) collective-permute-start(bf16[512,256]{1,0:T(8,128)(2,1)S(1)} %bitcast.86), channel_id=1, source_target_pairs={{0,12},{4,0},{8,4},{12,8},{1,13},{5,1},{9,5},{13,9},{2,14},{6,2},{... | collective-permute-start | bytes 786440 | tf_op jit(solution)/shard_map/ppermute | solution.py:202
  53.5 3.1 %collective-permute-start.4 = (bf16[384,256]{1,0:T(8,128)(2,1)S(1)}, bf16[384,256]{1,0:T(8,128)(2,1)S(1)}, u32[]{:S(2)}, u32[]{:S(2)}) collective-permute-start(bf16[384,256]{1,0:T(8,128)(2,1)S(1)} %bitcast.102), channel_id=1, source_target_pairs={{0,128},{128,256},{256,384},{1,129},{129,257},{257,385},{2,130},{1... | collective-permute-start | bytes 589832 | tf_op jit(solution)/shard_map/ppermute | solution.py:201
  56.6 4.4 %collective-permute-done.4.halo0 = bf16[384,256]{1,0:T(8,128)(2,1)S(1)} collective-permute-done((bf16[384,256]{1,0:T(8,128)(2,1)S(1)}, bf16[384,256]{1,0:T(8,128)(2,1)S(1)}, u32[]{:S(2)}, u32[]{:S(2)}) %collective-permute-start.4) | collective-permute-done | bytes 196640 | tf_op jit(solution)/shard_map/ppermute | solution.py:201
  61.0 1.9 collective-permute-start.7
  63.0 5.3 %collective-permute-start.6 = (bf16[384,256]{1,0:T(8,128)(2,1)S(1)}, bf16[384,256]{1,0:T(8,128)(2,1)S(1)}, u32[]{:S(2)}, u32[]{:S(2)}) collective-permute-start(bf16[384,256]{1,0:T(8,128)(2,1)S(1)} %collective-permute-done.4.halo0), channel_id=1, source_target_pairs={{0,8},{4,12},{8,0},{12,4},{1,9},{5,13},{9,1},{13,5},{2,10},{6,14},... | collective-permute-start | bytes 589832 | tf_op jit(solution)/shard_map/ppermute | solution.py:203
  68.3 1.9 collective-permute-start.5
  71.1 1.9 collective-permute-start.3
  73.6 2.5 %collective-permute-done.5.halo1 = bf16[384,256]{1,0:T(8,128)(2,1)S(1)} collective-permute-done((bf16[384,256]{1,0:T(8,128)(2,1)S(1)}, bf16[384,256]{1,0:T(8,128)(2,1)S(1)}, u32[]{:S(2)}, u32[]{:S(2)}) %collective-permute-start.5) | collective-permute-done | bytes 196640 | tf_op jit(solution)/shard_map/ppermute | solution.py:203
  77.1 1.9 collective-permute-start.8
  80.5 1.1 collective-permute-done.8.halo_other
  81.6 5.0 %broadcast_in_dim.66.key_code_ref = s32[7168,128]{1,0:T(8,128)} broadcast(s32[7168]{0:T(1024)} %bitcast.106), dimensions={0} | broadcast | bytes 3698688 | tf_op jit(solution)/shard_map/broadcast_in_dim | solution.py:169
  86.6 28.9 %attend.1 = (bf16[512,256]{1,0:T(8,128)(2,1)}, f32[4,896,256]{2,1,0:T(8,128)}, bf16[4,896,256]{2,1,0:T(8,128)(2,1)}) custom-call(s32[10]{0:T(128)} %pad_add_fusion.where_ref, s32[4,128]{1,0:T(4,128)} %fusion.9.query_code_ref, s32[7168,128]{1,0:T(8,128)} %broadcast_in_dim.66.key_code_ref, bf16[512,512]{1,0:T(8,128)(2,1)} %bitcast.89, ...), custom_call_target="tpu_custom_call" | custom-call | tf_op jit(solution)/shard_map/attend/pallas_call | solution.py:143
  115.5 1.9 collective-permute-start.9
  117.4 4.0 %collective-permute-done.9 = bf16[4,896,256]{2,1,0:T(8,128)(2,1)S(1)} collective-permute-done((bf16[4,896,256]{2,1,0:T(8,128)(2,1)}, bf16[4,896,256]{2,1,0:T(8,128)(2,1)S(1)}, u32[]{:S(2)}, u32[]{:S(2)}) %collective-permute-start.9) | collective-permute-done | bytes 1835040 | tf_op jit(solution)/shard_map/ppermute | solution.py:213
  121.4 4.4 %fusion.12 = (bf16[4,896,256]{2,1,0:T(8,128)(2,1)S(1)}, f32[4,896,256]{2,1,0:T(8,128)}) fusion(f32[4,896,256]{2,1,0:T(8,128)} %get-tuple-element.7, bf16[4,896,256]{2,1,0:T(8,128)(2,1)S(1)} %collective-permute-done.9), kind=kLoop, calls=%fused_computation.61 | loop fusion | flops 2752512 | bytes 11010048 | tf_op jit(solution)/shard_map/convert.5
  125.9 5.3 %collective-permute-start.10 = (bf16[896,256]{1,0:T(8,128)(2,1)S(1)}, bf16[896,256]{1,0:T(8,128)(2,1)S(1)}, u32[]{:S(2)}, u32[]{:S(2)}) collective-permute-start(bf16[896,256]{1,0:T(8,128)(2,1)S(1)} %get-tuple-element.13), channel_id=1, source_target_pairs={{0,4},{4,8},{8,12},{12,0},{1,5},{5,9},{9,13},{13,1},{2,6},{6,10},{... | collective-permute-start | bytes 1376264 | tf_op jit(solution)/shard_map/ppermute | solution.py:216
  131.2 1.9 collective-permute-start.12
  133.1 3.4 %collective-permute-start.11 = (bf16[896,256]{1,0:T(8,128)(2,1)S(1)}, bf16[896,256]{1,0:T(8,128)(2,1)S(1)}, u32[]{:S(2)}, u32[]{:S(2)}) collective-permute-start(bf16[896,256]{1,0:T(8,128)(2,1)S(1)} %get-tuple-element.15), channel_id=1, source_target_pairs={{0,8},{4,12},{8,0},{12,4},{1,9},{5,13},{9,1},{13,5},{2,10},{6,14},... | collective-permute-start | bytes 1376264 | tf_op jit(solution)/shard_map/ppermute | solution.py:216
  136.5 12.0 %all-to-all-start.2 = ((bf16[16,32,256]{2,1,0:T(8,128)(2,1)}), bf16[16,32,256]{2,1,0:T(8,128)(2,1)S(1)}, u32[]{:S(2)}, u32[]{:S(2)}) async-start(bf16[16,32,256]{2,1,0:T(8,128)(2,1)} %bitcast.25), calls=%async_computation.2 | async-start | bytes 524288 | tf_op jit(solution)/shard_map/all_to_all | solution.py:210
  148.5 2.5 %collective-permute-done.10 = bf16[896,256]{1,0:T(8,128)(2,1)S(1)} collective-permute-done((bf16[896,256]{1,0:T(8,128)(2,1)S(1)}, bf16[896,256]{1,0:T(8,128)(2,1)S(1)}, u32[]{:S(2)}, u32[]{:S(2)}) %collective-permute-start.10) | collective-permute-done | bytes 458784 | tf_op jit(solution)/shard_map/ppermute | solution.py:216
  151.1 4.1 %collective-permute-done.12 = bf16[896,256]{1,0:T(8,128)(2,1)S(1)} collective-permute-done((bf16[896,256]{1,0:T(8,128)(2,1)S(1)}, bf16[896,256]{1,0:T(8,128)(2,1)S(1)}, u32[]{:S(2)}, u32[]{:S(2)}) %collective-permute-start.12) | collective-permute-done | bytes 458784 | tf_op jit(solution)/shard_map/ppermute | solution.py:216
  155.2 1.4 fusion.2
  156.6 1.9 collective-permute-start.13
  158.5 5.8 %collective-permute-done.13 = bf16[384,256]{1,0:T(8,128)(2,1)S(1)} collective-permute-done((bf16[384,256]{1,0:T(8,128)(2,1)S(1)}, bf16[384,256]{1,0:T(8,128)(2,1)S(1)}, u32[]{:S(2)}, u32[]{:S(2)}) %collective-permute-start.13) | collective-permute-done | bytes 196640 | tf_op jit(solution)/shard_map/ppermute | solution.py:217
  165.1 1.3 all-to-all-done.2
  166.4 10.7 %all-to-all-start.3 = ((bf16[16,32,256]{2,1,0:T(8,128)(2,1)}), bf16[16,32,256]{2,1,0:T(8,128)(2,1)S(1)}, u32[]{:S(2)}, u32[]{:S(2)}) async-start(bf16[16,32,256]{2,1,0:T(8,128)(2,1)} %bitcast.31), calls=%async_computation.3 | async-start | bytes 524288 | tf_op jit(solution)/shard_map/all_to_all | solution.py:221
  177.9 16.8 %all-to-all-done.3 = bf16[16,32,256]{2,1,0:T(8,128)(2,1)S(1)} async-done(((bf16[16,32,256]{2,1,0:T(8,128)(2,1)}), bf16[16,32,256]{2,1,0:T(8,128)(2,1)S(1)}, u32[]{:S(2)}, u32[]{:S(2)}) %all-to-all-start.3) | async-done | bytes 262176 | tf_op jit(solution)/shard_map/all_to_all | solution.py:221
  (64 shorter events, 14.3 us)
Async XLA Ops:
  0.6 0.9 copy-start
  2.5 70.6 %copy-start.11 = (s32[8,4]{0,1:T(4,128)S(1)}, s32[8,4]{0,1:T(4,128)}, u32[]{:S(2)}) copy-start(s32[8,4]{0,1:T(4,128)} %param.9) | copy-start | bytes 388
  3.2 33.1 %all-to-all-start.1 = ((bf16[16,32,256]{2,1,0:T(8,128)(2,1)}), bf16[16,32,256]{2,1,0:T(8,128)(2,1)S(1)}, u32[]{:S(2)}, u32[]{:S(2)}) async-start(bf16[16,32,256]{2,1,0:T(8,128)(2,1)} %pad_maximum_fusion.3), calls=%async_computation.1 | async-start | bytes 524288 | tf_op jit(solution)/shard_map/all_to_all | solution.py:196
  36.4 50.2 %copy-start.1 = (bf16[16,32,256]{2,1,0:T(8,128)(2,1)}, bf16[16,32,256]{2,1,0:T(8,128)(2,1)S(1)}, u32[]{:S(2)}) copy-start(bf16[16,32,256]{2,1,0:T(8,128)(2,1)S(1)} %all-to-all-done.1) | copy-start | bytes 786436
  36.4 44.1 %all-to-all-start = ((bf16[16,32,512]{2,1,0:T(8,128)(2,1)}), bf16[16,32,512]{2,1,0:T(8,128)(2,1)S(1)}, u32[]{:S(2)}, u32[]{:S(2)}) async-start(bf16[16,32,512]{2,1,0:T(8,128)(2,1)} %pad_maximum_fusion.2), calls=%async_computation | async-start | bytes 1048576 | tf_op jit(solution)/shard_map/all_to_all | solution.py:198
  42.8 25.5 %collective-permute-start.2 = (bf16[512,256]{1,0:T(8,128)(2,1)S(1)}, bf16[512,256]{1,0:T(8,128)(2,1)S(1)}, u32[]{:S(2)}, u32[]{:S(2)}) collective-permute-start(bf16[512,256]{1,0:T(8,128)(2,1)S(1)} %bitcast.84), channel_id=1, source_target_pairs={{0,4},{4,8},{8,12},{12,0},{1,5},{5,9},{9,13},{13,1},{2,6},{6,10},{... | collective-permute-start | bytes 786440 | tf_op jit(solution)/shard_map/ppermute | solution.py:202
  46.3 24.0 %collective-permute-start.1 = (bf16[512,256]{1,0:T(8,128)(2,1)S(1)}, bf16[512,256]{1,0:T(8,128)(2,1)S(1)}, u32[]{:S(2)}, u32[]{:S(2)}) collective-permute-start(bf16[512,256]{1,0:T(8,128)(2,1)S(1)} %bitcast.85), channel_id=1, source_target_pairs={{0,8},{4,12},{8,0},{12,4},{1,9},{5,13},{9,1},{13,5},{2,10},{6,14},... | collective-permute-start | bytes 786440 | tf_op jit(solution)/shard_map/ppermute | solution.py:202
  49.1 21.1 %collective-permute-start = (bf16[512,256]{1,0:T(8,128)(2,1)S(1)}, bf16[512,256]{1,0:T(8,128)(2,1)S(1)}, u32[]{:S(2)}, u32[]{:S(2)}) collective-permute-start(bf16[512,256]{1,0:T(8,128)(2,1)S(1)} %bitcast.86), channel_id=1, source_target_pairs={{0,12},{4,0},{8,4},{12,8},{1,13},{5,1},{9,5},{13,9},{2,14},{6,2},{... | collective-permute-start | bytes 786440 | tf_op jit(solution)/shard_map/ppermute | solution.py:202
  53.5 7.6 %collective-permute-start.4 = (bf16[384,256]{1,0:T(8,128)(2,1)S(1)}, bf16[384,256]{1,0:T(8,128)(2,1)S(1)}, u32[]{:S(2)}, u32[]{:S(2)}) collective-permute-start(bf16[384,256]{1,0:T(8,128)(2,1)S(1)} %bitcast.102), channel_id=1, source_target_pairs={{0,128},{128,256},{256,384},{1,129},{129,257},{257,385},{2,130},{1... | collective-permute-start | bytes 589832 | tf_op jit(solution)/shard_map/ppermute | solution.py:201
  61.0 18.8 %copy-start.7 = (bf16[384,256]{1,0:T(8,128)(2,1)}, bf16[384,256]{1,0:T(8,128)(2,1)S(1)}, u32[]{:S(2)}) copy-start(bf16[384,256]{1,0:T(8,128)(2,1)S(1)} %collective-permute-done.4.halo0) | copy-start | bytes 589828
  61.0 12.1 %collective-permute-start.7 = (bf16[384,256]{1,0:T(8,128)(2,1)S(1)}, bf16[384,256]{1,0:T(8,128)(2,1)S(1)}, u32[]{:S(2)}, u32[]{:S(2)}) collective-permute-start(bf16[384,256]{1,0:T(8,128)(2,1)S(1)} %collective-permute-done.4.halo0), channel_id=1, source_target_pairs={{0,4},{4,8},{8,12},{12,0},{1,5},{5,9},{9,13},{13,1},{2,6},{6,10},{... | collective-permute-start | bytes 589832 | tf_op jit(solution)/shard_map/ppermute | solution.py:203
  63.0 10.6 %collective-permute-start.6 = (bf16[384,256]{1,0:T(8,128)(2,1)S(1)}, bf16[384,256]{1,0:T(8,128)(2,1)S(1)}, u32[]{:S(2)}, u32[]{:S(2)}) collective-permute-start(bf16[384,256]{1,0:T(8,128)(2,1)S(1)} %collective-permute-done.4.halo0), channel_id=1, source_target_pairs={{0,8},{4,12},{8,0},{12,4},{1,9},{5,13},{9,1},{13,5},{2,10},{6,14},... | collective-permute-start | bytes 589832 | tf_op jit(solution)/shard_map/ppermute | solution.py:203
  68.3 18.2 %copy-start.4 = (bf16[512,256]{1,0:T(8,128)(2,1)}, bf16[512,256]{1,0:T(8,128)(2,1)S(1)}, u32[]{:S(2)}) copy-start(bf16[512,256]{1,0:T(8,128)(2,1)S(1)} %collective-permute-done.2.own3) | copy-start | bytes 786436
  68.3 7.8 %collective-permute-start.5 = (bf16[384,256]{1,0:T(8,128)(2,1)S(1)}, bf16[384,256]{1,0:T(8,128)(2,1)S(1)}, u32[]{:S(2)}, u32[]{:S(2)}) collective-permute-start(bf16[384,256]{1,0:T(8,128)(2,1)S(1)} %collective-permute-done.4.halo0), channel_id=1, source_target_pairs={{0,12},{4,0},{8,4},{12,8},{1,13},{5,1},{9,5},{13,9},{2,14},{6,2},{... | collective-permute-start | bytes 589832 | tf_op jit(solution)/shard_map/ppermute | solution.py:203
  70.2 16.3 %copy-start.5 = (bf16[512,256]{1,0:T(8,128)(2,1)}, bf16[512,256]{1,0:T(8,128)(2,1)S(1)}, u32[]{:S(2)}) copy-start(bf16[512,256]{1,0:T(8,128)(2,1)S(1)} %collective-permute-done.1.own2) | copy-start | bytes 786436
  70.3 0.7 copy-start.6
  71.1 10.4 %collective-permute-start.3 = (bf16[4,512,256]{2,1,0:T(8,128)(2,1)S(1)}, bf16[4,512,256]{2,1,0:T(8,128)(2,1)S(1)}, u32[]{:S(2)}, u32[]{:S(2)}) collective-permute-start(bf16[4,512,256]{2,1,0:T(8,128)(2,1)S(1)} %pad_maximum_fusion), channel_id=1, source_target_pairs={{0,16},{16,0},{1,17},{17,1},{2,18},{18,2},{3,19},{19,3},{4,20},{20... | collective-permute-start | bytes 3145736 | tf_op jit(solution)/shard_map/ppermute | solution.py:204
  73.2 6.6 %copy-start.8 = (bf16[384,256]{1,0:T(8,128)(2,1)}, bf16[384,256]{1,0:T(8,128)(2,1)S(1)}, u32[]{:S(2)}) copy-start(bf16[384,256]{1,0:T(8,128)(2,1)S(1)} %collective-permute-done.7.halo3) | copy-start | bytes 589828
  73.6 6.3 %copy-start.9 = (bf16[384,256]{1,0:T(8,128)(2,1)}, bf16[384,256]{1,0:T(8,128)(2,1)S(1)}, u32[]{:S(2)}) copy-start(bf16[384,256]{1,0:T(8,128)(2,1)S(1)} %collective-permute-done.6.halo2) | copy-start | bytes 589828
  76.1 3.8 %copy-start.10 = (bf16[384,256]{1,0:T(8,128)(2,1)}, bf16[384,256]{1,0:T(8,128)(2,1)S(1)}, u32[]{:S(2)}) copy-start(bf16[384,256]{1,0:T(8,128)(2,1)S(1)} %collective-permute-done.5.halo1) | copy-start | bytes 589828
  77.1 4.5 %collective-permute-start.8 = (bf16[4,384,256]{2,1,0:T(8,128)(2,1)}, bf16[4,384,256]{2,1,0:T(8,128)(2,1)}, u32[]{:S(2)}, u32[]{:S(2)}) collective-permute-start(bf16[4,384,256]{2,1,0:T(8,128)(2,1)} %pad_maximum_fusion.1), channel_id=1, source_target_pairs={{0,16},{16,0},{1,17},{17,1},{2,18},{18,2},{3,19},{19,3},{4,20},{20... | collective-permute-start | bytes 2359304 | tf_op jit(solution)/shard_map/ppermute | solution.py:205
  80.5 6.1 %copy-start.2 = (bf16[16,32,512]{2,1,0:T(8,128)(2,1)}, bf16[16,32,512]{2,1,0:T(8,128)(2,1)S(1)}, u32[]{:S(2)}) copy-start(bf16[16,32,512]{2,1,0:T(8,128)(2,1)S(1)} %all-to-all-done) | copy-start | bytes 1572868
  81.6 5.0 %copy-start.3 = (bf16[4,512,256]{2,1,0:T(8,128)(2,1)}, bf16[4,512,256]{2,1,0:T(8,128)(2,1)S(1)}, u32[]{:S(2)}) copy-start(bf16[4,512,256]{2,1,0:T(8,128)(2,1)S(1)} %collective-permute-done.3.own_other) | copy-start | bytes 3145732
  115.5 5.9 %collective-permute-start.9 = (bf16[4,896,256]{2,1,0:T(8,128)(2,1)}, bf16[4,896,256]{2,1,0:T(8,128)(2,1)S(1)}, u32[]{:S(2)}, u32[]{:S(2)}) collective-permute-start(bf16[4,896,256]{2,1,0:T(8,128)(2,1)} %get-tuple-element.8), channel_id=1, source_target_pairs={{0,16},{16,0},{1,17},{17,1},{2,18},{18,2},{3,19},{19,3},{4,20},{20... | collective-permute-start | bytes 5505032 | tf_op jit(solution)/shard_map/ppermute | solution.py:213
  125.9 25.2 %collective-permute-start.10 = (bf16[896,256]{1,0:T(8,128)(2,1)S(1)}, bf16[896,256]{1,0:T(8,128)(2,1)S(1)}, u32[]{:S(2)}, u32[]{:S(2)}) collective-permute-start(bf16[896,256]{1,0:T(8,128)(2,1)S(1)} %get-tuple-element.13), channel_id=1, source_target_pairs={{0,4},{4,8},{8,12},{12,0},{1,5},{5,9},{9,13},{13,1},{2,6},{6,10},{... | collective-permute-start | bytes 1376264 | tf_op jit(solution)/shard_map/ppermute | solution.py:216
  131.2 24.0 %collective-permute-start.12 = (bf16[896,256]{1,0:T(8,128)(2,1)S(1)}, bf16[896,256]{1,0:T(8,128)(2,1)S(1)}, u32[]{:S(2)}, u32[]{:S(2)}) collective-permute-start(bf16[896,256]{1,0:T(8,128)(2,1)S(1)} %get-tuple-element.14), channel_id=1, source_target_pairs={{0,12},{4,0},{8,4},{12,8},{1,13},{5,1},{9,5},{13,9},{2,14},{6,2},{... | collective-permute-start | bytes 1376264 | tf_op jit(solution)/shard_map/ppermute | solution.py:216
  133.1 22.1 %collective-permute-start.11 = (bf16[896,256]{1,0:T(8,128)(2,1)S(1)}, bf16[896,256]{1,0:T(8,128)(2,1)S(1)}, u32[]{:S(2)}, u32[]{:S(2)}) collective-permute-start(bf16[896,256]{1,0:T(8,128)(2,1)S(1)} %get-tuple-element.15), channel_id=1, source_target_pairs={{0,8},{4,12},{8,0},{12,4},{1,9},{5,13},{9,1},{13,5},{2,10},{6,14},... | collective-permute-start | bytes 1376264 | tf_op jit(solution)/shard_map/ppermute | solution.py:216
  136.5 29.9 %all-to-all-start.2 = ((bf16[16,32,256]{2,1,0:T(8,128)(2,1)}), bf16[16,32,256]{2,1,0:T(8,128)(2,1)S(1)}, u32[]{:S(2)}, u32[]{:S(2)}) async-start(bf16[16,32,256]{2,1,0:T(8,128)(2,1)} %bitcast.25), calls=%async_computation.2 | async-start | bytes 524288 | tf_op jit(solution)/shard_map/all_to_all | solution.py:210
  156.6 7.8 %collective-permute-start.13 = (bf16[384,256]{1,0:T(8,128)(2,1)S(1)}, bf16[384,256]{1,0:T(8,128)(2,1)S(1)}, u32[]{:S(2)}, u32[]{:S(2)}) collective-permute-start(bf16[384,256]{1,0:T(8,128)(2,1)S(1)} %slice.120), channel_id=1, source_target_pairs={{128,0},{256,128},{384,256},{129,1},{257,129},{385,257},{130,2},{2... | collective-permute-start | bytes 589832 | tf_op jit(solution)/shard_map/ppermute | solution.py:217
  166.4 28.2 %all-to-all-start.3 = ((bf16[16,32,256]{2,1,0:T(8,128)(2,1)}), bf16[16,32,256]{2,1,0:T(8,128)(2,1)S(1)}, u32[]{:S(2)}, u32[]{:S(2)}) async-start(bf16[16,32,256]{2,1,0:T(8,128)(2,1)} %bitcast.31), calls=%async_computation.3 | async-start | bytes 524288 | tf_op jit(solution)/shard_map/all_to_all | solution.py:221

commit v2 on v1

v2 whole, which is shorter than its diff:
```python
import jax
import jax.numpy as jnp
from jax import lax
from jax.experimental import pallas as pl
from jax.experimental.pallas import tpu as pltpu
from jax.sharding import Mesh, PartitionSpec as P

HEAD_DIM = 128
WINDOW = 4096
SOFT_CAP = 50.0
SCORE_SCALE = 1.0 / 12.0
LOG2_E = 1.4426950408889634

X, ZH, CORE, Y, ZL = 4, 4, 2, 4, 4
HEADS = ZH * ZL
SLAB = 4096
RUN = 128
RUNS = ZH + 1
SLOTS = 2 * RUNS
KB = 256
BLOCKS = SLOTS * 512 // KB
MOST = 14
PACK_STEP = 1 << 15


def token_codes(positions, pack_table):
    starts = pack_table[:, 0]
    pack_id = jnp.sum((positions[:, None] >= starts[None, :]).astype(jnp.int32), axis=1) - 1
    chosen = pack_id[:, None] == jnp.arange(pack_table.shape[0], dtype=jnp.int32)[None, :]
    bounds = jnp.sum(jnp.where(chosen[:, :, None], pack_table[None, :, :], 0), axis=1)
    role = (positions >= bounds[:, 1]).astype(jnp.int32) + (positions >= bounds[:, 2]).astype(
        jnp.int32
    )
    logical = (
        jnp.where(role == 2, positions - bounds[:, 2] + bounds[:, 1], positions) - bounds[:, 0]
    )
    return pack_id, logical, role, bounds[:, 0]


def by_two(low, stop, step, carry):
    pairs = (stop - low) // 2

    def both(i, carry):
        return step(low + 2 * i + 1, step(low + 2 * i, carry))

    carry = lax.fori_loop(0, pairs, both, carry)
    return lax.fori_loop(low + 2 * pairs, stop, step, carry)


def attend(
    where_ref, query_code_ref, key_code_ref, qg_ref, tail_ref,
    five0, five1, five2, five3, other_five,
    dq_ref, mine_ref, other_ref,
    keys, values, keys_t, values_t, ratios, expos, sums,
):
    y = where_ref[2 * RUNS]
    core = where_ref[2 * RUNS + 1]
    f32, b16 = jnp.float32, jnp.bfloat16

    def slot_of(run, side):
        return 2 * run + 1 + side if run < ZH else 9 * (1 - side)

    def place(slot, row, piece):
        block = slot * 2 + row // 2
        at = pl.multiple_of((row % 2) * RUN, RUN)
        keys[block, pl.ds(at, RUN), :] = piece[:, :HEAD_DIM]
        values[block, pl.ds(at, RUN), :] = piece[:, HEAD_DIM:]

    for dy, five in enumerate((five0, five1, five2, five3)):
        row = (y + dy) % Y
        for run in range(RUNS):
            rows = slice(run * RUN, (run + 1) * RUN)
            place(slot_of(run, core), row, five[rows, :])
            place(slot_of(run, 1 - core), row, other_five[dy, rows, :])

    for block in range(BLOCKS):
        keys_t[block] = keys[block].T
        values_t[block] = values[block].T
        sums[block] = jnp.zeros((KB, 2 * HEAD_DIM), f32)

    def one_run(run, source, rows):
        low = where_ref[run]
        high = where_ref[RUNS + run]
        query = jnp.concatenate([source[rows, 0:128], source[rows, 128:256]], axis=0)
        grad = jnp.concatenate([source[rows, 256:384], source[rows, 384:512]], axis=0)
        query_t = query.T
        grad_t = grad.T
        query_code = query_code_ref[run : run + 1, :]

        def forward(block, carry):
            total, weighted = carry
            raw = jnp.dot(keys[block], query_t, preferred_element_type=f32)
            ratio = jnp.tanh(raw * (SCORE_SCALE / SOFT_CAP))
            expo = jnp.exp2(ratio * (SOFT_CAP * LOG2_E))
            gap = query_code - key_code_ref[pl.ds(pl.multiple_of(block * KB, KB), KB), :]
            seen = (gap >= 0) & (gap < 8 * WINDOW) & ((gap & 7) != 1)
            expo = jnp.concatenate(
                [jnp.where(seen, expo[:, :RUN], 0.0), jnp.where(seen, expo[:, RUN:], 0.0)], axis=1
            )
            ratios[block - low] = ratio
            expos[block - low] = expo
            total = total + jnp.sum(expo, axis=0, keepdims=True)
            weighted = weighted + jnp.dot(
                values_t[block], expo.astype(b16), preferred_element_type=f32
            )
            return total, weighted

        total, weighted = by_two(
            low, high + 1, forward,
            (jnp.zeros((1, 2 * RUN), f32), jnp.zeros((HEAD_DIM, 2 * RUN), f32)),
        )
        scale = jnp.where(total > 0.0, 1.0 / total, 0.0)
        delta = jnp.sum(grad_t.astype(f32) * weighted, axis=0, keepdims=True) * scale

        def backward(block, dq_t):
            ratio = ratios[block - low]
            prob = expos[block - low] * scale
            dprob = jnp.dot(values[block], grad_t, preferred_element_type=f32)
            dscore = prob * (dprob - delta) * ((1.0 - ratio * ratio) * SCORE_SCALE)
            dscore = dscore.astype(b16)
            dq_t = dq_t + jnp.dot(keys_t[block], dscore, preferred_element_type=f32)
            dk = jnp.dot(dscore, query, preferred_element_type=f32)
            dv = jnp.dot(prob.astype(b16), grad, preferred_element_type=f32)
            sums[block] = sums[block] + jnp.concatenate([dk, dv], axis=1)
            return dq_t

        dq_t = by_two(low, high + 1, backward, jnp.zeros((HEAD_DIM, 2 * RUN), f32))
        out = slice(run * RUN, (run + 1) * RUN)
        dq_ref[out, 0:128] = dq_t[:, :RUN].T.astype(b16)
        dq_ref[out, 128:256] = dq_t[:, RUN:].T.astype(b16)

    for run in range(ZH):
        one_run(run, qg_ref, slice(run * RUN, (run + 1) * RUN))

    @pl.when(core == 0)
    def _():
        one_run(ZH, tail_ref, slice(0, RUN))

    @pl.when(core != 0)
    def _():
        dq_ref[ZH * RUN :, :] = jnp.zeros((RUN, 256), b16)

    for dy in range(Y):
        row = (y + dy) % Y
        at = pl.multiple_of((row % 2) * RUN, RUN)
        for run in range(RUNS):
            rows = slice(run * RUN, (run + 1) * RUN)
            mine_ref[dy, rows, :] = sums[slot_of(run, core) * 2 + row // 2, pl.ds(at, RUN), :]
            other_ref[dy, rows, :] = sums[
                slot_of(run, 1 - core) * 2 + row // 2, pl.ds(at, RUN), :
            ].astype(b16)


def call_attend(where, query_code, key_code, qg, tail, pieces):
    vmem = pl.BlockSpec(memory_space=pltpu.VMEM)
    rows = RUNS * RUN
    return pl.pallas_call(
        attend,
        out_shape=(
            jax.ShapeDtypeStruct((rows, 256), jnp.bfloat16),
            jax.ShapeDtypeStruct((Y, rows, 256), jnp.float32),
            jax.ShapeDtypeStruct((Y, rows, 256), jnp.bfloat16),
        ),
        in_specs=[pl.BlockSpec(memory_space=pltpu.SMEM)] + [vmem] * 9,
        out_specs=(vmem, vmem, vmem),
        scratch_shapes=[
            pltpu.VMEM((BLOCKS, KB, HEAD_DIM), jnp.bfloat16),
            pltpu.VMEM((BLOCKS, KB, HEAD_DIM), jnp.bfloat16),
            pltpu.VMEM((BLOCKS, HEAD_DIM, KB), jnp.bfloat16),
            pltpu.VMEM((BLOCKS, HEAD_DIM, KB), jnp.bfloat16),
            pltpu.VMEM((MOST, KB, 2 * RUN), jnp.float32),
            pltpu.VMEM((MOST, KB, 2 * RUN), jnp.float32),
            pltpu.VMEM((BLOCKS, KB, 2 * HEAD_DIM), jnp.float32),
        ],
        compiler_params=pltpu.CompilerParams(vmem_limit_bytes=50 << 20),
        name="attend",
    )(where, query_code, key_code, qg, tail, *pieces)


def tables(x, core, y, pack_table):
    first = x * SLAB - 512
    pack, logical, role, _ = token_codes(
        first + jnp.arange(SLOTS * 512, dtype=jnp.int32), pack_table
    )
    key_code = jnp.broadcast_to(
        (8 * (pack * PACK_STEP + logical) + role)[:, None], (SLOTS * 512, RUN)
    )
    runs = jnp.arange(RUNS, dtype=jnp.int32)
    tail = runs == ZH
    begin = x * SLAB + runs * 1024 + jnp.where(tail, 0, core * 512) + y * RUN
    position = begin[:, None] + jnp.arange(RUN, dtype=jnp.int32)[None, :]
    pack, logical, role, start = (
        part.reshape(RUNS, RUN) for part in token_codes(position.reshape(-1), pack_table)
    )
    home = pack // 2
    taken = jnp.where(tail[:, None], (home == x) & (core == 0), home >= x)
    taken = taken & (position < pack_table[-1, 3])
    query_code = jnp.where(taken, 8 * (pack * PACK_STEP + logical) + 4 - role, -(1 << 30))
    high = (begin - first) // KB
    low = (jnp.min(jnp.where(taken, start, 1 << 28), axis=1) - first) // KB
    low = jnp.maximum(jnp.maximum(low, high - (MOST - 1)), 0)
    some = jnp.any(taken, axis=1)
    low, high = jnp.where(some, low, 1), jnp.where(some, high, 0)
    where = jnp.concatenate([low, high, jnp.stack([y, core])])
    return where, query_code, key_code


def ring(size, by):
    return [(i, (i + by) % size) for i in range(size)]


def local(query_states, key_states, value_states, grad_out, pack_table):
    b16, f32 = jnp.bfloat16, jnp.float32
    x, core, y = lax.axis_index("x"), lax.axis_index("core"), lax.axis_index("y")
    z = ("zh", "zl")
    tokens = query_states.shape[0]
    borders = [(2 * i, 2 * i - 2) for i in range(1, X)] + [
        (2 * i + 1, 2 * i + 3) for i in range(X - 1)
    ]
    back = [(b, a) for a, b in borders]
    tails = [(2 * i, 2 * i - 2) for i in range(1, X)]

    def by_head(value):
        return jnp.transpose(value.reshape(tokens, HEADS, -1), (1, 0, 2))

    kv = jnp.concatenate([by_head(key_states), by_head(value_states)], axis=2)
    kv = lax.all_to_all(kv, z, split_axis=0, concat_axis=0, tiled=True).reshape(ZH * RUN, 256)
    qg = jnp.concatenate([by_head(query_states), by_head(grad_out)], axis=2)
    where, query_code, key_code = tables(x, core, y, pack_table)
    qg, where, query_code, key_code = lax.optimization_barrier((qg, where, query_code, key_code))
    qg = lax.all_to_all(qg, z, split_axis=0, concat_axis=0, tiled=True).reshape(ZH * RUN, 512)

    border = lax.dynamic_slice(kv, (core * (ZH - 1) * RUN, 0), (RUN, 256))
    border = lax.ppermute(border, ("x", "core"), borders)
    five = jnp.concatenate([kv, border], axis=0)
    fives = [five] + [lax.ppermute(five, "y", ring(Y, -dy)) for dy in range(1, Y)]
    other_five = lax.ppermute(jnp.stack(fives), "core", ring(CORE, 1))
    tail = lax.ppermute(qg[:RUN], ("x", "core"), tails)
    dq, mine, other = call_attend(
        where, query_code, key_code, qg, tail, (*fives, other_five)
    )

    dq_tail = lax.ppermute(dq[ZH * RUN :], ("x", "core"), [(b, a) for a, b in tails])
    dq = jnp.concatenate(
        [(dq[:RUN].astype(f32) + dq_tail.astype(f32)).astype(b16), dq[RUN : ZH * RUN]], axis=0
    )
    dq = lax.all_to_all(dq.reshape(HEADS, tokens, 256), z, split_axis=0, concat_axis=0, tiled=True)
    grad_query = jnp.transpose(dq, (1, 0, 2)).reshape(tokens, HEADS * 256)

    part = mine + lax.ppermute(other, "core", ring(CORE, 1)).astype(f32)
    total = part[0]
    for dy in range(1, Y):
        total = total + lax.ppermute(part[dy].astype(b16), "y", ring(Y, dy)).astype(f32)
    border = lax.ppermute(total[ZH * RUN :].astype(b16), ("x", "core"), back).astype(f32)
    gap = (ZH - 1) * RUN
    total = total[: ZH * RUN] + jnp.where(
        core == 0, jnp.pad(border, ((0, gap), (0, 0))), jnp.pad(border, ((gap, 0), (0, 0)))
    )
    dkv = lax.all_to_all(
        total.astype(b16).reshape(HEADS, tokens, 256), z, split_axis=0, concat_axis=0, tiled=True
    )
    dkv = jnp.transpose(dkv, (1, 0, 2))
    grad_key = dkv[:, :, :HEAD_DIM].reshape(tokens, HEADS * HEAD_DIM)
    grad_value = dkv[:, :, HEAD_DIM:].reshape(tokens, HEADS * HEAD_DIM)
    return grad_query, grad_key, grad_value


def solution(mesh):
    axes = ("x", "zh", "core", "y", "zl")
    fine = Mesh(mesh.devices.reshape(X, ZH, CORE, Y, ZL), axes)
    spread = P(axes, None)
    return jax.shard_map(
        local,
        mesh=fine,
        in_specs=(spread, spread, spread, spread, P()),
        out_specs=(spread, spread, spread),
        check_vma=False,
    )
```

time: 197 us -> 182 us (0.924)
  the two profiles are of different devices: /device:TPU:44 before, /device:TPU:36 now
where the time goes in v2:
time: 182 us; the launch traced here: 181 us
  starting transfers between devices  78.9 us (43%)
  waiting for transfers between devices  58.7 us (32%)
  Pallas kernels  26.5 us (15%)
  local copies, waits for them, and re-layouts  8.26 us (5%)
  other arithmetic  7.47 us (4%)
    pallas_call x1, Pallas kernels, call_attend(): pl.pallas_call(attend, out_shape=(jax.ShapeDtypeStruct((rows, 256), jnp.b...  26.5 us
    all_to_all x1, starting transfers between devices, local(): lax.all_to_all(kv, z, split_axis=0, concat_axis=0, tiled=True)  15.2 us
    all_to_all x1, waiting for transfers between devices, local(): lax.all_to_all(total.astype(b16).reshape(HEADS, tokens, 256), z, split_ax...  13.9 us
    all_to_all x1, starting transfers between devices, local(): lax.all_to_all(dq.reshape(HEADS, tokens, 256), z, split_axis=0, concat_ax...  12.3 us
    all_to_all x1, starting transfers between devices, local(): lax.all_to_all(total.astype(b16).reshape(HEADS, tokens, 256), z, split_ax...  12 us
    ppermute x3, starting transfers between devices, local(): lax.ppermute(five, 'y', ring(Y, -dy))  11.6 us
    all_to_all x1, waiting for transfers between devices, local(): lax.all_to_all(kv, z, split_axis=0, concat_axis=0, tiled=True)  10.9 us
    ppermute x3, starting transfers between devices, local(): lax.ppermute(part[dy].astype(b16), 'y', ring(Y, dy)).astype(f32)  8.97 us
  transfers between devices with their start and end apart: 16, of which 12 were waited for; matrix products, arithmetic and copies ran while one was open for 6% of the time, Pallas kernels for 0%

profile of v2, /device:TPU:36, one launch (start us, length us, event | category | flops | bytes accessed | tf_op | source)
XLA Modules:
  0.0 180.8 jit_solution(3055068570847988461)
XLA Ops:
  1.5 1.0 bitcast_bitcast_fusion.2
  3.3 15.2 %all-to-all-start.1 = ((bf16[16,32,256]{2,1,0:T(8,128)(2,1)}), bf16[16,32,256]{2,1,0:T(8,128)(2,1)S(1)}, u32[]{:S(2)}, u32[]{:S(2)}) async-start(bf16[16,32,256]{2,1,0:T(8,128)(2,1)} %pad_maximum_fusion.3), calls=%async_computation.1 | async-start | bytes 524288 | tf_op jit(solution)/shard_map/all_to_all | solution.py:227
  22.1 3.4 %broadcast_in_dim.98.key_code_ref = s32[5120,128]{1,0:T(8,128)} broadcast(s32[5120]{0:T(1024)S(1)} %bitcast.138), dimensions={0} | broadcast | bytes 2641920 | tf_op jit(solution)/shard_map/broadcast_in_dim | solution.py:185
  25.5 10.9 %all-to-all-done.1 = bf16[16,32,256]{2,1,0:T(8,128)(2,1)S(1)} async-done(((bf16[16,32,256]{2,1,0:T(8,128)(2,1)}), bf16[16,32,256]{2,1,0:T(8,128)(2,1)S(1)}, u32[]{:S(2)}, u32[]{:S(2)}) %all-to-all-start.1) | async-done | bytes 262176 | tf_op jit(solution)/shard_map/all_to_all | solution.py:227
  36.4 6.2 %all-to-all-start = ((bf16[16,32,512]{2,1,0:T(8,128)(2,1)}), bf16[16,32,512]{2,1,0:T(8,128)(2,1)S(1)}, u32[]{:S(2)}, u32[]{:S(2)}) async-start(bf16[16,32,512]{2,1,0:T(8,128)(2,1)} %pad_maximum_fusion.1), calls=%async_computation | async-start | bytes 1048576 | tf_op jit(solution)/shard_map/all_to_all | solution.py:231
  42.7 2.4 %collective-permute-start.1 = (bf16[128,256]{1,0:T(8,128)(2,1)S(1)}, bf16[128,256]{1,0:T(8,128)(2,1)S(1)}, u32[]{:S(2)}, u32[]{:S(2)}) collective-permute-start(bf16[128,256]{1,0:T(8,128)(2,1)S(1)} %constant_dynamic-slice_fusion), channel_id=1, source_target_pairs={{128,0},{256,128},{384,256},{16,144},{144,272},{272,400},{129,1},{... | collective-permute-start | bytes 196616 | tf_op jit(solution)/shard_map/ppermute | solution.py:234
  45.1 3.7 %collective-permute-done.1 = bf16[128,256]{1,0:T(8,128)(2,1)S(1)} collective-permute-done((bf16[128,256]{1,0:T(8,128)(2,1)S(1)}, bf16[128,256]{1,0:T(8,128)(2,1)S(1)}, u32[]{:S(2)}, u32[]{:S(2)}) %collective-permute-start.1) | collective-permute-done | bytes 65568 | tf_op jit(solution)/shard_map/ppermute | solution.py:234
  48.9 3.5 %collective-permute-start.4 = (bf16[640,256]{1,0:T(8,128)(2,1)S(1)}, bf16[640,256]{1,0:T(8,128)(2,1)S(1)}, u32[]{:S(2)}, u32[]{:S(2)}) collective-permute-start(bf16[640,256]{1,0:T(8,128)(2,1)S(1)} %get-tuple-element.30.five0), channel_id=1, source_target_pairs={{0,4},{4,8},{8,12},{12,0},{1,5},{5,9},{9,13},{13,1},{2,6},{6,10},{... | collective-permute-start | bytes 983048 | tf_op jit(solution)/shard_map/ppermute | solution.py:236
  52.4 4.8 %collective-permute-start.3 = (bf16[640,256]{1,0:T(8,128)(2,1)S(1)}, bf16[640,256]{1,0:T(8,128)(2,1)S(1)}, u32[]{:S(2)}, u32[]{:S(2)}) collective-permute-start(bf16[640,256]{1,0:T(8,128)(2,1)S(1)} %get-tuple-element.30.five0), channel_id=1, source_target_pairs={{0,8},{4,12},{8,0},{12,4},{1,9},{5,13},{9,1},{13,5},{2,10},{6,14},... | collective-permute-start | bytes 983048 | tf_op jit(solution)/shard_map/ppermute | solution.py:236
  57.2 3.3 %collective-permute-start.2 = (bf16[640,256]{1,0:T(8,128)(2,1)S(1)}, bf16[640,256]{1,0:T(8,128)(2,1)S(1)}, u32[]{:S(2)}, u32[]{:S(2)}) collective-permute-start(bf16[640,256]{1,0:T(8,128)(2,1)S(1)} %get-tuple-element.30.five0), channel_id=1, source_target_pairs={{0,12},{4,0},{8,4},{12,8},{1,13},{5,1},{9,5},{13,9},{2,14},{6,2},{... | collective-permute-start | bytes 983048 | tf_op jit(solution)/shard_map/ppermute | solution.py:236
  60.4 1.0 collective-permute-done.4.five3
  61.4 6.5 %collective-permute-done.3.five2 = bf16[640,256]{1,0:T(8,128)(2,1)S(1)} collective-permute-done((bf16[640,256]{1,0:T(8,128)(2,1)S(1)}, bf16[640,256]{1,0:T(8,128)(2,1)S(1)}, u32[]{:S(2)}, u32[]{:S(2)}) %collective-permute-start.3) | collective-permute-done | bytes 327712 | tf_op jit(solution)/shard_map/ppermute | solution.py:236
  67.9 1.3 collective-permute-done.2.five1
  69.4 1.9 %collective-permute-start.5 = (bf16[4,640,256]{2,1,0:T(8,128)(2,1)S(1)}, bf16[4,640,256]{2,1,0:T(8,128)(2,1)}, u32[]{:S(2)}, u32[]{:S(2)}) collective-permute-start(bf16[4,640,256]{2,1,0:T(8,128)(2,1)S(1)} %pad_maximum_fusion), channel_id=1, source_target_pairs={{0,16},{16,0},{1,17},{17,1},{2,18},{18,2},{3,19},{19,3},{4,20},{20... | collective-permute-start | bytes 3932168 | tf_op jit(solution)/shard_map/ppermute | solution.py:237
  71.4 2.4 %collective-permute-start = (bf16[128,512]{1,0:T(8,128)(2,1)S(1)}, bf16[128,512]{1,0:T(8,128)(2,1)S(1)}, u32[]{:S(2)}, u32[]{:S(2)}) collective-permute-start(bf16[128,512]{1,0:T(8,128)(2,1)S(1)} %bitcast.137), channel_id=1, source_target_pairs={{128,0},{256,128},{384,256},{129,1},{257,129},{385,257},{130,2},{2... | collective-permute-start | bytes 393224 | tf_op jit(solution)/shard_map/ppermute | solution.py:238
  73.8 4.4 %collective-permute-done.tail_ref = bf16[128,512]{1,0:T(8,128)(2,1)S(1)} collective-permute-done((bf16[128,512]{1,0:T(8,128)(2,1)S(1)}, bf16[128,512]{1,0:T(8,128)(2,1)S(1)}, u32[]{:S(2)}, u32[]{:S(2)}) %collective-permute-start) | collective-permute-done | bytes 131104 | tf_op jit(solution)/shard_map/ppermute | solution.py:238
  78.2 26.5 %attend.1 = (bf16[640,256]{1,0:T(8,128)(2,1)S(1)}, f32[4,640,256]{2,1,0:T(8,128)}, bf16[4,640,256]{2,1,0:T(8,128)(2,1)S(1)}) custom-call(s32[12]{0:T(128)S(1)} %pad_add_fusion.where_ref, s32[5,128]{1,0:T(8,128)S(1)} %get-tuple-element.11.query_code_ref, s32[5120,128]{1,0:T(8,128)} %broadcast_in_dim.98.key_code_ref, bf16[512,512]{1,0:T(8,128)(2,1)S(1)} %bitcast.124, ...), custom_call_target="tpu_custom_call" | custom-call | tf_op jit(solution)/shard_map/attend/pallas_call | solution.py:157
  104.7 1.9 %collective-permute-start.7 = (bf16[4,640,256]{2,1,0:T(8,128)(2,1)S(1)}, bf16[4,640,256]{2,1,0:T(8,128)(2,1)S(1)}, u32[]{:S(2)}, u32[]{:S(2)}) collective-permute-start(bf16[4,640,256]{2,1,0:T(8,128)(2,1)S(1)} %get-tuple-element.16), channel_id=1, source_target_pairs={{0,16},{16,0},{1,17},{17,1},{2,18},{18,2},{3,19},{19,3},{4,20},{20... | collective-permute-start | bytes 3932168 | tf_op jit(solution)/shard_map/ppermute | solution.py:250
  106.7 1.9 %collective-permute-start.6 = (bf16[128,256]{1,0:T(8,128)(2,1)S(1)}, bf16[128,256]{1,0:T(8,128)(2,1)S(1)}, u32[]{:S(2)}, u32[]{:S(2)}) collective-permute-start(bf16[128,256]{1,0:T(8,128)(2,1)S(1)} %slice.84), channel_id=1, source_target_pairs={{0,128},{128,256},{256,384},{1,129},{129,257},{257,385},{2,130},{1... | collective-permute-start | bytes 196616 | tf_op jit(solution)/shard_map/ppermute | solution.py:243
  108.6 4.2 %collective-permute-done.6 = bf16[128,256]{1,0:T(8,128)(2,1)S(1)} collective-permute-done((bf16[128,256]{1,0:T(8,128)(2,1)S(1)}, bf16[128,256]{1,0:T(8,128)(2,1)S(1)}, u32[]{:S(2)}, u32[]{:S(2)}) %collective-permute-start.6) | collective-permute-done | bytes 65568 | tf_op jit(solution)/shard_map/ppermute | solution.py:243
  113.6 12.3 %all-to-all-start.2 = ((bf16[16,32,256]{2,1,0:T(8,128)(2,1)}), bf16[16,32,256]{2,1,0:T(8,128)(2,1)S(1)}, u32[]{:S(2)}, u32[]{:S(2)}) async-start(bf16[16,32,256]{2,1,0:T(8,128)(2,1)} %bitcast.19), calls=%async_computation.2 | async-start | bytes 524288 | tf_op jit(solution)/shard_map/all_to_all | solution.py:247
  125.9 2.1 %fusion.24 = (bf16[4,640,256]{2,1,0:T(8,128)(2,1)S(1)}, f32[4,640,256]{2,1,0:T(8,128)S(1)}) fusion(f32[4,640,256]{2,1,0:T(8,128)} %get-tuple-element.15, bf16[4,640,256]{2,1,0:T(8,128)(2,1)S(1)} %collective-permute-done.7), kind=kLoop, calls=%fused_computation.90 | loop fusion | flops 1966080 | bytes 7864320 | tf_op jit(solution)/shard_map/convert.3
  128.1 1.9 %collective-permute-start.8 = (bf16[640,256]{1,0:T(8,128)(2,1)S(1)}, bf16[640,256]{1,0:T(8,128)(2,1)S(1)}, u32[]{:S(2)}, u32[]{:S(2)}) collective-permute-start(bf16[640,256]{1,0:T(8,128)(2,1)S(1)} %get-tuple-element.26), channel_id=1, source_target_pairs={{0,4},{4,8},{8,12},{12,0},{1,5},{5,9},{9,13},{13,1},{2,6},{6,10},{... | collective-permute-start | bytes 983048 | tf_op jit(solution)/shard_map/ppermute | solution.py:253
  130.0 5.1 %collective-permute-start.10 = (bf16[640,256]{1,0:T(8,128)(2,1)S(1)}, bf16[640,256]{1,0:T(8,128)(2,1)S(1)}, u32[]{:S(2)}, u32[]{:S(2)}) collective-permute-start(bf16[640,256]{1,0:T(8,128)(2,1)S(1)} %get-tuple-element.27), channel_id=1, source_target_pairs={{0,12},{4,0},{8,4},{12,8},{1,13},{5,1},{9,5},{13,9},{2,14},{6,2},{... | collective-permute-start | bytes 983048 | tf_op jit(solution)/shard_map/ppermute | solution.py:253
  135.2 1.9 %collective-permute-start.9 = (bf16[640,256]{1,0:T(8,128)(2,1)S(1)}, bf16[640,256]{1,0:T(8,128)(2,1)S(1)}, u32[]{:S(2)}, u32[]{:S(2)}) collective-permute-start(bf16[640,256]{1,0:T(8,128)(2,1)S(1)} %get-tuple-element.28), channel_id=1, source_target_pairs={{0,8},{4,12},{8,0},{12,4},{1,9},{5,13},{9,1},{13,5},{2,10},{6,14},... | collective-permute-start | bytes 983048 | tf_op jit(solution)/shard_map/ppermute | solution.py:253
  137.1 4.7 %collective-permute-done.8 = bf16[640,256]{1,0:T(8,128)(2,1)S(1)} collective-permute-done((bf16[640,256]{1,0:T(8,128)(2,1)S(1)}, bf16[640,256]{1,0:T(8,128)(2,1)S(1)}, u32[]{:S(2)}, u32[]{:S(2)}) %collective-permute-start.8) | collective-permute-done | bytes 327712 | tf_op jit(solution)/shard_map/ppermute | solution.py:253
  141.8 1.8 collective-permute-done.10
  143.5 2.1 %collective-permute-done.9 = bf16[640,256]{1,0:T(8,128)(2,1)S(1)} collective-permute-done((bf16[640,256]{1,0:T(8,128)(2,1)S(1)}, bf16[640,256]{1,0:T(8,128)(2,1)S(1)}, u32[]{:S(2)}, u32[]{:S(2)}) %collective-permute-start.9) | collective-permute-done | bytes 327712 | tf_op jit(solution)/shard_map/ppermute | solution.py:253
  145.8 1.9 %collective-permute-start.11 = (bf16[128,256]{1,0:T(8,128)(2,1)S(1)}, bf16[128,256]{1,0:T(8,128)(2,1)S(1)}, u32[]{:S(2)}, u32[]{:S(2)}) collective-permute-start(bf16[128,256]{1,0:T(8,128)(2,1)S(1)} %slice.135), channel_id=1, source_target_pairs={{0,128},{128,256},{256,384},{144,16},{272,144},{400,272},{1,129},{... | collective-permute-start | bytes 196616 | tf_op jit(solution)/shard_map/ppermute | solution.py:254
  147.7 4.2 %collective-permute-done.11 = bf16[128,256]{1,0:T(8,128)(2,1)S(1)} collective-permute-done((bf16[128,256]{1,0:T(8,128)(2,1)S(1)}, bf16[128,256]{1,0:T(8,128)(2,1)S(1)}, u32[]{:S(2)}, u32[]{:S(2)}) %collective-permute-start.11) | collective-permute-done | bytes 65568 | tf_op jit(solution)/shard_map/ppermute | solution.py:254
  152.7 12.0 %all-to-all-start.3 = ((bf16[16,32,256]{2,1,0:T(8,128)(2,1)}), bf16[16,32,256]{2,1,0:T(8,128)(2,1)S(1)}, u32[]{:S(2)}, u32[]{:S(2)}) async-start(bf16[16,32,256]{2,1,0:T(8,128)(2,1)} %bitcast.25), calls=%async_computation.3 | async-start | bytes 524288 | tf_op jit(solution)/shard_map/all_to_all | solution.py:259
  165.5 13.9 %all-to-all-done.3 = bf16[16,32,256]{2,1,0:T(8,128)(2,1)S(1)} async-done(((bf16[16,32,256]{2,1,0:T(8,128)(2,1)}), bf16[16,32,256]{2,1,0:T(8,128)(2,1)S(1)}, u32[]{:S(2)}, u32[]{:S(2)}) %all-to-all-start.3) | async-done | bytes 262176 | tf_op jit(solution)/shard_map/all_to_all | solution.py:259
  (54 shorter events, 9.2 us)
Async XLA Ops:
  0.6 0.9 copy-start
  0.6 17.8 %copy-start.3 = (s32[8,4]{0,1:T(4,128)S(1)}, s32[8,4]{0,1:T(4,128)}, u32[]{:S(2)}) copy-start(s32[8,4]{0,1:T(4,128)} %param.9) | copy-start | bytes 388
  0.7 20.3 %copy-start.1 = (bf16[32,4096]{1,0:T(8,128)(2,1)S(1)}, bf16[32,4096]{1,0:T(8,128)(2,1)}, u32[]{:S(2)}) copy-start(bf16[32,4096]{1,0:T(8,128)(2,1)} %param.8) | copy-start | bytes 786436
  1.5 19.4 %copy-start.2 = (bf16[32,4096]{1,0:T(8,128)(2,1)S(1)}, bf16[32,4096]{1,0:T(8,128)(2,1)}, u32[]{:S(2)}) copy-start(bf16[32,4096]{1,0:T(8,128)(2,1)} %param.5) | copy-start | bytes 786436
  3.3 33.1 %all-to-all-start.1 = ((bf16[16,32,256]{2,1,0:T(8,128)(2,1)}), bf16[16,32,256]{2,1,0:T(8,128)(2,1)S(1)}, u32[]{:S(2)}, u32[]{:S(2)}) async-start(bf16[16,32,256]{2,1,0:T(8,128)(2,1)} %pad_maximum_fusion.3), calls=%async_computation.1 | async-start | bytes 524288 | tf_op jit(solution)/shard_map/all_to_all | solution.py:227
  36.4 34.9 %all-to-all-start = ((bf16[16,32,512]{2,1,0:T(8,128)(2,1)}), bf16[16,32,512]{2,1,0:T(8,128)(2,1)S(1)}, u32[]{:S(2)}, u32[]{:S(2)}) async-start(bf16[16,32,512]{2,1,0:T(8,128)(2,1)} %pad_maximum_fusion.1), calls=%async_computation | async-start | bytes 1048576 | tf_op jit(solution)/shard_map/all_to_all | solution.py:231
  42.7 6.2 %collective-permute-start.1 = (bf16[128,256]{1,0:T(8,128)(2,1)S(1)}, bf16[128,256]{1,0:T(8,128)(2,1)S(1)}, u32[]{:S(2)}, u32[]{:S(2)}) collective-permute-start(bf16[128,256]{1,0:T(8,128)(2,1)S(1)} %constant_dynamic-slice_fusion), channel_id=1, source_target_pairs={{128,0},{256,128},{384,256},{16,144},{144,272},{272,400},{129,1},{... | collective-permute-start | bytes 196616 | tf_op jit(solution)/shard_map/ppermute | solution.py:234
  48.9 12.6 %collective-permute-start.4 = (bf16[640,256]{1,0:T(8,128)(2,1)S(1)}, bf16[640,256]{1,0:T(8,128)(2,1)S(1)}, u32[]{:S(2)}, u32[]{:S(2)}) collective-permute-start(bf16[640,256]{1,0:T(8,128)(2,1)S(1)} %get-tuple-element.30.five0), channel_id=1, source_target_pairs={{0,4},{4,8},{8,12},{12,0},{1,5},{5,9},{9,13},{13,1},{2,6},{6,10},{... | collective-permute-start | bytes 983048 | tf_op jit(solution)/shard_map/ppermute | solution.py:236
  52.4 15.6 %collective-permute-start.3 = (bf16[640,256]{1,0:T(8,128)(2,1)S(1)}, bf16[640,256]{1,0:T(8,128)(2,1)S(1)}, u32[]{:S(2)}, u32[]{:S(2)}) collective-permute-start(bf16[640,256]{1,0:T(8,128)(2,1)S(1)} %get-tuple-element.30.five0), channel_id=1, source_target_pairs={{0,8},{4,12},{8,0},{12,4},{1,9},{5,13},{9,1},{13,5},{2,10},{6,14},... | collective-permute-start | bytes 983048 | tf_op jit(solution)/shard_map/ppermute | solution.py:236
  57.2 12.1 %collective-permute-start.2 = (bf16[640,256]{1,0:T(8,128)(2,1)S(1)}, bf16[640,256]{1,0:T(8,128)(2,1)S(1)}, u32[]{:S(2)}, u32[]{:S(2)}) collective-permute-start(bf16[640,256]{1,0:T(8,128)(2,1)S(1)} %get-tuple-element.30.five0), channel_id=1, source_target_pairs={{0,12},{4,0},{8,4},{12,8},{1,13},{5,1},{9,5},{13,9},{2,14},{6,2},{... | collective-permute-start | bytes 983048 | tf_op jit(solution)/shard_map/ppermute | solution.py:236
  69.4 8.8 %collective-permute-start.5 = (bf16[4,640,256]{2,1,0:T(8,128)(2,1)S(1)}, bf16[4,640,256]{2,1,0:T(8,128)(2,1)}, u32[]{:S(2)}, u32[]{:S(2)}) collective-permute-start(bf16[4,640,256]{2,1,0:T(8,128)(2,1)S(1)} %pad_maximum_fusion), channel_id=1, source_target_pairs={{0,16},{16,0},{1,17},{17,1},{2,18},{18,2},{3,19},{19,3},{4,20},{20... | collective-permute-start | bytes 3932168 | tf_op jit(solution)/shard_map/ppermute | solution.py:237
  71.4 6.9 %collective-permute-start = (bf16[128,512]{1,0:T(8,128)(2,1)S(1)}, bf16[128,512]{1,0:T(8,128)(2,1)S(1)}, u32[]{:S(2)}, u32[]{:S(2)}) collective-permute-start(bf16[128,512]{1,0:T(8,128)(2,1)S(1)} %bitcast.137), channel_id=1, source_target_pairs={{128,0},{256,128},{384,256},{129,1},{257,129},{385,257},{130,2},{2... | collective-permute-start | bytes 393224 | tf_op jit(solution)/shard_map/ppermute | solution.py:238
  104.7 21.2 %collective-permute-start.7 = (bf16[4,640,256]{2,1,0:T(8,128)(2,1)S(1)}, bf16[4,640,256]{2,1,0:T(8,128)(2,1)S(1)}, u32[]{:S(2)}, u32[]{:S(2)}) collective-permute-start(bf16[4,640,256]{2,1,0:T(8,128)(2,1)S(1)} %get-tuple-element.16), channel_id=1, source_target_pairs={{0,16},{16,0},{1,17},{17,1},{2,18},{18,2},{3,19},{19,3},{4,20},{20... | collective-permute-start | bytes 3932168 | tf_op jit(solution)/shard_map/ppermute | solution.py:250
  106.7 6.2 %collective-permute-start.6 = (bf16[128,256]{1,0:T(8,128)(2,1)S(1)}, bf16[128,256]{1,0:T(8,128)(2,1)S(1)}, u32[]{:S(2)}, u32[]{:S(2)}) collective-permute-start(bf16[128,256]{1,0:T(8,128)(2,1)S(1)} %slice.84), channel_id=1, source_target_pairs={{0,128},{128,256},{256,384},{1,129},{129,257},{257,385},{2,130},{1... | collective-permute-start | bytes 196616 | tf_op jit(solution)/shard_map/ppermute | solution.py:243
  113.6 39.2 %all-to-all-start.2 = ((bf16[16,32,256]{2,1,0:T(8,128)(2,1)}), bf16[16,32,256]{2,1,0:T(8,128)(2,1)S(1)}, u32[]{:S(2)}, u32[]{:S(2)}) async-start(bf16[16,32,256]{2,1,0:T(8,128)(2,1)} %bitcast.19), calls=%async_computation.2 | async-start | bytes 524288 | tf_op jit(solution)/shard_map/all_to_all | solution.py:247
  128.1 13.7 %collective-permute-start.8 = (bf16[640,256]{1,0:T(8,128)(2,1)S(1)}, bf16[640,256]{1,0:T(8,128)(2,1)S(1)}, u32[]{:S(2)}, u32[]{:S(2)}) collective-permute-start(bf16[640,256]{1,0:T(8,128)(2,1)S(1)} %get-tuple-element.26), channel_id=1, source_target_pairs={{0,4},{4,8},{8,12},{12,0},{1,5},{5,9},{9,13},{13,1},{2,6},{6,10},{... | collective-permute-start | bytes 983048 | tf_op jit(solution)/shard_map/ppermute | solution.py:253
  130.0 13.5 %collective-permute-start.10 = (bf16[640,256]{1,0:T(8,128)(2,1)S(1)}, bf16[640,256]{1,0:T(8,128)(2,1)S(1)}, u32[]{:S(2)}, u32[]{:S(2)}) collective-permute-start(bf16[640,256]{1,0:T(8,128)(2,1)S(1)} %get-tuple-element.27), channel_id=1, source_target_pairs={{0,12},{4,0},{8,4},{12,8},{1,13},{5,1},{9,5},{13,9},{2,14},{6,2},{... | collective-permute-start | bytes 983048 | tf_op jit(solution)/shard_map/ppermute | solution.py:253
  135.2 10.5 %collective-permute-start.9 = (bf16[640,256]{1,0:T(8,128)(2,1)S(1)}, bf16[640,256]{1,0:T(8,128)(2,1)S(1)}, u32[]{:S(2)}, u32[]{:S(2)}) collective-permute-start(bf16[640,256]{1,0:T(8,128)(2,1)S(1)} %get-tuple-element.28), channel_id=1, source_target_pairs={{0,8},{4,12},{8,0},{12,4},{1,9},{5,13},{9,1},{13,5},{2,10},{6,14},... | collective-permute-start | bytes 983048 | tf_op jit(solution)/shard_map/ppermute | solution.py:253
  145.8 6.2 %collective-permute-start.11 = (bf16[128,256]{1,0:T(8,128)(2,1)S(1)}, bf16[128,256]{1,0:T(8,128)(2,1)S(1)}, u32[]{:S(2)}, u32[]{:S(2)}) collective-permute-start(bf16[128,256]{1,0:T(8,128)(2,1)S(1)} %slice.135), channel_id=1, source_target_pairs={{0,128},{128,256},{256,384},{144,16},{272,144},{400,272},{1,129},{... | collective-permute-start | bytes 196616 | tf_op jit(solution)/shard_map/ppermute | solution.py:254
  152.7 26.7 %all-to-all-start.3 = ((bf16[16,32,256]{2,1,0:T(8,128)(2,1)}), bf16[16,32,256]{2,1,0:T(8,128)(2,1)S(1)}, u32[]{:S(2)}, u32[]{:S(2)}) async-start(bf16[16,32,256]{2,1,0:T(8,128)(2,1)} %bitcast.25), calls=%async_computation.3 | async-start | bytes 524288 | tf_op jit(solution)/shard_map/all_to_all | solution.py:259

commit v3 on v2

--- a/solution.py
+++ b/solution.py
@@ -47,18 +47,15 @@
     return lax.fori_loop(low + 2 * pairs, stop, step, carry)
 
 
-def attend(
-    where_ref, query_code_ref, key_code_ref, qg_ref, tail_ref,
-    five0, five1, five2, five3, other_five,
-    dq_ref, mine_ref, other_ref,
-    keys, values, keys_t, values_t, ratios, expos, sums,
+def slot_of(run, side):
+    return 2 * run + 1 + side if run < ZH else 9 * (1 - side)
+
+
+def arrange(
+    where_ref, five0, five1, five2, five3, other_five, keys, values, keys_t, values_t
 ):
     y = where_ref[2 * RUNS]
     core = where_ref[2 * RUNS + 1]
-    f32, b16 = jnp.float32, jnp.bfloat16
-
-    def slot_of(run, side):
-        return 2 * run + 1 + side if run < ZH else 9 * (1 - side)
 
     def place(slot, row, piece):
         block = slot * 2 + row // 2
@@ -76,6 +73,18 @@
     for block in range(BLOCKS):
         keys_t[block] = keys[block].T
         values_t[block] = values[block].T
+
+
+def attend(
+    where_ref, query_code_ref, key_code_ref, qg_ref, tail_ref, keys, values, keys_t, values_t,
+    dq_ref, mine_ref, other_ref,
+    ratios, expos, sums,
+):
+    y = where_ref[2 * RUNS]
+    core = where_ref[2 * RUNS + 1]
+    f32, b16 = jnp.float32, jnp.bfloat16
+
+    for block in range(BLOCKS):
         sums[block] = jnp.zeros((KB, 2 * HEAD_DIM), f32)
 
     def one_run(run, source, rows):
@@ -151,7 +160,21 @@
             ].astype(b16)
 
 
-def call_attend(where, query_code, key_code, qg, tail, pieces):
+def call_arrange(where, pieces):
+    vmem = pl.BlockSpec(memory_space=pltpu.VMEM)
+    straight = jax.ShapeDtypeStruct((BLOCKS, KB, HEAD_DIM), jnp.bfloat16)
+    turned = jax.ShapeDtypeStruct((BLOCKS, HEAD_DIM, KB), jnp.bfloat16)
+    return pl.pallas_call(
+        arrange,
+        out_shape=(straight, straight, turned, turned),
+        in_specs=[pl.BlockSpec(memory_space=pltpu.SMEM)] + [vmem] * 5,
+        out_specs=(vmem,) * 4,
+        compiler_params=pltpu.CompilerParams(vmem_limit_bytes=12 << 20),
+        name="arrange",
+    )(where, *pieces)
+
+
+def call_attend(where, query_code, key_code, qg, tail, arranged):
     vmem = pl.BlockSpec(memory_space=pltpu.VMEM)
     rows = RUNS * RUN
     return pl.pallas_call(
@@ -161,20 +184,16 @@
             jax.ShapeDtypeStruct((Y, rows, 256), jnp.float32),
             jax.ShapeDtypeStruct((Y, rows, 256), jnp.bfloat16),
         ),
-        in_specs=[pl.BlockSpec(memory_space=pltpu.SMEM)] + [vmem] * 9,
+        in_specs=[pl.BlockSpec(memory_space=pltpu.SMEM)] + [vmem] * 8,
         out_specs=(vmem, vmem, vmem),
         scratch_shapes=[
-            pltpu.VMEM((BLOCKS, KB, HEAD_DIM), jnp.bfloat16),
-            pltpu.VMEM((BLOCKS, KB, HEAD_DIM), jnp.bfloat16),
-            pltpu.VMEM((BLOCKS, HEAD_DIM, KB), jnp.bfloat16),
-            pltpu.VMEM((BLOCKS, HEAD_DIM, KB), jnp.bfloat16),
             pltpu.VMEM((MOST, KB, 2 * RUN), jnp.float32),
             pltpu.VMEM((MOST, KB, 2 * RUN), jnp.float32),
             pltpu.VMEM((BLOCKS, KB, 2 * HEAD_DIM), jnp.float32),
         ],
-        compiler_params=pltpu.CompilerParams(vmem_limit_bytes=50 << 20),
+        compiler_params=pltpu.CompilerParams(vmem_limit_bytes=32 << 20),
         name="attend",
-    )(where, query_code, key_code, qg, tail, *pieces)
+    )(where, query_code, key_code, qg, tail, *arranged)
 
 
 def tables(x, core, y, pack_table):
@@ -182,9 +201,8 @@
     pack, logical, role, _ = token_codes(
         first + jnp.arange(SLOTS * 512, dtype=jnp.int32), pack_table
     )
-    key_code = jnp.broadcast_to(
-        (8 * (pack * PACK_STEP + logical) + role)[:, None], (SLOTS * 512, RUN)
-    )
+    key_code = 8 * (pack * PACK_STEP + logical) + role
+    key_code = jnp.broadcast_to(key_code[:, None], (SLOTS * 512, RUN))
     runs = jnp.arange(RUNS, dtype=jnp.int32)
     tail = runs == ZH
     begin = x * SLAB + runs * 1024 + jnp.where(tail, 0, core * 512) + y * RUN
@@ -224,30 +242,34 @@
         return jnp.transpose(value.reshape(tokens, HEADS, -1), (1, 0, 2))
 
     kv = jnp.concatenate([by_head(key_states), by_head(value_states)], axis=2)
-    kv = lax.all_to_all(kv, z, split_axis=0, concat_axis=0, tiled=True).reshape(ZH * RUN, 256)
     qg = jnp.concatenate([by_head(query_states), by_head(grad_out)], axis=2)
+    kv = lax.all_to_all(kv, z, split_axis=0, concat_axis=0, tiled=True)
+    kv = kv.reshape(ZH * RUN, 256)
     where, query_code, key_code = tables(x, core, y, pack_table)
     qg, where, query_code, key_code = lax.optimization_barrier((qg, where, query_code, key_code))
-    qg = lax.all_to_all(qg, z, split_axis=0, concat_axis=0, tiled=True).reshape(ZH * RUN, 512)
+    qg = lax.all_to_all(qg, z, split_axis=0, concat_axis=0, tiled=True)
+    qg = qg.reshape(ZH * RUN, 512)
 
     border = lax.dynamic_slice(kv, (core * (ZH - 1) * RUN, 0), (RUN, 256))
     border = lax.ppermute(border, ("x", "core"), borders)
     five = jnp.concatenate([kv, border], axis=0)
     fives = [five] + [lax.ppermute(five, "y", ring(Y, -dy)) for dy in range(1, Y)]
-    other_five = lax.ppermute(jnp.stack(fives), "core", ring(CORE, 1))
+    stack = jnp.stack(fives)
+    other_five = lax.ppermute(stack, "core", ring(CORE, 1))
+    arranged = call_arrange(where, (*fives, other_five))
     tail = lax.ppermute(qg[:RUN], ("x", "core"), tails)
-    dq, mine, other = call_attend(
-        where, query_code, key_code, qg, tail, (*fives, other_five)
-    )
-
+    dq, mine, other = call_attend(where, query_code, key_code, qg, tail, arranged)
+
+    other = lax.ppermute(other, "core", ring(CORE, 1))
     dq_tail = lax.ppermute(dq[ZH * RUN :], ("x", "core"), [(b, a) for a, b in tails])
     dq = jnp.concatenate(
         [(dq[:RUN].astype(f32) + dq_tail.astype(f32)).astype(b16), dq[RUN : ZH * RUN]], axis=0
     )
-    dq = lax.all_to_all(dq.reshape(HEADS, tokens, 256), z, split_axis=0, concat_axis=0, tiled=True)
+    dq = dq.reshape(HEADS, tokens, 256)
+    dq = lax.all_to_all(dq, z, split_axis=0, concat_axis=0, tiled=True)
     grad_query = jnp.transpose(dq, (1, 0, 2)).reshape(tokens, HEADS * 256)
 
-    part = mine + lax.ppermute(other, "core", ring(CORE, 1)).astype(f32)
+    part = mine + other.astype(f32)
     total = part[0]
     for dy in range(1, Y):
         total = total + lax.ppermute(part[dy].astype(b16), "y", ring(Y, dy)).astype(f32)
@@ -256,9 +278,8 @@
     total = total[: ZH * RUN] + jnp.where(
         core == 0, jnp.pad(border, ((0, gap), (0, 0))), jnp.pad(border, ((gap, 0), (0, 0)))
     )
-    dkv = lax.all_to_all(
-        total.astype(b16).reshape(HEADS, tokens, 256), z, split_axis=0, concat_axis=0, tiled=True
-    )
+    dkv = total.astype(b16).reshape(HEADS, tokens, 256)
+    dkv = lax.all_to_all(dkv, z, split_axis=0, concat_axis=0, tiled=True)
     dkv = jnp.transpose(dkv, (1, 0, 2))
     grad_key = dkv[:, :, :HEAD_DIM].reshape(tokens, HEADS * HEAD_DIM)
     grad_value = dkv[:, :, HEAD_DIM:].reshape(tokens, HEADS * HEAD_DIM)

time: 182 us -> 181 us (level)
  the two profiles are of different devices: /device:TPU:36 before, /device:TPU:42 now
where the time goes in v3:
time: 181 us; the launch traced here: 180 us
  starting transfers between devices  80.4 us (44%)
  waiting for transfers between devices  58.6 us (32%)
  Pallas kernels  19.7 us (11%)
  local copies, waits for them, and re-layouts  11.7 us (6%)
  other arithmetic  8.56 us (5%)
    pallas_call x1, Pallas kernels, call_attend(): pl.pallas_call(attend, out_shape=(jax.ShapeDtypeStruct((rows, 256), jnp.b...  17.3 us
    all_to_all x1, starting transfers between devices, local(): kv = lax.all_to_all(kv, z, split_axis=0, concat_axis=0, tiled=True)  15.2 us
    all_to_all x1, waiting for transfers between devices, local(): dkv = lax.all_to_all(dkv, z, split_axis=0, concat_axis=0, tiled=True)  13.9 us
    all_to_all x1, waiting for transfers between devices, local(): kv = lax.all_to_all(kv, z, split_axis=0, concat_axis=0, tiled=True)  13.6 us
    all_to_all x1, starting transfers between devices, local(): dq = lax.all_to_all(dq, z, split_axis=0, concat_axis=0, tiled=True)  12.3 us
    all_to_all x1, starting transfers between devices, local(): dkv = lax.all_to_all(dkv, z, split_axis=0, concat_axis=0, tiled=True)  12 us
    ppermute x3, starting transfers between devices, local(): lax.ppermute(part[dy].astype(b16), 'y', ring(Y, dy)).astype(f32)  11.9 us
    ppermute x3, starting transfers between devices, local(): lax.ppermute(five, 'y', ring(Y, -dy))  10.7 us
  transfers between devices with their start and end apart: 16, of which 11 were waited for; matrix products, arithmetic and copies ran while one was open for 6% of the time, Pallas kernels for 1%

profile of v3, /device:TPU:42, one launch (start us, length us, event | category | flops | bytes accessed | tf_op | source)
XLA Modules:
  0.0 180.0 jit_solution(9470782627744136144)
XLA Ops:
  1.5 1.0 bitcast_bitcast_fusion.2
  3.3 15.2 %all-to-all-start.1 = ((bf16[16,32,256]{2,1,0:T(8,128)(2,1)}), bf16[16,32,256]{2,1,0:T(8,128)(2,1)S(1)}, u32[]{:S(2)}, u32[]{:S(2)}) async-start(bf16[16,32,256]{2,1,0:T(8,128)(2,1)} %pad_maximum_fusion.3), calls=%async_computation.1 | async-start | bytes 524288 | tf_op jit(solution)/shard_map/all_to_all | solution.py:246
  22.8 13.6 %all-to-all-done.1 = bf16[16,32,256]{2,1,0:T(8,128)(2,1)S(1)} async-done(((bf16[16,32,256]{2,1,0:T(8,128)(2,1)}), bf16[16,32,256]{2,1,0:T(8,128)(2,1)S(1)}, u32[]{:S(2)}, u32[]{:S(2)}) %all-to-all-start.1) | async-done | bytes 262176 | tf_op jit(solution)/shard_map/all_to_all | solution.py:246
  36.4 6.2 %all-to-all-start = ((bf16[16,32,512]{2,1,0:T(8,128)(2,1)}), bf16[16,32,512]{2,1,0:T(8,128)(2,1)S(1)}, u32[]{:S(2)}, u32[]{:S(2)}) async-start(bf16[16,32,512]{2,1,0:T(8,128)(2,1)} %pad_maximum_fusion.1), calls=%async_computation | async-start | bytes 1048576 | tf_op jit(solution)/shard_map/all_to_all | solution.py:250
  42.7 2.4 %collective-permute-start.1 = (bf16[128,256]{1,0:T(8,128)(2,1)S(1)}, bf16[128,256]{1,0:T(8,128)(2,1)S(1)}, u32[]{:S(2)}, u32[]{:S(2)}) collective-permute-start(bf16[128,256]{1,0:T(8,128)(2,1)S(1)} %constant_dynamic-slice_fusion), channel_id=1, source_target_pairs={{128,0},{256,128},{384,256},{16,144},{144,272},{272,400},{129,1},{... | collective-permute-start | bytes 196616 | tf_op jit(solution)/shard_map/ppermute | solution.py:254
  45.1 3.7 %collective-permute-done.1 = bf16[128,256]{1,0:T(8,128)(2,1)S(1)} collective-permute-done((bf16[128,256]{1,0:T(8,128)(2,1)S(1)}, bf16[128,256]{1,0:T(8,128)(2,1)S(1)}, u32[]{:S(2)}, u32[]{:S(2)}) %collective-permute-start.1) | collective-permute-done | bytes 65568 | tf_op jit(solution)/shard_map/ppermute | solution.py:254
  48.9 3.5 %collective-permute-start.4 = (bf16[640,256]{1,0:T(8,128)(2,1)S(1)}, bf16[640,256]{1,0:T(8,128)(2,1)S(1)}, u32[]{:S(2)}, u32[]{:S(2)}) collective-permute-start(bf16[640,256]{1,0:T(8,128)(2,1)S(1)} %get-tuple-element.38.five0), channel_id=1, source_target_pairs={{0,4},{4,8},{8,12},{12,0},{1,5},{5,9},{9,13},{13,1},{2,6},{6,10},{... | collective-permute-start | bytes 983048 | tf_op jit(solution)/shard_map/ppermute | solution.py:256
  52.4 2.8 %collective-permute-start.3 = (bf16[640,256]{1,0:T(8,128)(2,1)S(1)}, bf16[640,256]{1,0:T(8,128)(2,1)S(1)}, u32[]{:S(2)}, u32[]{:S(2)}) collective-permute-start(bf16[640,256]{1,0:T(8,128)(2,1)S(1)} %get-tuple-element.38.five0), channel_id=1, source_target_pairs={{0,8},{4,12},{8,0},{12,4},{1,9},{5,13},{9,1},{13,5},{2,10},{6,14},... | collective-permute-start | bytes 983048 | tf_op jit(solution)/shard_map/ppermute | solution.py:256
  55.2 4.3 %collective-permute-start.2 = (bf16[640,256]{1,0:T(8,128)(2,1)S(1)}, bf16[640,256]{1,0:T(8,128)(2,1)S(1)}, u32[]{:S(2)}, u32[]{:S(2)}) collective-permute-start(bf16[640,256]{1,0:T(8,128)(2,1)S(1)} %get-tuple-element.38.five0), channel_id=1, source_target_pairs={{0,12},{4,0},{8,4},{12,8},{1,13},{5,1},{9,5},{13,9},{2,14},{6,2},{... | collective-permute-start | bytes 983048 | tf_op jit(solution)/shard_map/ppermute | solution.py:256
  60.9 5.4 %collective-permute-done.3.five2 = bf16[640,256]{1,0:T(8,128)(2,1)S(1)} collective-permute-done((bf16[640,256]{1,0:T(8,128)(2,1)S(1)}, bf16[640,256]{1,0:T(8,128)(2,1)S(1)}, u32[]{:S(2)}, u32[]{:S(2)}) %collective-permute-start.3) | collective-permute-done | bytes 327712 | tf_op jit(solution)/shard_map/ppermute | solution.py:256
  66.3 3.8 %collective-permute-done.2.five1 = bf16[640,256]{1,0:T(8,128)(2,1)S(1)} collective-permute-done((bf16[640,256]{1,0:T(8,128)(2,1)S(1)}, bf16[640,256]{1,0:T(8,128)(2,1)S(1)}, u32[]{:S(2)}, u32[]{:S(2)}) %collective-permute-start.2) | collective-permute-done | bytes 327712 | tf_op jit(solution)/shard_map/ppermute | solution.py:256
  70.2 1.2 pad_maximum_fusion
  71.4 1.9 %collective-permute-start.5 = (bf16[4,640,256]{2,1,0:T(8,128)(2,1)}, bf16[4,640,256]{2,1,0:T(8,128)(2,1)}, u32[]{:S(2)}, u32[]{:S(2)}) collective-permute-start(bf16[4,640,256]{2,1,0:T(8,128)(2,1)} %pad_maximum_fusion), channel_id=1, source_target_pairs={{0,16},{16,0},{1,17},{17,1},{2,18},{18,2},{3,19},{19,3},{4,20},{20... | collective-permute-start | bytes 3932168 | tf_op jit(solution)/shard_map/ppermute | solution.py:258
  73.4 1.9 %collective-permute-start = (bf16[128,512]{1,0:T(8,128)(2,1)S(1)}, bf16[128,512]{1,0:T(8,128)(2,1)S(1)}, u32[]{:S(2)}, u32[]{:S(2)}) collective-permute-start(bf16[128,512]{1,0:T(8,128)(2,1)S(1)} %bitcast.135), channel_id=1, source_target_pairs={{128,0},{256,128},{384,256},{129,1},{257,129},{385,257},{130,2},{2... | collective-permute-start | bytes 393224 | tf_op jit(solution)/shard_map/ppermute | solution.py:260
  75.3 1.4 collective-permute-done.5.other_five
  80.6 2.5 %arrange.1 = (bf16[20,256,128]{2,1,0:T(8,128)(2,1)S(1)}, bf16[20,256,128]{2,1,0:T(8,128)(2,1)S(1)}, bf16[20,128,256]{2,1,0:T(8,128)(2,1)S(1)}, bf16[20,128,256]{2,1,0:T(8,128)(2,1)S(1)}) custom-call(s32[12]{0:T(128)S(1)} %pad_add_fusion.where_ref, bf16[640,256]{1,0:T(8,128)(2,1)S(1)} %copy-done.9, bf16[640,256]{1,0:T(8,128)(2,1)S(1)} %copy-done.7, ...), custom_call_target="tpu_custom_call" | custom-call | tf_op jit(solution)/shard_map/arrange/pallas_call | solution.py:167
  83.1 17.3 %attend.1 = (bf16[640,256]{1,0:T(8,128)(2,1)S(1)}, f32[4,640,256]{2,1,0:T(8,128)S(1)}, bf16[4,640,256]{2,1,0:T(8,128)(2,1)}) custom-call(s32[12]{0:T(128)S(1)} %pad_add_fusion.where_ref, s32[5,128]{1,0:T(8,128)S(1)} %get-tuple-element.15.query_code_ref, s32[5120,128]{1,0:T(8,128)S(1)} %broadcast_in_dim.98.key_code_ref, bf16[512,512]{1,0:T(8,128)(2,1)S(1)} %bitcast.124, ...), custom_call_target="tpu_custom_call" | custom-call | tf_op jit(solution)/shard_map/attend/pallas_call | solution.py:180
  100.3 1.5 copy-done.1
  101.8 1.9 %collective-permute-start.7 = (bf16[4,640,256]{2,1,0:T(8,128)(2,1)}, bf16[4,640,256]{2,1,0:T(8,128)(2,1)S(1)}, u32[]{:S(2)}, u32[]{:S(2)}) collective-permute-start(bf16[4,640,256]{2,1,0:T(8,128)(2,1)} %get-tuple-element.24), channel_id=1, source_target_pairs={{0,16},{16,0},{1,17},{17,1},{2,18},{18,2},{3,19},{19,3},{4,20},{20... | collective-permute-start | bytes 3932168 | tf_op jit(solution)/shard_map/ppermute | solution.py:263
  103.8 1.9 %collective-permute-start.6 = (bf16[128,256]{1,0:T(8,128)(2,1)S(1)}, bf16[128,256]{1,0:T(8,128)(2,1)S(1)}, u32[]{:S(2)}, u32[]{:S(2)}) collective-permute-start(bf16[128,256]{1,0:T(8,128)(2,1)S(1)} %slice.84), channel_id=1, source_target_pairs={{0,128},{128,256},{256,384},{1,129},{129,257},{257,385},{2,130},{1... | collective-permute-start | bytes 196616 | tf_op jit(solution)/shard_map/ppermute | solution.py:264
  105.7 4.2 %collective-permute-done.6 = bf16[128,256]{1,0:T(8,128)(2,1)S(1)} collective-permute-done((bf16[128,256]{1,0:T(8,128)(2,1)S(1)}, bf16[128,256]{1,0:T(8,128)(2,1)S(1)}, u32[]{:S(2)}, u32[]{:S(2)}) %collective-permute-start.6) | collective-permute-done | bytes 65568 | tf_op jit(solution)/shard_map/ppermute | solution.py:264
  110.7 12.3 %all-to-all-start.2 = ((bf16[16,32,256]{2,1,0:T(8,128)(2,1)}), bf16[16,32,256]{2,1,0:T(8,128)(2,1)S(1)}, u32[]{:S(2)}, u32[]{:S(2)}) async-start(bf16[16,32,256]{2,1,0:T(8,128)(2,1)} %bitcast.19), calls=%async_computation.2 | async-start | bytes 524288 | tf_op jit(solution)/shard_map/all_to_all | solution.py:269
  123.0 2.1 %fusion.24 = (bf16[4,640,256]{2,1,0:T(8,128)(2,1)S(1)}, f32[4,640,256]{2,1,0:T(8,128)S(1)}) fusion(f32[4,640,256]{2,1,0:T(8,128)} %copy-done.1, bf16[4,640,256]{2,1,0:T(8,128)(2,1)S(1)} %collective-permute-done.7), kind=kLoop, calls=%fused_computation.90 | loop fusion | flops 1966080 | bytes 7864320 | tf_op jit(solution)/shard_map/convert.3
  125.2 6.7 %collective-permute-start.8 = (bf16[640,256]{1,0:T(8,128)(2,1)S(1)}, bf16[640,256]{1,0:T(8,128)(2,1)S(1)}, u32[]{:S(2)}, u32[]{:S(2)}) collective-permute-start(bf16[640,256]{1,0:T(8,128)(2,1)S(1)} %get-tuple-element.34), channel_id=1, source_target_pairs={{0,4},{4,8},{8,12},{12,0},{1,5},{5,9},{9,13},{13,1},{2,6},{6,10},{... | collective-permute-start | bytes 983048 | tf_op jit(solution)/shard_map/ppermute | solution.py:275
  131.9 1.9 %collective-permute-start.10 = (bf16[640,256]{1,0:T(8,128)(2,1)S(1)}, bf16[640,256]{1,0:T(8,128)(2,1)S(1)}, u32[]{:S(2)}, u32[]{:S(2)}) collective-permute-start(bf16[640,256]{1,0:T(8,128)(2,1)S(1)} %get-tuple-element.35), channel_id=1, source_target_pairs={{0,12},{4,0},{8,4},{12,8},{1,13},{5,1},{9,5},{13,9},{2,14},{6,2},{... | collective-permute-start | bytes 983048 | tf_op jit(solution)/shard_map/ppermute | solution.py:275
  133.8 3.4 %collective-permute-start.9 = (bf16[640,256]{1,0:T(8,128)(2,1)S(1)}, bf16[640,256]{1,0:T(8,128)(2,1)S(1)}, u32[]{:S(2)}, u32[]{:S(2)}) collective-permute-start(bf16[640,256]{1,0:T(8,128)(2,1)S(1)} %get-tuple-element.36), channel_id=1, source_target_pairs={{0,8},{4,12},{8,0},{12,4},{1,9},{5,13},{9,1},{13,5},{2,10},{6,14},... | collective-permute-start | bytes 983048 | tf_op jit(solution)/shard_map/ppermute | solution.py:275
  137.2 2.8 %collective-permute-done.8 = bf16[640,256]{1,0:T(8,128)(2,1)S(1)} collective-permute-done((bf16[640,256]{1,0:T(8,128)(2,1)S(1)}, bf16[640,256]{1,0:T(8,128)(2,1)S(1)}, u32[]{:S(2)}, u32[]{:S(2)}) %collective-permute-start.8) | collective-permute-done | bytes 327712 | tf_op jit(solution)/shard_map/ppermute | solution.py:275
  140.0 4.9 %collective-permute-done.10 = bf16[640,256]{1,0:T(8,128)(2,1)S(1)} collective-permute-done((bf16[640,256]{1,0:T(8,128)(2,1)S(1)}, bf16[640,256]{1,0:T(8,128)(2,1)S(1)}, u32[]{:S(2)}, u32[]{:S(2)}) %collective-permute-start.10) | collective-permute-done | bytes 327712 | tf_op jit(solution)/shard_map/ppermute | solution.py:275
  145.0 1.9 %collective-permute-start.11 = (bf16[128,256]{1,0:T(8,128)(2,1)S(1)}, bf16[128,256]{1,0:T(8,128)(2,1)S(1)}, u32[]{:S(2)}, u32[]{:S(2)}) collective-permute-start(bf16[128,256]{1,0:T(8,128)(2,1)S(1)} %slice.135), channel_id=1, source_target_pairs={{0,128},{128,256},{256,384},{144,16},{272,144},{400,272},{1,129},{... | collective-permute-start | bytes 196616 | tf_op jit(solution)/shard_map/ppermute | solution.py:276
  146.9 4.2 %collective-permute-done.11 = bf16[128,256]{1,0:T(8,128)(2,1)S(1)} collective-permute-done((bf16[128,256]{1,0:T(8,128)(2,1)S(1)}, bf16[128,256]{1,0:T(8,128)(2,1)S(1)}, u32[]{:S(2)}, u32[]{:S(2)}) %collective-permute-start.11) | collective-permute-done | bytes 65568 | tf_op jit(solution)/shard_map/ppermute | solution.py:276
  151.9 12.0 %all-to-all-start.3 = ((bf16[16,32,256]{2,1,0:T(8,128)(2,1)}), bf16[16,32,256]{2,1,0:T(8,128)(2,1)S(1)}, u32[]{:S(2)}, u32[]{:S(2)}) async-start(bf16[16,32,256]{2,1,0:T(8,128)(2,1)} %bitcast.25), calls=%async_computation.3 | async-start | bytes 524288 | tf_op jit(solution)/shard_map/all_to_all | solution.py:282
  164.7 13.9 %all-to-all-done.3 = bf16[16,32,256]{2,1,0:T(8,128)(2,1)S(1)} async-done(((bf16[16,32,256]{2,1,0:T(8,128)(2,1)}), bf16[16,32,256]{2,1,0:T(8,128)(2,1)S(1)}, u32[]{:S(2)}, u32[]{:S(2)}) %all-to-all-start.3) | async-done | bytes 262176 | tf_op jit(solution)/shard_map/all_to_all | solution.py:282
  (73 shorter events, 15.1 us)
Async XLA Ops:
  0.6 0.9 copy-start
  0.6 17.8 %copy-start.12 = (s32[8,4]{0,1:T(4,128)S(1)}, s32[8,4]{0,1:T(4,128)}, u32[]{:S(2)}) copy-start(s32[8,4]{0,1:T(4,128)} %param.9) | copy-start | bytes 388
  0.7 20.3 %copy-start.10 = (bf16[32,4096]{1,0:T(8,128)(2,1)S(1)}, bf16[32,4096]{1,0:T(8,128)(2,1)}, u32[]{:S(2)}) copy-start(bf16[32,4096]{1,0:T(8,128)(2,1)} %param.8) | copy-start | bytes 786436
  1.5 19.4 %copy-start.11 = (bf16[32,4096]{1,0:T(8,128)(2,1)S(1)}, bf16[32,4096]{1,0:T(8,128)(2,1)}, u32[]{:S(2)}) copy-start(bf16[32,4096]{1,0:T(8,128)(2,1)} %param.5) | copy-start | bytes 786436
  3.3 33.1 %all-to-all-start.1 = ((bf16[16,32,256]{2,1,0:T(8,128)(2,1)}), bf16[16,32,256]{2,1,0:T(8,128)(2,1)S(1)}, u32[]{:S(2)}, u32[]{:S(2)}) async-start(bf16[16,32,256]{2,1,0:T(8,128)(2,1)} %pad_maximum_fusion.3), calls=%async_computation.1 | async-start | bytes 524288 | tf_op jit(solution)/shard_map/all_to_all | solution.py:246
  36.4 36.9 %all-to-all-start = ((bf16[16,32,512]{2,1,0:T(8,128)(2,1)}), bf16[16,32,512]{2,1,0:T(8,128)(2,1)S(1)}, u32[]{:S(2)}, u32[]{:S(2)}) async-start(bf16[16,32,512]{2,1,0:T(8,128)(2,1)} %pad_maximum_fusion.1), calls=%async_computation | async-start | bytes 1048576 | tf_op jit(solution)/shard_map/all_to_all | solution.py:250
  42.7 6.2 %collective-permute-start.1 = (bf16[128,256]{1,0:T(8,128)(2,1)S(1)}, bf16[128,256]{1,0:T(8,128)(2,1)S(1)}, u32[]{:S(2)}, u32[]{:S(2)}) collective-permute-start(bf16[128,256]{1,0:T(8,128)(2,1)S(1)} %constant_dynamic-slice_fusion), channel_id=1, source_target_pairs={{128,0},{256,128},{384,256},{16,144},{144,272},{272,400},{129,1},{... | collective-permute-start | bytes 196616 | tf_op jit(solution)/shard_map/ppermute | solution.py:254
  48.9 12.1 %collective-permute-start.4 = (bf16[640,256]{1,0:T(8,128)(2,1)S(1)}, bf16[640,256]{1,0:T(8,128)(2,1)S(1)}, u32[]{:S(2)}, u32[]{:S(2)}) collective-permute-start(bf16[640,256]{1,0:T(8,128)(2,1)S(1)} %get-tuple-element.38.five0), channel_id=1, source_target_pairs={{0,4},{4,8},{8,12},{12,0},{1,5},{5,9},{9,13},{13,1},{2,6},{6,10},{... | collective-permute-start | bytes 983048 | tf_op jit(solution)/shard_map/ppermute | solution.py:256
  52.4 14.0 %collective-permute-start.3 = (bf16[640,256]{1,0:T(8,128)(2,1)S(1)}, bf16[640,256]{1,0:T(8,128)(2,1)S(1)}, u32[]{:S(2)}, u32[]{:S(2)}) collective-permute-start(bf16[640,256]{1,0:T(8,128)(2,1)S(1)} %get-tuple-element.38.five0), channel_id=1, source_target_pairs={{0,8},{4,12},{8,0},{12,4},{1,9},{5,13},{9,1},{13,5},{2,10},{6,14},... | collective-permute-start | bytes 983048 | tf_op jit(solution)/shard_map/ppermute | solution.py:256
  55.2 15.0 %collective-permute-start.2 = (bf16[640,256]{1,0:T(8,128)(2,1)S(1)}, bf16[640,256]{1,0:T(8,128)(2,1)S(1)}, u32[]{:S(2)}, u32[]{:S(2)}) collective-permute-start(bf16[640,256]{1,0:T(8,128)(2,1)S(1)} %get-tuple-element.38.five0), channel_id=1, source_target_pairs={{0,12},{4,0},{8,4},{12,8},{1,13},{5,1},{9,5},{13,9},{2,14},{6,2},{... | collective-permute-start | bytes 983048 | tf_op jit(solution)/shard_map/ppermute | solution.py:256
  59.5 0.7 copy-start.8
  60.9 10.5 %copy-start.2 = (bf16[640,256]{1,0:T(8,128)(2,1)}, bf16[640,256]{1,0:T(8,128)(2,1)S(1)}, u32[]{:S(2)}) copy-start(bf16[640,256]{1,0:T(8,128)(2,1)S(1)} %collective-permute-done.4.five3) | copy-start | bytes 983044
  66.3 5.1 %copy-start.4 = (bf16[640,256]{1,0:T(8,128)(2,1)}, bf16[640,256]{1,0:T(8,128)(2,1)S(1)}, u32[]{:S(2)}) copy-start(bf16[640,256]{1,0:T(8,128)(2,1)S(1)} %collective-permute-done.3.five2) | copy-start | bytes 983044
  70.2 1.2 copy-start.6
  71.4 5.3 %collective-permute-start.5 = (bf16[4,640,256]{2,1,0:T(8,128)(2,1)}, bf16[4,640,256]{2,1,0:T(8,128)(2,1)}, u32[]{:S(2)}, u32[]{:S(2)}) collective-permute-start(bf16[4,640,256]{2,1,0:T(8,128)(2,1)} %pad_maximum_fusion), channel_id=1, source_target_pairs={{0,16},{16,0},{1,17},{17,1},{2,18},{18,2},{3,19},{19,3},{4,20},{20... | collective-permute-start | bytes 3932168 | tf_op jit(solution)/shard_map/ppermute | solution.py:258
  73.4 9.7 %collective-permute-start = (bf16[128,512]{1,0:T(8,128)(2,1)S(1)}, bf16[128,512]{1,0:T(8,128)(2,1)S(1)}, u32[]{:S(2)}, u32[]{:S(2)}) collective-permute-start(bf16[128,512]{1,0:T(8,128)(2,1)S(1)} %bitcast.135), channel_id=1, source_target_pairs={{128,0},{256,128},{384,256},{129,1},{257,129},{385,257},{130,2},{2... | collective-permute-start | bytes 393224 | tf_op jit(solution)/shard_map/ppermute | solution.py:260
  76.7 1.0 copy-start.3
  77.7 1.0 copy-start.5
  78.6 1.0 copy-start.7
  79.6 1.0 copy-start.9
  100.3 1.5 copy-start.1
  101.8 21.2 %collective-permute-start.7 = (bf16[4,640,256]{2,1,0:T(8,128)(2,1)}, bf16[4,640,256]{2,1,0:T(8,128)(2,1)S(1)}, u32[]{:S(2)}, u32[]{:S(2)}) collective-permute-start(bf16[4,640,256]{2,1,0:T(8,128)(2,1)} %get-tuple-element.24), channel_id=1, source_target_pairs={{0,16},{16,0},{1,17},{17,1},{2,18},{18,2},{3,19},{19,3},{4,20},{20... | collective-permute-start | bytes 3932168 | tf_op jit(solution)/shard_map/ppermute | solution.py:263
  103.8 6.2 %collective-permute-start.6 = (bf16[128,256]{1,0:T(8,128)(2,1)S(1)}, bf16[128,256]{1,0:T(8,128)(2,1)S(1)}, u32[]{:S(2)}, u32[]{:S(2)}) collective-permute-start(bf16[128,256]{1,0:T(8,128)(2,1)S(1)} %slice.84), channel_id=1, source_target_pairs={{0,128},{128,256},{256,384},{1,129},{129,257},{257,385},{2,130},{1... | collective-permute-start | bytes 196616 | tf_op jit(solution)/shard_map/ppermute | solution.py:264
  110.7 41.3 %all-to-all-start.2 = ((bf16[16,32,256]{2,1,0:T(8,128)(2,1)}), bf16[16,32,256]{2,1,0:T(8,128)(2,1)S(1)}, u32[]{:S(2)}, u32[]{:S(2)}) async-start(bf16[16,32,256]{2,1,0:T(8,128)(2,1)} %bitcast.19), calls=%async_computation.2 | async-start | bytes 524288 | tf_op jit(solution)/shard_map/all_to_all | solution.py:269
  125.2 14.7 %collective-permute-start.8 = (bf16[640,256]{1,0:T(8,128)(2,1)S(1)}, bf16[640,256]{1,0:T(8,128)(2,1)S(1)}, u32[]{:S(2)}, u32[]{:S(2)}) collective-permute-start(bf16[640,256]{1,0:T(8,128)(2,1)S(1)} %get-tuple-element.34), channel_id=1, source_target_pairs={{0,4},{4,8},{8,12},{12,0},{1,5},{5,9},{9,13},{13,1},{2,6},{6,10},{... | collective-permute-start | bytes 983048 | tf_op jit(solution)/shard_map/ppermute | solution.py:275
  131.9 13.0 %collective-permute-start.10 = (bf16[640,256]{1,0:T(8,128)(2,1)S(1)}, bf16[640,256]{1,0:T(8,128)(2,1)S(1)}, u32[]{:S(2)}, u32[]{:S(2)}) collective-permute-start(bf16[640,256]{1,0:T(8,128)(2,1)S(1)} %get-tuple-element.35), channel_id=1, source_target_pairs={{0,12},{4,0},{8,4},{12,8},{1,13},{5,1},{9,5},{13,9},{2,14},{6,2},{... | collective-permute-start | bytes 983048 | tf_op jit(solution)/shard_map/ppermute | solution.py:275
  133.8 11.0 %collective-permute-start.9 = (bf16[640,256]{1,0:T(8,128)(2,1)S(1)}, bf16[640,256]{1,0:T(8,128)(2,1)S(1)}, u32[]{:S(2)}, u32[]{:S(2)}) collective-permute-start(bf16[640,256]{1,0:T(8,128)(2,1)S(1)} %get-tuple-element.36), channel_id=1, source_target_pairs={{0,8},{4,12},{8,0},{12,4},{1,9},{5,13},{9,1},{13,5},{2,10},{6,14},... | collective-permute-start | bytes 983048 | tf_op jit(solution)/shard_map/ppermute | solution.py:275
  145.0 6.2 %collective-permute-start.11 = (bf16[128,256]{1,0:T(8,128)(2,1)S(1)}, bf16[128,256]{1,0:T(8,128)(2,1)S(1)}, u32[]{:S(2)}, u32[]{:S(2)}) collective-permute-start(bf16[128,256]{1,0:T(8,128)(2,1)S(1)} %slice.135), channel_id=1, source_target_pairs={{0,128},{128,256},{256,384},{144,16},{272,144},{400,272},{1,129},{... | collective-permute-start | bytes 196616 | tf_op jit(solution)/shard_map/ppermute | solution.py:276
  151.9 26.7 %all-to-all-start.3 = ((bf16[16,32,256]{2,1,0:T(8,128)(2,1)}), bf16[16,32,256]{2,1,0:T(8,128)(2,1)S(1)}, u32[]{:S(2)}, u32[]{:S(2)}) async-start(bf16[16,32,256]{2,1,0:T(8,128)(2,1)} %bitcast.25), calls=%async_computation.3 | async-start | bytes 524288 | tf_op jit(solution)/shard_map/all_to_all | solution.py:282

commit v4 on v3

--- a/solution.py
+++ b/solution.py
@@ -52,7 +52,7 @@
 
 
 def arrange(
-    where_ref, five0, five1, five2, five3, other_five, keys, values, keys_t, values_t
+    where_ref, my_five, other_five, keys, values, keys_t, values_t
 ):
     y = where_ref[2 * RUNS]
     core = where_ref[2 * RUNS + 1]
@@ -63,11 +63,11 @@
         keys[block, pl.ds(at, RUN), :] = piece[:, :HEAD_DIM]
         values[block, pl.ds(at, RUN), :] = piece[:, HEAD_DIM:]
 
-    for dy, five in enumerate((five0, five1, five2, five3)):
+    for dy in range(Y):
         row = (y + dy) % Y
         for run in range(RUNS):
             rows = slice(run * RUN, (run + 1) * RUN)
-            place(slot_of(run, core), row, five[rows, :])
+            place(slot_of(run, core), row, my_five[dy, rows, :])
             place(slot_of(run, 1 - core), row, other_five[dy, rows, :])
 
     for block in range(BLOCKS):
@@ -75,79 +75,94 @@
         values_t[block] = values[block].T
 
 
+def one_run(run, source, rows, refs, dq_ref, out, ratios, expos, sums):
+    where_ref, query_code_ref, key_code_ref, keys, values, keys_t, values_t = refs
+    f32, b16 = jnp.float32, jnp.bfloat16
+    low = where_ref[run]
+    high = where_ref[RUNS + run]
+    query = jnp.concatenate([source[rows, 0:128], source[rows, 128:256]], axis=0)
+    grad = jnp.concatenate([source[rows, 256:384], source[rows, 384:512]], axis=0)
+    query_t = query.T
+    grad_t = grad.T
+    query_code = query_code_ref[run : run + 1, :]
+
+    def forward(block, carry):
+        total, weighted = carry
+        raw = jnp.dot(keys[block], query_t, preferred_element_type=f32)
+        ratio = jnp.tanh(raw * (SCORE_SCALE / SOFT_CAP))
+        expo = jnp.exp2(ratio * (SOFT_CAP * LOG2_E))
+        gap = query_code - key_code_ref[pl.ds(pl.multiple_of(block * KB, KB), KB), :]
+        seen = (gap >= 0) & (gap < 8 * WINDOW) & ((gap & 7) != 1)
+        expo = jnp.concatenate(
+            [jnp.where(seen, expo[:, :RUN], 0.0), jnp.where(seen, expo[:, RUN:], 0.0)], axis=1
+        )
+        ratios[block - low] = ratio
+        expos[block - low] = expo
+        total = total + jnp.sum(expo, axis=0, keepdims=True)
+        weighted = weighted + jnp.dot(
+            values_t[block], expo.astype(b16), preferred_element_type=f32
+        )
+        return total, weighted
+
+    total, weighted = by_two(
+        low, high + 1, forward,
+        (jnp.zeros((1, 2 * RUN), f32), jnp.zeros((HEAD_DIM, 2 * RUN), f32)),
+    )
+    scale = jnp.where(total > 0.0, 1.0 / total, 0.0)
+    delta = jnp.sum(grad_t.astype(f32) * weighted, axis=0, keepdims=True) * scale
+
+    def backward(block, dq_t):
+        ratio = ratios[block - low]
+        prob = expos[block - low] * scale
+        dprob = jnp.dot(values[block], grad_t, preferred_element_type=f32)
+        dscore = prob * (dprob - delta) * ((1.0 - ratio * ratio) * SCORE_SCALE)
+        dscore = dscore.astype(b16)
+        dq_t = dq_t + jnp.dot(keys_t[block], dscore, preferred_element_type=f32)
+        dk = jnp.dot(dscore, query, preferred_element_type=f32)
+        dv = jnp.dot(prob.astype(b16), grad, preferred_element_type=f32)
+        sums[block] = sums[block] + jnp.concatenate([dk, dv], axis=1)
+        return dq_t
+
+    dq_t = by_two(low, high + 1, backward, jnp.zeros((HEAD_DIM, 2 * RUN), f32))
+    dq_ref[out, 0:128] = dq_t[:, :RUN].T.astype(b16)
+    dq_ref[out, 128:256] = dq_t[:, RUN:].T.astype(b16)
+
+
+def attend_tail(
+    where_ref, query_code_ref, key_code_ref, keys, values, keys_t, values_t, tail_ref,
+    dq_ref, sums,
+    ratios, expos,
+):
+    refs = (where_ref, query_code_ref, key_code_ref, keys, values, keys_t, values_t)
+    whole = slice(0, RUN)
+    for block in range(BLOCKS):
+        sums[block] = jnp.zeros((KB, 2 * HEAD_DIM), jnp.float32)
+    core = where_ref[2 * RUNS + 1]
+
+    @pl.when(core == 0)
+    def _():
+        one_run(ZH, tail_ref, whole, refs, dq_ref, whole, ratios, expos, sums)
+
+    @pl.when(core != 0)
+    def _():
+        dq_ref[...] = jnp.zeros((RUN, 256), jnp.bfloat16)
+
+
 def attend(
-    where_ref, query_code_ref, key_code_ref, qg_ref, tail_ref, keys, values, keys_t, values_t,
+    where_ref, query_code_ref, key_code_ref, keys, values, keys_t, values_t, qg_ref, tail_sums,
     dq_ref, mine_ref, other_ref,
     ratios, expos, sums,
 ):
     y = where_ref[2 * RUNS]
     core = where_ref[2 * RUNS + 1]
-    f32, b16 = jnp.float32, jnp.bfloat16
-
+    b16 = jnp.bfloat16
+    refs = (where_ref, query_code_ref, key_code_ref, keys, values, keys_t, values_t)
     for block in range(BLOCKS):
-        sums[block] = jnp.zeros((KB, 2 * HEAD_DIM), f32)
-
-    def one_run(run, source, rows):
-        low = where_ref[run]
-        high = where_ref[RUNS + run]
-        query = jnp.concatenate([source[rows, 0:128], source[rows, 128:256]], axis=0)
-        grad = jnp.concatenate([source[rows, 256:384], source[rows, 384:512]], axis=0)
-        query_t = query.T
-        grad_t = grad.T
-        query_code = query_code_ref[run : run + 1, :]
-
-        def forward(block, carry):
-            total, weighted = carry
-            raw = jnp.dot(keys[block], query_t, preferred_element_type=f32)
-            ratio = jnp.tanh(raw * (SCORE_SCALE / SOFT_CAP))
-            expo = jnp.exp2(ratio * (SOFT_CAP * LOG2_E))
-            gap = query_code - key_code_ref[pl.ds(pl.multiple_of(block * KB, KB), KB), :]
-            seen = (gap >= 0) & (gap < 8 * WINDOW) & ((gap & 7) != 1)
-            expo = jnp.concatenate(
-                [jnp.where(seen, expo[:, :RUN], 0.0), jnp.where(seen, expo[:, RUN:], 0.0)], axis=1
-            )
-            ratios[block - low] = ratio
-            expos[block - low] = expo
-            total = total + jnp.sum(expo, axis=0, keepdims=True)
-            weighted = weighted + jnp.dot(
-                values_t[block], expo.astype(b16), preferred_element_type=f32
-            )
-            return total, weighted
-
-        total, weighted = by_two(
-            low, high + 1, forward,
-            (jnp.zeros((1, 2 * RUN), f32), jnp.zeros((HEAD_DIM, 2 * RUN), f32)),
-        )
-        scale = jnp.where(total > 0.0, 1.0 / total, 0.0)
-        delta = jnp.sum(grad_t.astype(f32) * weighted, axis=0, keepdims=True) * scale
-
-        def backward(block, dq_t):
-            ratio = ratios[block - low]
-            prob = expos[block - low] * scale
-            dprob = jnp.dot(values[block], grad_t, preferred_element_type=f32)
-            dscore = prob * (dprob - delta) * ((1.0 - ratio * ratio) * SCORE_SCALE)
-            dscore = dscore.astype(b16)
-            dq_t = dq_t + jnp.dot(keys_t[block], dscore, preferred_element_type=f32)
-            dk = jnp.dot(dscore, query, preferred_element_type=f32)
-            dv = jnp.dot(prob.astype(b16), grad, preferred_element_type=f32)
-            sums[block] = sums[block] + jnp.concatenate([dk, dv], axis=1)
-            return dq_t
-
-        dq_t = by_two(low, high + 1, backward, jnp.zeros((HEAD_DIM, 2 * RUN), f32))
-        out = slice(run * RUN, (run + 1) * RUN)
-        dq_ref[out, 0:128] = dq_t[:, :RUN].T.astype(b16)
-        dq_ref[out, 128:256] = dq_t[:, RUN:].T.astype(b16)
+        sums[block] = tail_sums[block]
 
     for run in range(ZH):
-        one_run(run, qg_ref, slice(run * RUN, (run + 1) * RUN))
-
-    @pl.when(core == 0)
-    def _():
-        one_run(ZH, tail_ref, slice(0, RUN))
-
-    @pl.when(core != 0)
-    def _():
-        dq_ref[ZH * RUN :, :] = jnp.zeros((RUN, 256), b16)
+        rows = slice(run * RUN, (run + 1) * RUN)
+        one_run(run, qg_ref, rows, refs, dq_ref, rows, ratios, expos, sums)
 
     for dy in range(Y):
         row = (y + dy) % Y
@@ -167,20 +182,39 @@
     return pl.pallas_call(
         arrange,
         out_shape=(straight, straight, turned, turned),
-        in_specs=[pl.BlockSpec(memory_space=pltpu.SMEM)] + [vmem] * 5,
+        in_specs=[pl.BlockSpec(memory_space=pltpu.SMEM)] + [vmem] * 2,
         out_specs=(vmem,) * 4,
         compiler_params=pltpu.CompilerParams(vmem_limit_bytes=12 << 20),
         name="arrange",
     )(where, *pieces)
 
 
-def call_attend(where, query_code, key_code, qg, tail, arranged):
+def call_tail(where, query_code, key_code, arranged, tail):
+    vmem = pl.BlockSpec(memory_space=pltpu.VMEM)
+    return pl.pallas_call(
+        attend_tail,
+        out_shape=(
+            jax.ShapeDtypeStruct((RUN, 256), jnp.bfloat16),
+            jax.ShapeDtypeStruct((BLOCKS, KB, 2 * HEAD_DIM), jnp.float32),
+        ),
+        in_specs=[pl.BlockSpec(memory_space=pltpu.SMEM)] + [vmem] * 7,
+        out_specs=(vmem, vmem),
+        scratch_shapes=[
+            pltpu.VMEM((MOST, KB, 2 * RUN), jnp.float32),
+            pltpu.VMEM((MOST, KB, 2 * RUN), jnp.float32),
+        ],
+        compiler_params=pltpu.CompilerParams(vmem_limit_bytes=24 << 20),
+        name="attend_tail",
+    )(where, query_code, key_code, *arranged, tail)
+
+
+def call_attend(where, query_code, key_code, arranged, qg, tail_sums):
     vmem = pl.BlockSpec(memory_space=pltpu.VMEM)
     rows = RUNS * RUN
     return pl.pallas_call(
         attend,
         out_shape=(
-            jax.ShapeDtypeStruct((rows, 256), jnp.bfloat16),
+            jax.ShapeDtypeStruct((ZH * RUN, 256), jnp.bfloat16),
             jax.ShapeDtypeStruct((Y, rows, 256), jnp.float32),
             jax.ShapeDtypeStruct((Y, rows, 256), jnp.bfloat16),
         ),
@@ -191,9 +225,9 @@
             pltpu.VMEM((MOST, KB, 2 * RUN), jnp.float32),
             pltpu.VMEM((BLOCKS, KB, 2 * HEAD_DIM), jnp.float32),
         ],
-        compiler_params=pltpu.CompilerParams(vmem_limit_bytes=32 << 20),
+        compiler_params=pltpu.CompilerParams(vmem_limit_bytes=36 << 20),
         name="attend",
-    )(where, query_code, key_code, qg, tail, *arranged)
+    )(where, query_code, key_code, *arranged, qg, tail_sums)
 
 
 def tables(x, core, y, pack_table):
@@ -256,14 +290,15 @@
     fives = [five] + [lax.ppermute(five, "y", ring(Y, -dy)) for dy in range(1, Y)]
     stack = jnp.stack(fives)
     other_five = lax.ppermute(stack, "core", ring(CORE, 1))
-    arranged = call_arrange(where, (*fives, other_five))
+    arranged = call_arrange(where, (stack, other_five))
     tail = lax.ppermute(qg[:RUN], ("x", "core"), tails)
-    dq, mine, other = call_attend(where, query_code, key_code, qg, tail, arranged)
+    dq_tail, tail_sums = call_tail(where, query_code, key_code, arranged, tail)
+    dq_tail = lax.ppermute(dq_tail, ("x", "core"), [(b, a) for a, b in tails])
+    dq, mine, other = call_attend(where, query_code, key_code, arranged, qg, tail_sums)
 
     other = lax.ppermute(other, "core", ring(CORE, 1))
-    dq_tail = lax.ppermute(dq[ZH * RUN :], ("x", "core"), [(b, a) for a, b in tails])
     dq = jnp.concatenate(
-        [(dq[:RUN].astype(f32) + dq_tail.astype(f32)).astype(b16), dq[RUN : ZH * RUN]], axis=0
+        [(dq[:RUN].astype(f32) + dq_tail.astype(f32)).astype(b16), dq[RUN:]], axis=0
     )
     dq = dq.reshape(HEADS, tokens, 256)
     dq = lax.all_to_all(dq, z, split_axis=0, concat_axis=0, tiled=True)

time: 181 us -> 177 us (0.978)
  local copies, waits for them, and re-layouts: 11.7 us -> 7.09 us
    unnamed x27 -> x11, local copies, waits for them, and re-layouts: 7.07 us -> 2.46 us
    pallas_call x1 -> x2, Pallas kernels: 17.3 us -> 18 us  [the longest x1 12.2 us: call_attend(): pl.pallas_call(attend, out_shape=(jax.ShapeDtypeStruct((ZH * RUN, 256), j...]
  transfers between devices with their start and end apart: 16 -> 16, of which waited for: 11 -> 13; matrix products, arithmetic and copies ran while one was open for 6% -> 6% of each run, Pallas kernels for 1% -> 2%
where the time goes in v4:
time: 177 us; the launch traced here: 176 us
  starting transfers between devices  80.4 us (45%)
  waiting for transfers between devices  57.8 us (33%)
  Pallas kernels  20.9 us (12%)
  other arithmetic  8.52 us (5%)
  local copies, waits for them, and re-layouts  7.09 us (4%)
    all_to_all x1, starting transfers between devices, local(): kv = lax.all_to_all(kv, z, split_axis=0, concat_axis=0, tiled=True)  15.2 us
    all_to_all x1, waiting for transfers between devices, local(): dkv = lax.all_to_all(dkv, z, split_axis=0, concat_axis=0, tiled=True)  13.9 us
    all_to_all x1, waiting for transfers between devices, local(): kv = lax.all_to_all(kv, z, split_axis=0, concat_axis=0, tiled=True)  13.6 us
    ppermute x3, starting transfers between devices, local(): lax.ppermute(part[dy].astype(b16), 'y', ring(Y, dy)).astype(f32)  12.8 us
    pallas_call x1, Pallas kernels, call_attend(): pl.pallas_call(attend, out_shape=(jax.ShapeDtypeStruct((ZH * RUN, 256), j...  12.2 us
    all_to_all x1, starting transfers between devices, local(): dkv = lax.all_to_all(dkv, z, split_axis=0, concat_axis=0, tiled=True)  12 us
    all_to_all x1, starting transfers between devices, local(): dq = lax.all_to_all(dq, z, split_axis=0, concat_axis=0, tiled=True)  11.6 us
    ppermute x3, starting transfers between devices, local(): lax.ppermute(five, 'y', ring(Y, -dy))  10 us
  transfers between devices with their start and end apart: 16, of which 13 were waited for; matrix products, arithmetic and copies ran while one was open for 6% of the time, Pallas kernels for 2%

profile of v4, /device:TPU:42, one launch (start us, length us, event | category | flops | bytes accessed | tf_op | source)
XLA Modules:
  0.0 175.7 jit_solution(14864261742278446816)
XLA Ops:
  3.3 15.2 %all-to-all-start = ((bf16[16,32,256]{2,1,0:T(8,128)(2,1)}), bf16[16,32,256]{2,1,0:T(8,128)(2,1)S(1)}, u32[]{:S(2)}, u32[]{:S(2)}) async-start(bf16[16,32,256]{2,1,0:T(8,128)(2,1)} %pad_maximum_fusion.3), calls=%async_computation | async-start | bytes 524288 | tf_op jit(solution)/shard_map/all_to_all | solution.py:280
  22.8 13.6 %all-to-all-done = bf16[16,32,256]{2,1,0:T(8,128)(2,1)S(1)} async-done(((bf16[16,32,256]{2,1,0:T(8,128)(2,1)}), bf16[16,32,256]{2,1,0:T(8,128)(2,1)S(1)}, u32[]{:S(2)}, u32[]{:S(2)}) %all-to-all-start) | async-done | bytes 262176 | tf_op jit(solution)/shard_map/all_to_all | solution.py:280
  36.4 6.2 %all-to-all-start.1 = ((bf16[16,32,512]{2,1,0:T(8,128)(2,1)}), bf16[16,32,512]{2,1,0:T(8,128)(2,1)S(1)}, u32[]{:S(2)}, u32[]{:S(2)}) async-start(bf16[16,32,512]{2,1,0:T(8,128)(2,1)} %pad_maximum_fusion.1), calls=%async_computation.1 | async-start | bytes 1048576 | tf_op jit(solution)/shard_map/all_to_all | solution.py:284
  42.7 2.4 %collective-permute-start = (bf16[128,256]{1,0:T(8,128)(2,1)S(1)}, bf16[128,256]{1,0:T(8,128)(2,1)S(1)}, u32[]{:S(2)}, u32[]{:S(2)}) collective-permute-start(bf16[128,256]{1,0:T(8,128)(2,1)S(1)} %constant_dynamic-slice_fusion), channel_id=1, source_target_pairs={{128,0},{256,128},{384,256},{16,144},{144,272},{272,400},{129,1},{... | collective-permute-start | bytes 196616 | tf_op jit(solution)/shard_map/ppermute | solution.py:288
  45.1 3.7 %collective-permute-done = bf16[128,256]{1,0:T(8,128)(2,1)S(1)} collective-permute-done((bf16[128,256]{1,0:T(8,128)(2,1)S(1)}, bf16[128,256]{1,0:T(8,128)(2,1)S(1)}, u32[]{:S(2)}, u32[]{:S(2)}) %collective-permute-start) | collective-permute-done | bytes 65568 | tf_op jit(solution)/shard_map/ppermute | solution.py:288
  48.9 4.2 %collective-permute-start.2 = (bf16[640,256]{1,0:T(8,128)(2,1)S(1)}, bf16[640,256]{1,0:T(8,128)(2,1)S(1)}, u32[]{:S(2)}, u32[]{:S(2)}) collective-permute-start(bf16[640,256]{1,0:T(8,128)(2,1)S(1)} %get-tuple-element.42), channel_id=1, source_target_pairs={{0,8},{4,12},{8,0},{12,4},{1,9},{5,13},{9,1},{13,5},{2,10},{6,14},... | collective-permute-start | bytes 983048 | tf_op jit(solution)/shard_map/ppermute | solution.py:290
  53.1 3.3 %collective-permute-start.1 = (bf16[640,256]{1,0:T(8,128)(2,1)S(1)}, bf16[640,256]{1,0:T(8,128)(2,1)S(1)}, u32[]{:S(2)}, u32[]{:S(2)}) collective-permute-start(bf16[640,256]{1,0:T(8,128)(2,1)S(1)} %get-tuple-element.42), channel_id=1, source_target_pairs={{0,12},{4,0},{8,4},{12,8},{1,13},{5,1},{9,5},{13,9},{2,14},{6,2},{... | collective-permute-start | bytes 983048 | tf_op jit(solution)/shard_map/ppermute | solution.py:290
  56.3 2.6 %collective-permute-start.3 = (bf16[640,256]{1,0:T(8,128)(2,1)S(1)}, bf16[640,256]{1,0:T(8,128)(2,1)S(1)}, u32[]{:S(2)}, u32[]{:S(2)}) collective-permute-start(bf16[640,256]{1,0:T(8,128)(2,1)S(1)} %get-tuple-element.42), channel_id=1, source_target_pairs={{0,4},{4,8},{8,12},{12,0},{1,5},{5,9},{9,13},{13,1},{2,6},{6,10},{... | collective-permute-start | bytes 983048 | tf_op jit(solution)/shard_map/ppermute | solution.py:290
  58.9 3.9 %collective-permute-done.2 = bf16[640,256]{1,0:T(8,128)(2,1)S(1)} collective-permute-done((bf16[640,256]{1,0:T(8,128)(2,1)S(1)}, bf16[640,256]{1,0:T(8,128)(2,1)S(1)}, u32[]{:S(2)}, u32[]{:S(2)}) %collective-permute-start.2) | collective-permute-done | bytes 327712 | tf_op jit(solution)/shard_map/ppermute | solution.py:290
  62.9 4.1 %collective-permute-done.1 = bf16[640,256]{1,0:T(8,128)(2,1)S(1)} collective-permute-done((bf16[640,256]{1,0:T(8,128)(2,1)S(1)}, bf16[640,256]{1,0:T(8,128)(2,1)S(1)}, u32[]{:S(2)}, u32[]{:S(2)}) %collective-permute-start.1) | collective-permute-done | bytes 327712 | tf_op jit(solution)/shard_map/ppermute | solution.py:290
  67.1 1.3 pad_maximum_fusion.my_five
  68.3 1.9 %collective-permute-start.4 = (bf16[4,640,256]{2,1,0:T(8,128)(2,1)}, bf16[4,640,256]{2,1,0:T(8,128)(2,1)}, u32[]{:S(2)}, u32[]{:S(2)}) collective-permute-start(bf16[4,640,256]{2,1,0:T(8,128)(2,1)} %pad_maximum_fusion.my_five), channel_id=1, source_target_pairs={{0,16},{16,0},{1,17},{17,1},{2,18},{18,2},{3,19},{19,3},{4,20},{20... | collective-permute-start | bytes 3932168 | tf_op jit(solution)/shard_map/ppermute | solution.py:292
  71.0 2.4 %collective-permute-start.5 = (bf16[128,512]{1,0:T(8,128)(2,1)S(1)}, bf16[128,512]{1,0:T(8,128)(2,1)S(1)}, u32[]{:S(2)}, u32[]{:S(2)}) collective-permute-start(bf16[128,512]{1,0:T(8,128)(2,1)S(1)} %bitcast.135), channel_id=1, source_target_pairs={{128,0},{256,128},{384,256},{129,1},{257,129},{385,257},{130,2},{2... | collective-permute-start | bytes 393224 | tf_op jit(solution)/shard_map/ppermute | solution.py:294
  73.6 2.9 %arrange.1 = (bf16[20,256,128]{2,1,0:T(8,128)(2,1)S(1)}, bf16[20,256,128]{2,1,0:T(8,128)(2,1)S(1)}, bf16[20,128,256]{2,1,0:T(8,128)(2,1)S(1)}, bf16[20,128,256]{2,1,0:T(8,128)(2,1)S(1)}) custom-call(s32[12]{0:T(128)S(1)} %pad_add_fusion.where_ref, bf16[4,640,256]{2,1,0:T(8,128)(2,1)} %pad_maximum_fusion.my_five, ...), custom_call_target="tpu_custom_call" | custom-call | tf_op jit(solution)/shard_map/arrange/pallas_call | solution.py:182
  76.5 1.4 collective-permute-done.5.tail_ref
  77.9 5.8 %attend_tail.1 = (bf16[128,256]{1,0:T(8,128)(2,1)S(1)}, f32[20,256,256]{2,1,0:T(8,128)S(1)}) custom-call(s32[12]{0:T(128)S(1)} %pad_add_fusion.where_ref, s32[5,128]{1,0:T(8,128)S(1)} %get-tuple-element.17.query_code_ref, s32[5120,128]{1,0:T(8,128)S(1)} %broadcast_in_dim.98.key_code_ref, bf16[20,256,128]{2,1,0:T(8,128)(2,1)S(1)} %get-tuple-element.19.keys, ...), custom_call_target="tpu_custom_call" | custom-call | tf_op jit(solution)/shard_map/attend_tail/pallas_call | solution.py:194
  83.7 12.2 %attend.1 = (bf16[512,256]{1,0:T(8,128)(2,1)S(1)}, f32[4,640,256]{2,1,0:T(8,128)S(1)}, bf16[4,640,256]{2,1,0:T(8,128)(2,1)}) custom-call(s32[12]{0:T(128)S(1)} %pad_add_fusion.where_ref, s32[5,128]{1,0:T(8,128)S(1)} %get-tuple-element.17.query_code_ref, s32[5120,128]{1,0:T(8,128)S(1)} %broadcast_in_dim.98.key_code_ref, ...), custom_call_target="tpu_custom_call" | custom-call | tf_op jit(solution)/shard_map/attend/pallas_call | solution.py:214
  95.9 1.5 copy-done.1
  97.5 1.9 %collective-permute-start.7 = (bf16[4,640,256]{2,1,0:T(8,128)(2,1)}, bf16[4,640,256]{2,1,0:T(8,128)(2,1)S(1)}, u32[]{:S(2)}, u32[]{:S(2)}) collective-permute-start(bf16[4,640,256]{2,1,0:T(8,128)(2,1)} %get-tuple-element.28), channel_id=1, source_target_pairs={{0,16},{16,0},{1,17},{17,1},{2,18},{18,2},{3,19},{19,3},{4,20},{20... | collective-permute-start | bytes 3932168 | tf_op jit(solution)/shard_map/ppermute | solution.py:299
  99.4 1.9 %collective-permute-start.6 = (bf16[128,256]{1,0:T(8,128)(2,1)S(1)}, bf16[128,256]{1,0:T(8,128)(2,1)S(1)}, u32[]{:S(2)}, u32[]{:S(2)}) collective-permute-start(bf16[128,256]{1,0:T(8,128)(2,1)S(1)} %get-tuple-element.26), channel_id=1, source_target_pairs={{0,128},{128,256},{256,384},{1,129},{129,257},{257,385},{2,130},{1... | collective-permute-start | bytes 196616 | tf_op jit(solution)/shard_map/ppermute | solution.py:296
  101.3 4.2 %collective-permute-done.6 = bf16[128,256]{1,0:T(8,128)(2,1)S(1)} collective-permute-done((bf16[128,256]{1,0:T(8,128)(2,1)S(1)}, bf16[128,256]{1,0:T(8,128)(2,1)S(1)}, u32[]{:S(2)}, u32[]{:S(2)}) %collective-permute-start.6) | collective-permute-done | bytes 65568 | tf_op jit(solution)/shard_map/ppermute | solution.py:296
  106.3 11.6 %all-to-all-start.2 = ((bf16[16,32,256]{2,1,0:T(8,128)(2,1)}), bf16[16,32,256]{2,1,0:T(8,128)(2,1)S(1)}, u32[]{:S(2)}, u32[]{:S(2)}) async-start(bf16[16,32,256]{2,1,0:T(8,128)(2,1)} %bitcast.19), calls=%async_computation.2 | async-start | bytes 524288 | tf_op jit(solution)/shard_map/all_to_all | solution.py:304
  117.8 2.1 %fusion.24 = (bf16[4,640,256]{2,1,0:T(8,128)(2,1)S(1)}, f32[4,640,256]{2,1,0:T(8,128)S(1)}) fusion(f32[4,640,256]{2,1,0:T(8,128)} %copy-done.1, bf16[4,640,256]{2,1,0:T(8,128)(2,1)S(1)} %collective-permute-done.7), kind=kLoop, calls=%fused_computation.90 | loop fusion | flops 1966080 | bytes 7864320 | tf_op jit(solution)/shard_map/convert.3
  120.1 7.5 %collective-permute-start.8 = (bf16[640,256]{1,0:T(8,128)(2,1)S(1)}, bf16[640,256]{1,0:T(8,128)(2,1)S(1)}, u32[]{:S(2)}, u32[]{:S(2)}) collective-permute-start(bf16[640,256]{1,0:T(8,128)(2,1)S(1)} %get-tuple-element.38), channel_id=1, source_target_pairs={{0,4},{4,8},{8,12},{12,0},{1,5},{5,9},{9,13},{13,1},{2,6},{6,10},{... | collective-permute-start | bytes 983048 | tf_op jit(solution)/shard_map/ppermute | solution.py:310
  127.6 1.9 %collective-permute-start.10 = (bf16[640,256]{1,0:T(8,128)(2,1)S(1)}, bf16[640,256]{1,0:T(8,128)(2,1)S(1)}, u32[]{:S(2)}, u32[]{:S(2)}) collective-permute-start(bf16[640,256]{1,0:T(8,128)(2,1)S(1)} %get-tuple-element.39), channel_id=1, source_target_pairs={{0,12},{4,0},{8,4},{12,8},{1,13},{5,1},{9,5},{13,9},{2,14},{6,2},{... | collective-permute-start | bytes 983048 | tf_op jit(solution)/shard_map/ppermute | solution.py:310
  129.5 3.4 %collective-permute-start.9 = (bf16[640,256]{1,0:T(8,128)(2,1)S(1)}, bf16[640,256]{1,0:T(8,128)(2,1)S(1)}, u32[]{:S(2)}, u32[]{:S(2)}) collective-permute-start(bf16[640,256]{1,0:T(8,128)(2,1)S(1)} %get-tuple-element.40), channel_id=1, source_target_pairs={{0,8},{4,12},{8,0},{12,4},{1,9},{5,13},{9,1},{13,5},{2,10},{6,14},... | collective-permute-start | bytes 983048 | tf_op jit(solution)/shard_map/ppermute | solution.py:310
  132.9 2.8 %collective-permute-done.8 = bf16[640,256]{1,0:T(8,128)(2,1)S(1)} collective-permute-done((bf16[640,256]{1,0:T(8,128)(2,1)S(1)}, bf16[640,256]{1,0:T(8,128)(2,1)S(1)}, u32[]{:S(2)}, u32[]{:S(2)}) %collective-permute-start.8) | collective-permute-done | bytes 327712 | tf_op jit(solution)/shard_map/ppermute | solution.py:310
  135.7 4.9 %collective-permute-done.10 = bf16[640,256]{1,0:T(8,128)(2,1)S(1)} collective-permute-done((bf16[640,256]{1,0:T(8,128)(2,1)S(1)}, bf16[640,256]{1,0:T(8,128)(2,1)S(1)}, u32[]{:S(2)}, u32[]{:S(2)}) %collective-permute-start.10) | collective-permute-done | bytes 327712 | tf_op jit(solution)/shard_map/ppermute | solution.py:310
  140.7 1.9 %collective-permute-start.11 = (bf16[128,256]{1,0:T(8,128)(2,1)S(1)}, bf16[128,256]{1,0:T(8,128)(2,1)S(1)}, u32[]{:S(2)}, u32[]{:S(2)}) collective-permute-start(bf16[128,256]{1,0:T(8,128)(2,1)S(1)} %slice.131), channel_id=1, source_target_pairs={{0,128},{128,256},{256,384},{144,16},{272,144},{400,272},{1,129},{... | collective-permute-start | bytes 196616 | tf_op jit(solution)/shard_map/ppermute | solution.py:311
  142.6 4.2 %collective-permute-done.11 = bf16[128,256]{1,0:T(8,128)(2,1)S(1)} collective-permute-done((bf16[128,256]{1,0:T(8,128)(2,1)S(1)}, bf16[128,256]{1,0:T(8,128)(2,1)S(1)}, u32[]{:S(2)}, u32[]{:S(2)}) %collective-permute-start.11) | collective-permute-done | bytes 65568 | tf_op jit(solution)/shard_map/ppermute | solution.py:311
  147.6 12.0 %all-to-all-start.3 = ((bf16[16,32,256]{2,1,0:T(8,128)(2,1)}), bf16[16,32,256]{2,1,0:T(8,128)(2,1)S(1)}, u32[]{:S(2)}, u32[]{:S(2)}) async-start(bf16[16,32,256]{2,1,0:T(8,128)(2,1)} %bitcast.25), calls=%async_computation.3 | async-start | bytes 524288 | tf_op jit(solution)/shard_map/all_to_all | solution.py:317
  160.4 13.9 %all-to-all-done.3 = bf16[16,32,256]{2,1,0:T(8,128)(2,1)S(1)} async-done(((bf16[16,32,256]{2,1,0:T(8,128)(2,1)}), bf16[16,32,256]{2,1,0:T(8,128)(2,1)S(1)}, u32[]{:S(2)}, u32[]{:S(2)}) %all-to-all-start.3) | async-done | bytes 262176 | tf_op jit(solution)/shard_map/all_to_all | solution.py:317
  (57 shorter events, 11.7 us)
Async XLA Ops:
  0.6 0.9 copy-start
  0.6 17.8 %copy-start.4 = (s32[8,4]{0,1:T(4,128)S(1)}, s32[8,4]{0,1:T(4,128)}, u32[]{:S(2)}) copy-start(s32[8,4]{0,1:T(4,128)} %param.9) | copy-start | bytes 388
  0.7 20.2 %copy-start.2 = (bf16[32,4096]{1,0:T(8,128)(2,1)S(1)}, bf16[32,4096]{1,0:T(8,128)(2,1)}, u32[]{:S(2)}) copy-start(bf16[32,4096]{1,0:T(8,128)(2,1)} %param.8) | copy-start | bytes 786436
  1.5 19.4 %copy-start.3 = (bf16[32,4096]{1,0:T(8,128)(2,1)S(1)}, bf16[32,4096]{1,0:T(8,128)(2,1)}, u32[]{:S(2)}) copy-start(bf16[32,4096]{1,0:T(8,128)(2,1)} %param.5) | copy-start | bytes 786436
  3.3 33.1 %all-to-all-start = ((bf16[16,32,256]{2,1,0:T(8,128)(2,1)}), bf16[16,32,256]{2,1,0:T(8,128)(2,1)S(1)}, u32[]{:S(2)}, u32[]{:S(2)}) async-start(bf16[16,32,256]{2,1,0:T(8,128)(2,1)} %pad_maximum_fusion.3), calls=%async_computation | async-start | bytes 524288 | tf_op jit(solution)/shard_map/all_to_all | solution.py:280
  36.4 34.6 %all-to-all-start.1 = ((bf16[16,32,512]{2,1,0:T(8,128)(2,1)}), bf16[16,32,512]{2,1,0:T(8,128)(2,1)S(1)}, u32[]{:S(2)}, u32[]{:S(2)}) async-start(bf16[16,32,512]{2,1,0:T(8,128)(2,1)} %pad_maximum_fusion.1), calls=%async_computation.1 | async-start | bytes 1048576 | tf_op jit(solution)/shard_map/all_to_all | solution.py:284
  42.7 6.2 %collective-permute-start = (bf16[128,256]{1,0:T(8,128)(2,1)S(1)}, bf16[128,256]{1,0:T(8,128)(2,1)S(1)}, u32[]{:S(2)}, u32[]{:S(2)}) collective-permute-start(bf16[128,256]{1,0:T(8,128)(2,1)S(1)} %constant_dynamic-slice_fusion), channel_id=1, source_target_pairs={{128,0},{256,128},{384,256},{16,144},{144,272},{272,400},{129,1},{... | collective-permute-start | bytes 196616 | tf_op jit(solution)/shard_map/ppermute | solution.py:288
  48.9 14.0 %collective-permute-start.2 = (bf16[640,256]{1,0:T(8,128)(2,1)S(1)}, bf16[640,256]{1,0:T(8,128)(2,1)S(1)}, u32[]{:S(2)}, u32[]{:S(2)}) collective-permute-start(bf16[640,256]{1,0:T(8,128)(2,1)S(1)} %get-tuple-element.42), channel_id=1, source_target_pairs={{0,8},{4,12},{8,0},{12,4},{1,9},{5,13},{9,1},{13,5},{2,10},{6,14},... | collective-permute-start | bytes 983048 | tf_op jit(solution)/shard_map/ppermute | solution.py:290
  53.1 13.9 %collective-permute-start.1 = (bf16[640,256]{1,0:T(8,128)(2,1)S(1)}, bf16[640,256]{1,0:T(8,128)(2,1)S(1)}, u32[]{:S(2)}, u32[]{:S(2)}) collective-permute-start(bf16[640,256]{1,0:T(8,128)(2,1)S(1)} %get-tuple-element.42), channel_id=1, source_target_pairs={{0,12},{4,0},{8,4},{12,8},{1,13},{5,1},{9,5},{13,9},{2,14},{6,2},{... | collective-permute-start | bytes 983048 | tf_op jit(solution)/shard_map/ppermute | solution.py:290
  56.3 10.7 %collective-permute-start.3 = (bf16[640,256]{1,0:T(8,128)(2,1)S(1)}, bf16[640,256]{1,0:T(8,128)(2,1)S(1)}, u32[]{:S(2)}, u32[]{:S(2)}) collective-permute-start(bf16[640,256]{1,0:T(8,128)(2,1)S(1)} %get-tuple-element.42), channel_id=1, source_target_pairs={{0,4},{4,8},{8,12},{12,0},{1,5},{5,9},{9,13},{13,1},{2,6},{6,10},{... | collective-permute-start | bytes 983048 | tf_op jit(solution)/shard_map/ppermute | solution.py:290
  68.3 5.3 %collective-permute-start.4 = (bf16[4,640,256]{2,1,0:T(8,128)(2,1)}, bf16[4,640,256]{2,1,0:T(8,128)(2,1)}, u32[]{:S(2)}, u32[]{:S(2)}) collective-permute-start(bf16[4,640,256]{2,1,0:T(8,128)(2,1)} %pad_maximum_fusion.my_five), channel_id=1, source_target_pairs={{0,16},{16,0},{1,17},{17,1},{2,18},{18,2},{3,19},{19,3},{4,20},{20... | collective-permute-start | bytes 3932168 | tf_op jit(solution)/shard_map/ppermute | solution.py:292
  71.0 6.9 %collective-permute-start.5 = (bf16[128,512]{1,0:T(8,128)(2,1)S(1)}, bf16[128,512]{1,0:T(8,128)(2,1)S(1)}, u32[]{:S(2)}, u32[]{:S(2)}) collective-permute-start(bf16[128,512]{1,0:T(8,128)(2,1)S(1)} %bitcast.135), channel_id=1, source_target_pairs={{128,0},{256,128},{384,256},{129,1},{257,129},{385,257},{130,2},{2... | collective-permute-start | bytes 393224 | tf_op jit(solution)/shard_map/ppermute | solution.py:294
  95.9 1.5 copy-start.1
  97.5 20.4 %collective-permute-start.7 = (bf16[4,640,256]{2,1,0:T(8,128)(2,1)}, bf16[4,640,256]{2,1,0:T(8,128)(2,1)S(1)}, u32[]{:S(2)}, u32[]{:S(2)}) collective-permute-start(bf16[4,640,256]{2,1,0:T(8,128)(2,1)} %get-tuple-element.28), channel_id=1, source_target_pairs={{0,16},{16,0},{1,17},{17,1},{2,18},{18,2},{3,19},{19,3},{4,20},{20... | collective-permute-start | bytes 3932168 | tf_op jit(solution)/shard_map/ppermute | solution.py:299
  99.4 6.2 %collective-permute-start.6 = (bf16[128,256]{1,0:T(8,128)(2,1)S(1)}, bf16[128,256]{1,0:T(8,128)(2,1)S(1)}, u32[]{:S(2)}, u32[]{:S(2)}) collective-permute-start(bf16[128,256]{1,0:T(8,128)(2,1)S(1)} %get-tuple-element.26), channel_id=1, source_target_pairs={{0,128},{128,256},{256,384},{1,129},{129,257},{257,385},{2,130},{1... | collective-permute-start | bytes 196616 | tf_op jit(solution)/shard_map/ppermute | solution.py:296
  106.3 41.4 %all-to-all-start.2 = ((bf16[16,32,256]{2,1,0:T(8,128)(2,1)}), bf16[16,32,256]{2,1,0:T(8,128)(2,1)S(1)}, u32[]{:S(2)}, u32[]{:S(2)}) async-start(bf16[16,32,256]{2,1,0:T(8,128)(2,1)} %bitcast.19), calls=%async_computation.2 | async-start | bytes 524288 | tf_op jit(solution)/shard_map/all_to_all | solution.py:304
  120.1 15.6 %collective-permute-start.8 = (bf16[640,256]{1,0:T(8,128)(2,1)S(1)}, bf16[640,256]{1,0:T(8,128)(2,1)S(1)}, u32[]{:S(2)}, u32[]{:S(2)}) collective-permute-start(bf16[640,256]{1,0:T(8,128)(2,1)S(1)} %get-tuple-element.38), channel_id=1, source_target_pairs={{0,4},{4,8},{8,12},{12,0},{1,5},{5,9},{9,13},{13,1},{2,6},{6,10},{... | collective-permute-start | bytes 983048 | tf_op jit(solution)/shard_map/ppermute | solution.py:310
  127.6 13.0 %collective-permute-start.10 = (bf16[640,256]{1,0:T(8,128)(2,1)S(1)}, bf16[640,256]{1,0:T(8,128)(2,1)S(1)}, u32[]{:S(2)}, u32[]{:S(2)}) collective-permute-start(bf16[640,256]{1,0:T(8,128)(2,1)S(1)} %get-tuple-element.39), channel_id=1, source_target_pairs={{0,12},{4,0},{8,4},{12,8},{1,13},{5,1},{9,5},{13,9},{2,14},{6,2},{... | collective-permute-start | bytes 983048 | tf_op jit(solution)/shard_map/ppermute | solution.py:310
  129.5 11.0 %collective-permute-start.9 = (bf16[640,256]{1,0:T(8,128)(2,1)S(1)}, bf16[640,256]{1,0:T(8,128)(2,1)S(1)}, u32[]{:S(2)}, u32[]{:S(2)}) collective-permute-start(bf16[640,256]{1,0:T(8,128)(2,1)S(1)} %get-tuple-element.40), channel_id=1, source_target_pairs={{0,8},{4,12},{8,0},{12,4},{1,9},{5,13},{9,1},{13,5},{2,10},{6,14},... | collective-permute-start | bytes 983048 | tf_op jit(solution)/shard_map/ppermute | solution.py:310
  140.7 6.2 %collective-permute-start.11 = (bf16[128,256]{1,0:T(8,128)(2,1)S(1)}, bf16[128,256]{1,0:T(8,128)(2,1)S(1)}, u32[]{:S(2)}, u32[]{:S(2)}) collective-permute-start(bf16[128,256]{1,0:T(8,128)(2,1)S(1)} %slice.131), channel_id=1, source_target_pairs={{0,128},{128,256},{256,384},{144,16},{272,144},{400,272},{1,129},{... | collective-permute-start | bytes 196616 | tf_op jit(solution)/shard_map/ppermute | solution.py:311
  147.6 26.7 %all-to-all-start.3 = ((bf16[16,32,256]{2,1,0:T(8,128)(2,1)}), bf16[16,32,256]{2,1,0:T(8,128)(2,1)S(1)}, u32[]{:S(2)}, u32[]{:S(2)}) async-start(bf16[16,32,256]{2,1,0:T(8,128)(2,1)} %bitcast.25), calls=%async_computation.3 | async-start | bytes 524288 | tf_op jit(solution)/shard_map/all_to_all | solution.py:317

commit v5 on v4

--- a/solution.py
+++ b/solution.py
@@ -16,6 +16,7 @@
 SLAB = 4096
 RUN = 128
 RUNS = ZH + 1
+HALF = ZH // 2
 SLOTS = 2 * RUNS
 KB = 256
 BLOCKS = SLOTS * 512 // KB
@@ -148,8 +149,23 @@
         dq_ref[...] = jnp.zeros((RUN, 256), jnp.bfloat16)
 
 
-def attend(
-    where_ref, query_code_ref, key_code_ref, keys, values, keys_t, values_t, qg_ref, tail_sums,
+def attend_first(
+    where_ref, query_code_ref, key_code_ref, keys, values, keys_t, values_t, qg_ref,
+    dq_ref, sums,
+    ratios, expos,
+):
+    refs = (where_ref, query_code_ref, key_code_ref, keys, values, keys_t, values_t)
+    for block in range(BLOCKS):
+        sums[block] = jnp.zeros((KB, 2 * HEAD_DIM), jnp.float32)
+
+    for run in range(HALF):
+        rows = slice(run * RUN, (run + 1) * RUN)
+        one_run(run, qg_ref, rows, refs, dq_ref, rows, ratios, expos, sums)
+
+
+def attend_last(
+    where_ref, query_code_ref, key_code_ref, keys, values, keys_t, values_t, qg_ref,
+    first_sums, tail_sums,
     dq_ref, mine_ref, other_ref,
     ratios, expos, sums,
 ):
@@ -158,18 +174,21 @@
     b16 = jnp.bfloat16
     refs = (where_ref, query_code_ref, key_code_ref, keys, values, keys_t, values_t)
     for block in range(BLOCKS):
-        sums[block] = tail_sums[block]
-
-    for run in range(ZH):
+        sums[block] = first_sums[block] + tail_sums[block]
+
+    for run in range(HALF, ZH):
         rows = slice(run * RUN, (run + 1) * RUN)
-        one_run(run, qg_ref, rows, refs, dq_ref, rows, ratios, expos, sums)
+        out = slice((run - HALF) * RUN, (run - HALF + 1) * RUN)
+        one_run(run, qg_ref, rows, refs, dq_ref, out, ratios, expos, sums)
 
     for dy in range(Y):
         row = (y + dy) % Y
         at = pl.multiple_of((row % 2) * RUN, RUN)
         for run in range(RUNS):
             rows = slice(run * RUN, (run + 1) * RUN)
-            mine_ref[dy, rows, :] = sums[slot_of(run, core) * 2 + row // 2, pl.ds(at, RUN), :]
+            mine_ref[dy, rows, :] = sums[
+                slot_of(run, core) * 2 + row // 2, pl.ds(at, RUN), :
+            ].astype(b16)
             other_ref[dy, rows, :] = sums[
                 slot_of(run, 1 - core) * 2 + row // 2, pl.ds(at, RUN), :
             ].astype(b16)
@@ -189,45 +208,20 @@
     )(where, *pieces)
 
 
-def call_tail(where, query_code, key_code, arranged, tail):
+def call_runs(kernel, out_shape, operands, more_scratch, grant):
     vmem = pl.BlockSpec(memory_space=pltpu.VMEM)
     return pl.pallas_call(
-        attend_tail,
-        out_shape=(
-            jax.ShapeDtypeStruct((RUN, 256), jnp.bfloat16),
-            jax.ShapeDtypeStruct((BLOCKS, KB, 2 * HEAD_DIM), jnp.float32),
-        ),
-        in_specs=[pl.BlockSpec(memory_space=pltpu.SMEM)] + [vmem] * 7,
-        out_specs=(vmem, vmem),
+        kernel,
+        out_shape=out_shape,
+        in_specs=[pl.BlockSpec(memory_space=pltpu.SMEM)] + [vmem] * (len(operands) - 1),
+        out_specs=(vmem,) * len(out_shape),
         scratch_shapes=[
             pltpu.VMEM((MOST, KB, 2 * RUN), jnp.float32),
             pltpu.VMEM((MOST, KB, 2 * RUN), jnp.float32),
+            *more_scratch,
         ],
-        compiler_params=pltpu.CompilerParams(vmem_limit_bytes=24 << 20),
-        name="attend_tail",
-    )(where, query_code, key_code, *arranged, tail)
-
-
-def call_attend(where, query_code, key_code, arranged, qg, tail_sums):
-    vmem = pl.BlockSpec(memory_space=pltpu.VMEM)
-    rows = RUNS * RUN
-    return pl.pallas_call(
-        attend,
-        out_shape=(
-            jax.ShapeDtypeStruct((ZH * RUN, 256), jnp.bfloat16),
-            jax.ShapeDtypeStruct((Y, rows, 256), jnp.float32),
-            jax.ShapeDtypeStruct((Y, rows, 256), jnp.bfloat16),
-        ),
-        in_specs=[pl.BlockSpec(memory_space=pltpu.SMEM)] + [vmem] * 8,
-        out_specs=(vmem, vmem, vmem),
-        scratch_shapes=[
-            pltpu.VMEM((MOST, KB, 2 * RUN), jnp.float32),
-            pltpu.VMEM((MOST, KB, 2 * RUN), jnp.float32),
-            pltpu.VMEM((BLOCKS, KB, 2 * HEAD_DIM), jnp.float32),
-        ],
-        compiler_params=pltpu.CompilerParams(vmem_limit_bytes=36 << 20),
-        name="attend",
-    )(where, query_code, key_code, *arranged, qg, tail_sums)
+        compiler_params=pltpu.CompilerParams(vmem_limit_bytes=grant << 20),
+    )(*operands)
 
 
 def tables(x, core, y, pack_table):
@@ -292,22 +286,39 @@
     other_five = lax.ppermute(stack, "core", ring(CORE, 1))
     arranged = call_arrange(where, (stack, other_five))
     tail = lax.ppermute(qg[:RUN], ("x", "core"), tails)
-    dq_tail, tail_sums = call_tail(where, query_code, key_code, arranged, tail)
+    common = (where, query_code, key_code, *arranged)
+    sums_shape = (BLOCKS, KB, 2 * HEAD_DIM)
+    shape = jax.ShapeDtypeStruct
+    dq_first, first_sums = call_runs(
+        attend_first,
+        (shape((HALF * RUN, 256), b16), shape(sums_shape, f32)), (*common, qg), (), 12,
+    )
+    dq_tail, tail_sums = call_runs(
+        attend_tail,
+        (shape((RUN, 256), b16), shape(sums_shape, f32)), (*common, tail), (), 12,
+    )
     dq_tail = lax.ppermute(dq_tail, ("x", "core"), [(b, a) for a, b in tails])
-    dq, mine, other = call_attend(where, query_code, key_code, arranged, qg, tail_sums)
+    dq_last, mine, other = call_runs(
+        attend_last,
+        (
+            shape(((ZH - HALF) * RUN, 256), b16),
+            shape((Y, RUNS * RUN, 256), b16),
+            shape((Y, RUNS * RUN, 256), b16),
+        ),
+        (*common, qg, first_sums, tail_sums), (pltpu.VMEM(sums_shape, f32),), 18,
+    )
 
     other = lax.ppermute(other, "core", ring(CORE, 1))
-    dq = jnp.concatenate(
-        [(dq[:RUN].astype(f32) + dq_tail.astype(f32)).astype(b16), dq[RUN:]], axis=0
-    )
+    dq_home = (dq_first[:RUN].astype(f32) + dq_tail.astype(f32)).astype(b16)
+    dq = jnp.concatenate([dq_home, dq_first[RUN:], dq_last], axis=0)
     dq = dq.reshape(HEADS, tokens, 256)
     dq = lax.all_to_all(dq, z, split_axis=0, concat_axis=0, tiled=True)
     grad_query = jnp.transpose(dq, (1, 0, 2)).reshape(tokens, HEADS * 256)
 
-    part = mine + other.astype(f32)
-    total = part[0]
+    sent = (mine[1:].astype(f32) + other[1:].astype(f32)).astype(b16)
+    total = mine[0].astype(f32) + other[0].astype(f32)
     for dy in range(1, Y):
-        total = total + lax.ppermute(part[dy].astype(b16), "y", ring(Y, dy)).astype(f32)
+        total = total + lax.ppermute(sent[dy - 1], "y", ring(Y, dy)).astype(f32)
     border = lax.ppermute(total[ZH * RUN :].astype(b16), ("x", "core"), back).astype(f32)
     gap = (ZH - 1) * RUN
     total = total[: ZH * RUN] + jnp.where(

time: 177 us -> 175 us (0.989)
  other arithmetic: 8.52 us -> 6.67 us
    another operation x1 -> x0, other arithmetic: 2.13 us -> none
    pallas_call x2 -> x3, Pallas kernels: 18 us -> 19.1 us  [call_runs(): pl.pallas_call(kernel, out_shape=out_shape, in_specs=[pl.BlockSpec(memory...]
  transfers between devices with their start and end apart: 16 -> 16, of which waited for: 13 -> 12; matrix products, arithmetic and copies ran while one was open for 6% -> 5% of each run, Pallas kernels for 2% -> 4%
where the time goes in v5:
time: 175 us; the launch traced here: 174 us
  starting transfers between devices  81.3 us (46%)
  waiting for transfers between devices  56.4 us (32%)
  Pallas kernels  22 us (13%)
  other arithmetic  6.67 us (4%)
  local copies, waits for them, and re-layouts  6.59 us (4%)
    pallas_call x3, Pallas kernels, call_runs(): pl.pallas_call(kernel, out_shape=out_shape, in_specs=[pl.BlockSpec(memory...  19.1 us
    all_to_all x1, starting transfers between devices, local(): kv = lax.all_to_all(kv, z, split_axis=0, concat_axis=0, tiled=True)  15.2 us
    all_to_all x1, waiting for transfers between devices, local(): dkv = lax.all_to_all(dkv, z, split_axis=0, concat_axis=0, tiled=True)  13.9 us
    all_to_all x1, waiting for transfers between devices, local(): kv = lax.all_to_all(kv, z, split_axis=0, concat_axis=0, tiled=True)  13.7 us
    ppermute x3, starting transfers between devices, local(): total = total + lax.ppermute(sent[dy - 1], 'y', ring(Y, dy)).astype(f32)  12.8 us
    all_to_all x1, starting transfers between devices, local(): dq = lax.all_to_all(dq, z, split_axis=0, concat_axis=0, tiled=True)  12.3 us
    all_to_all x1, starting transfers between devices, local(): dkv = lax.all_to_all(dkv, z, split_axis=0, concat_axis=0, tiled=True)  12 us
    ppermute x3, starting transfers between devices, local(): lax.ppermute(five, 'y', ring(Y, -dy))  10 us
  transfers between devices with their start and end apart: 16, of which 12 were waited for; matrix products, arithmetic and copies ran while one was open for 5% of the time, Pallas kernels for 4%

profile of v5, /device:TPU:42, one launch (start us, length us, event | category | flops | bytes accessed | tf_op | source)
XLA Modules:
  0.0 173.9 jit_solution(12728019481516498485)
XLA Ops:
  1.5 1.0 bitcast_bitcast_fusion.2
  3.3 15.2 %all-to-all-start = ((bf16[16,32,256]{2,1,0:T(8,128)(2,1)}), bf16[16,32,256]{2,1,0:T(8,128)(2,1)S(1)}, u32[]{:S(2)}, u32[]{:S(2)}) async-start(bf16[16,32,256]{2,1,0:T(8,128)(2,1)} %pad_maximum_fusion.3), calls=%async_computation | async-start | bytes 524288 | tf_op jit(solution)/shard_map/all_to_all | solution.py:274
  22.7 13.7 %all-to-all-done = bf16[16,32,256]{2,1,0:T(8,128)(2,1)S(1)} async-done(((bf16[16,32,256]{2,1,0:T(8,128)(2,1)}), bf16[16,32,256]{2,1,0:T(8,128)(2,1)S(1)}, u32[]{:S(2)}, u32[]{:S(2)}) %all-to-all-start) | async-done | bytes 262176 | tf_op jit(solution)/shard_map/all_to_all | solution.py:274
  36.4 6.2 %all-to-all-start.1 = ((bf16[16,32,512]{2,1,0:T(8,128)(2,1)}), bf16[16,32,512]{2,1,0:T(8,128)(2,1)S(1)}, u32[]{:S(2)}, u32[]{:S(2)}) async-start(bf16[16,32,512]{2,1,0:T(8,128)(2,1)} %pad_maximum_fusion.1), calls=%async_computation.1 | async-start | bytes 1048576 | tf_op jit(solution)/shard_map/all_to_all | solution.py:278
  42.7 2.4 %collective-permute-start = (bf16[128,256]{1,0:T(8,128)(2,1)S(1)}, bf16[128,256]{1,0:T(8,128)(2,1)S(1)}, u32[]{:S(2)}, u32[]{:S(2)}) collective-permute-start(bf16[128,256]{1,0:T(8,128)(2,1)S(1)} %constant_dynamic-slice_fusion), channel_id=1, source_target_pairs={{128,0},{256,128},{384,256},{16,144},{144,272},{272,400},{129,1},{... | collective-permute-start | bytes 196616 | tf_op jit(solution)/shard_map/ppermute | solution.py:282
  45.1 3.7 %collective-permute-done = bf16[128,256]{1,0:T(8,128)(2,1)S(1)} collective-permute-done((bf16[128,256]{1,0:T(8,128)(2,1)S(1)}, bf16[128,256]{1,0:T(8,128)(2,1)S(1)}, u32[]{:S(2)}, u32[]{:S(2)}) %collective-permute-start) | collective-permute-done | bytes 65568 | tf_op jit(solution)/shard_map/ppermute | solution.py:282
  48.9 4.2 %collective-permute-start.2 = (bf16[640,256]{1,0:T(8,128)(2,1)S(1)}, bf16[640,256]{1,0:T(8,128)(2,1)S(1)}, u32[]{:S(2)}, u32[]{:S(2)}) collective-permute-start(bf16[640,256]{1,0:T(8,128)(2,1)S(1)} %get-tuple-element.44), channel_id=1, source_target_pairs={{0,8},{4,12},{8,0},{12,4},{1,9},{5,13},{9,1},{13,5},{2,10},{6,14},... | collective-permute-start | bytes 983048 | tf_op jit(solution)/shard_map/ppermute | solution.py:284
  53.1 3.3 %collective-permute-start.1 = (bf16[640,256]{1,0:T(8,128)(2,1)S(1)}, bf16[640,256]{1,0:T(8,128)(2,1)S(1)}, u32[]{:S(2)}, u32[]{:S(2)}) collective-permute-start(bf16[640,256]{1,0:T(8,128)(2,1)S(1)} %get-tuple-element.44), channel_id=1, source_target_pairs={{0,12},{4,0},{8,4},{12,8},{1,13},{5,1},{9,5},{13,9},{2,14},{6,2},{... | collective-permute-start | bytes 983048 | tf_op jit(solution)/shard_map/ppermute | solution.py:284
  56.3 2.6 %collective-permute-start.3 = (bf16[640,256]{1,0:T(8,128)(2,1)S(1)}, bf16[640,256]{1,0:T(8,128)(2,1)S(1)}, u32[]{:S(2)}, u32[]{:S(2)}) collective-permute-start(bf16[640,256]{1,0:T(8,128)(2,1)S(1)} %get-tuple-element.44), channel_id=1, source_target_pairs={{0,4},{4,8},{8,12},{12,0},{1,5},{5,9},{9,13},{13,1},{2,6},{6,10},{... | collective-permute-start | bytes 983048 | tf_op jit(solution)/shard_map/ppermute | solution.py:284
  58.9 3.9 %collective-permute-done.2 = bf16[640,256]{1,0:T(8,128)(2,1)S(1)} collective-permute-done((bf16[640,256]{1,0:T(8,128)(2,1)S(1)}, bf16[640,256]{1,0:T(8,128)(2,1)S(1)}, u32[]{:S(2)}, u32[]{:S(2)}) %collective-permute-start.2) | collective-permute-done | bytes 327712 | tf_op jit(solution)/shard_map/ppermute | solution.py:284
  62.9 4.1 %collective-permute-done.1 = bf16[640,256]{1,0:T(8,128)(2,1)S(1)} collective-permute-done((bf16[640,256]{1,0:T(8,128)(2,1)S(1)}, bf16[640,256]{1,0:T(8,128)(2,1)S(1)}, u32[]{:S(2)}, u32[]{:S(2)}) %collective-permute-start.1) | collective-permute-done | bytes 327712 | tf_op jit(solution)/shard_map/ppermute | solution.py:284
  67.1 1.2 pad_maximum_fusion.my_five
  68.3 1.9 %collective-permute-start.4 = (bf16[4,640,256]{2,1,0:T(8,128)(2,1)}, bf16[4,640,256]{2,1,0:T(8,128)(2,1)}, u32[]{:S(2)}, u32[]{:S(2)}) collective-permute-start(bf16[4,640,256]{2,1,0:T(8,128)(2,1)} %pad_maximum_fusion.my_five), channel_id=1, source_target_pairs={{0,16},{16,0},{1,17},{17,1},{2,18},{18,2},{3,19},{19,3},{4,20},{20... | collective-permute-start | bytes 3932168 | tf_op jit(solution)/shard_map/ppermute | solution.py:286
  71.0 2.4 %collective-permute-start.5 = (bf16[128,512]{1,0:T(8,128)(2,1)S(1)}, bf16[128,512]{1,0:T(8,128)(2,1)S(1)}, u32[]{:S(2)}, u32[]{:S(2)}) collective-permute-start(bf16[128,512]{1,0:T(8,128)(2,1)S(1)} %bitcast.134), channel_id=1, source_target_pairs={{128,0},{256,128},{384,256},{129,1},{257,129},{385,257},{130,2},{2... | collective-permute-start | bytes 393224 | tf_op jit(solution)/shard_map/ppermute | solution.py:288
  73.6 2.9 %arrange.1 = (bf16[20,256,128]{2,1,0:T(8,128)(2,1)S(1)}, bf16[20,256,128]{2,1,0:T(8,128)(2,1)S(1)}, bf16[20,128,256]{2,1,0:T(8,128)(2,1)S(1)}, bf16[20,128,256]{2,1,0:T(8,128)(2,1)S(1)}) custom-call(s32[12]{0:T(128)S(1)} %pad_add_fusion.where_ref, bf16[4,640,256]{2,1,0:T(8,128)(2,1)} %pad_maximum_fusion.my_five, ...), custom_call_target="tpu_custom_call" | custom-call | tf_op jit(solution)/shard_map/arrange/pallas_call | solution.py:201
  76.5 3.5 %shard_map.76 = (bf16[256,256]{1,0:T(8,128)(2,1)S(1)}, f32[20,256,256]{2,1,0:T(8,128)S(1)}) custom-call(s32[12]{0:T(128)S(1)} %pad_add_fusion.where_ref, s32[5,128]{1,0:T(8,128)S(1)} %get-tuple-element.19.query_code_ref, s32[5120,128]{1,0:T(8,128)S(1)} %broadcast_in_dim.98.key_code_ref, bf16[20,256,128]{2,1,0:T(8,128)(2,1)S(1)} %get-tuple-element.21.keys, ...), custom_call_target="tpu_custom_call" | custom-call | tf_op jit(solution)/shard_map/pallas_call | solution.py:213
  80.0 5.8 %shard_map.77 = (bf16[128,256]{1,0:T(8,128)(2,1)S(1)}, f32[20,256,256]{2,1,0:T(8,128)S(1)}) custom-call(s32[12]{0:T(128)S(1)} %pad_add_fusion.where_ref, s32[5,128]{1,0:T(8,128)S(1)} %get-tuple-element.19.query_code_ref, s32[5120,128]{1,0:T(8,128)S(1)} %broadcast_in_dim.98.key_code_ref, bf16[20,256,128]{2,1,0:T(8,128)(2,1)S(1)} %get-tuple-element.21.keys, ...), custom_call_target="tpu_custom_call" | custom-call | tf_op jit(solution)/shard_map/pallas_call | solution.py:213
  85.9 9.7 %shard_map.78 = (bf16[256,256]{1,0:T(8,128)(2,1)S(1)}, bf16[4,640,256]{2,1,0:T(8,128)(2,1)S(1)}, bf16[4,640,256]{2,1,0:T(8,128)(2,1)}) custom-call(s32[12]{0:T(128)S(1)} %pad_add_fusion.where_ref, s32[5,128]{1,0:T(8,128)S(1)} %get-tuple-element.19.query_code_ref, s32[5120,128]{1,0:T(8,128)S(1)} %broadcast_in_dim.98.key_code_ref, ...), custom_call_target="tpu_custom_call" | custom-call | tf_op jit(solution)/shard_map/pallas_call | solution.py:213
  95.6 1.1 copy-done.1
  96.7 2.0 %collective-permute-start.7 = (bf16[4,640,256]{2,1,0:T(8,128)(2,1)}, bf16[4,640,256]{2,1,0:T(8,128)(2,1)S(1)}, u32[]{:S(2)}, u32[]{:S(2)}) collective-permute-start(bf16[4,640,256]{2,1,0:T(8,128)(2,1)} %get-tuple-element.32), channel_id=1, source_target_pairs={{0,16},{16,0},{1,17},{17,1},{2,18},{18,2},{3,19},{19,3},{4,20},{20... | collective-permute-start | bytes 3932168 | tf_op jit(solution)/shard_map/ppermute | solution.py:311
  98.7 1.9 %collective-permute-start.6 = (bf16[128,256]{1,0:T(8,128)(2,1)S(1)}, bf16[128,256]{1,0:T(8,128)(2,1)S(1)}, u32[]{:S(2)}, u32[]{:S(2)}) collective-permute-start(bf16[128,256]{1,0:T(8,128)(2,1)S(1)} %get-tuple-element.27), channel_id=1, source_target_pairs={{0,128},{128,256},{256,384},{1,129},{129,257},{257,385},{2,130},{1... | collective-permute-start | bytes 196616 | tf_op jit(solution)/shard_map/ppermute | solution.py:300
  100.6 4.2 %collective-permute-done.6 = bf16[128,256]{1,0:T(8,128)(2,1)S(1)} collective-permute-done((bf16[128,256]{1,0:T(8,128)(2,1)S(1)}, bf16[128,256]{1,0:T(8,128)(2,1)S(1)}, u32[]{:S(2)}, u32[]{:S(2)}) %collective-permute-start.6) | collective-permute-done | bytes 65568 | tf_op jit(solution)/shard_map/ppermute | solution.py:300
  105.6 12.3 %all-to-all-start.2 = ((bf16[16,32,256]{2,1,0:T(8,128)(2,1)}), bf16[16,32,256]{2,1,0:T(8,128)(2,1)S(1)}, u32[]{:S(2)}, u32[]{:S(2)}) async-start(bf16[16,32,256]{2,1,0:T(8,128)(2,1)} %bitcast.19), calls=%async_computation.2 | async-start | bytes 524288 | tf_op jit(solution)/shard_map/all_to_all | solution.py:315
  118.3 7.5 %collective-permute-start.8 = (bf16[640,256]{1,0:T(8,128)(2,1)S(1)}, bf16[640,256]{1,0:T(8,128)(2,1)S(1)}, u32[]{:S(2)}, u32[]{:S(2)}) collective-permute-start(bf16[640,256]{1,0:T(8,128)(2,1)S(1)} %get-tuple-element.40), channel_id=1, source_target_pairs={{0,4},{4,8},{8,12},{12,0},{1,5},{5,9},{9,13},{13,1},{2,6},{6,10},{... | collective-permute-start | bytes 983048 | tf_op jit(solution)/shard_map/ppermute | solution.py:321
  125.8 1.9 %collective-permute-start.10 = (bf16[640,256]{1,0:T(8,128)(2,1)S(1)}, bf16[640,256]{1,0:T(8,128)(2,1)S(1)}, u32[]{:S(2)}, u32[]{:S(2)}) collective-permute-start(bf16[640,256]{1,0:T(8,128)(2,1)S(1)} %get-tuple-element.41), channel_id=1, source_target_pairs={{0,12},{4,0},{8,4},{12,8},{1,13},{5,1},{9,5},{13,9},{2,14},{6,2},{... | collective-permute-start | bytes 983048 | tf_op jit(solution)/shard_map/ppermute | solution.py:321
  127.7 3.4 %collective-permute-start.9 = (bf16[640,256]{1,0:T(8,128)(2,1)S(1)}, bf16[640,256]{1,0:T(8,128)(2,1)S(1)}, u32[]{:S(2)}, u32[]{:S(2)}) collective-permute-start(bf16[640,256]{1,0:T(8,128)(2,1)S(1)} %get-tuple-element.42), channel_id=1, source_target_pairs={{0,8},{4,12},{8,0},{12,4},{1,9},{5,13},{9,1},{13,5},{2,10},{6,14},... | collective-permute-start | bytes 983048 | tf_op jit(solution)/shard_map/ppermute | solution.py:321
  131.1 2.8 %collective-permute-done.8 = bf16[640,256]{1,0:T(8,128)(2,1)S(1)} collective-permute-done((bf16[640,256]{1,0:T(8,128)(2,1)S(1)}, bf16[640,256]{1,0:T(8,128)(2,1)S(1)}, u32[]{:S(2)}, u32[]{:S(2)}) %collective-permute-start.8) | collective-permute-done | bytes 327712 | tf_op jit(solution)/shard_map/ppermute | solution.py:321
  133.8 4.9 %collective-permute-done.10 = bf16[640,256]{1,0:T(8,128)(2,1)S(1)} collective-permute-done((bf16[640,256]{1,0:T(8,128)(2,1)S(1)}, bf16[640,256]{1,0:T(8,128)(2,1)S(1)}, u32[]{:S(2)}, u32[]{:S(2)}) %collective-permute-start.10) | collective-permute-done | bytes 327712 | tf_op jit(solution)/shard_map/ppermute | solution.py:321
  138.9 1.9 %collective-permute-start.11 = (bf16[128,256]{1,0:T(8,128)(2,1)S(1)}, bf16[128,256]{1,0:T(8,128)(2,1)S(1)}, u32[]{:S(2)}, u32[]{:S(2)}) collective-permute-start(bf16[128,256]{1,0:T(8,128)(2,1)S(1)} %slice.138), channel_id=1, source_target_pairs={{0,128},{128,256},{256,384},{144,16},{272,144},{400,272},{1,129},{... | collective-permute-start | bytes 196616 | tf_op jit(solution)/shard_map/ppermute | solution.py:322
  140.9 4.2 %collective-permute-done.11 = bf16[128,256]{1,0:T(8,128)(2,1)S(1)} collective-permute-done((bf16[128,256]{1,0:T(8,128)(2,1)S(1)}, bf16[128,256]{1,0:T(8,128)(2,1)S(1)}, u32[]{:S(2)}, u32[]{:S(2)}) %collective-permute-start.11) | collective-permute-done | bytes 65568 | tf_op jit(solution)/shard_map/ppermute | solution.py:322
  145.9 12.0 %all-to-all-start.3 = ((bf16[16,32,256]{2,1,0:T(8,128)(2,1)}), bf16[16,32,256]{2,1,0:T(8,128)(2,1)S(1)}, u32[]{:S(2)}, u32[]{:S(2)}) async-start(bf16[16,32,256]{2,1,0:T(8,128)(2,1)} %bitcast.25), calls=%async_computation.3 | async-start | bytes 524288 | tf_op jit(solution)/shard_map/all_to_all | solution.py:328
  158.6 13.9 %all-to-all-done.3 = bf16[16,32,256]{2,1,0:T(8,128)(2,1)S(1)} async-done(((bf16[16,32,256]{2,1,0:T(8,128)(2,1)}), bf16[16,32,256]{2,1,0:T(8,128)(2,1)S(1)}, u32[]{:S(2)}, u32[]{:S(2)}) %all-to-all-start.3) | async-done | bytes 262176 | tf_op jit(solution)/shard_map/all_to_all | solution.py:328
  (60 shorter events, 11.0 us)
Async XLA Ops:
  0.6 0.9 copy-start
  0.6 17.8 %copy-start.5 = (s32[8,4]{0,1:T(4,128)S(1)}, s32[8,4]{0,1:T(4,128)}, u32[]{:S(2)}) copy-start(s32[8,4]{0,1:T(4,128)} %param.9) | copy-start | bytes 388
  0.7 20.2 %copy-start.3 = (bf16[32,4096]{1,0:T(8,128)(2,1)S(1)}, bf16[32,4096]{1,0:T(8,128)(2,1)}, u32[]{:S(2)}) copy-start(bf16[32,4096]{1,0:T(8,128)(2,1)} %param.8) | copy-start | bytes 786436
  1.5 19.3 %copy-start.4 = (bf16[32,4096]{1,0:T(8,128)(2,1)S(1)}, bf16[32,4096]{1,0:T(8,128)(2,1)}, u32[]{:S(2)}) copy-start(bf16[32,4096]{1,0:T(8,128)(2,1)} %param.5) | copy-start | bytes 786436
  3.3 33.1 %all-to-all-start = ((bf16[16,32,256]{2,1,0:T(8,128)(2,1)}), bf16[16,32,256]{2,1,0:T(8,128)(2,1)S(1)}, u32[]{:S(2)}, u32[]{:S(2)}) async-start(bf16[16,32,256]{2,1,0:T(8,128)(2,1)} %pad_maximum_fusion.3), calls=%async_computation | async-start | bytes 524288 | tf_op jit(solution)/shard_map/all_to_all | solution.py:274
  36.4 34.6 %all-to-all-start.1 = ((bf16[16,32,512]{2,1,0:T(8,128)(2,1)}), bf16[16,32,512]{2,1,0:T(8,128)(2,1)S(1)}, u32[]{:S(2)}, u32[]{:S(2)}) async-start(bf16[16,32,512]{2,1,0:T(8,128)(2,1)} %pad_maximum_fusion.1), calls=%async_computation.1 | async-start | bytes 1048576 | tf_op jit(solution)/shard_map/all_to_all | solution.py:278
  42.7 6.2 %collective-permute-start = (bf16[128,256]{1,0:T(8,128)(2,1)S(1)}, bf16[128,256]{1,0:T(8,128)(2,1)S(1)}, u32[]{:S(2)}, u32[]{:S(2)}) collective-permute-start(bf16[128,256]{1,0:T(8,128)(2,1)S(1)} %constant_dynamic-slice_fusion), channel_id=1, source_target_pairs={{128,0},{256,128},{384,256},{16,144},{144,272},{272,400},{129,1},{... | collective-permute-start | bytes 196616 | tf_op jit(solution)/shard_map/ppermute | solution.py:282
  48.9 14.0 %collective-permute-start.2 = (bf16[640,256]{1,0:T(8,128)(2,1)S(1)}, bf16[640,256]{1,0:T(8,128)(2,1)S(1)}, u32[]{:S(2)}, u32[]{:S(2)}) collective-permute-start(bf16[640,256]{1,0:T(8,128)(2,1)S(1)} %get-tuple-element.44), channel_id=1, source_target_pairs={{0,8},{4,12},{8,0},{12,4},{1,9},{5,13},{9,1},{13,5},{2,10},{6,14},... | collective-permute-start | bytes 983048 | tf_op jit(solution)/shard_map/ppermute | solution.py:284
  53.1 13.9 %collective-permute-start.1 = (bf16[640,256]{1,0:T(8,128)(2,1)S(1)}, bf16[640,256]{1,0:T(8,128)(2,1)S(1)}, u32[]{:S(2)}, u32[]{:S(2)}) collective-permute-start(bf16[640,256]{1,0:T(8,128)(2,1)S(1)} %get-tuple-element.44), channel_id=1, source_target_pairs={{0,12},{4,0},{8,4},{12,8},{1,13},{5,1},{9,5},{13,9},{2,14},{6,2},{... | collective-permute-start | bytes 983048 | tf_op jit(solution)/shard_map/ppermute | solution.py:284
  56.3 10.7 %collective-permute-start.3 = (bf16[640,256]{1,0:T(8,128)(2,1)S(1)}, bf16[640,256]{1,0:T(8,128)(2,1)S(1)}, u32[]{:S(2)}, u32[]{:S(2)}) collective-permute-start(bf16[640,256]{1,0:T(8,128)(2,1)S(1)} %get-tuple-element.44), channel_id=1, source_target_pairs={{0,4},{4,8},{8,12},{12,0},{1,5},{5,9},{9,13},{13,1},{2,6},{6,10},{... | collective-permute-start | bytes 983048 | tf_op jit(solution)/shard_map/ppermute | solution.py:284
  68.3 5.3 %collective-permute-start.4 = (bf16[4,640,256]{2,1,0:T(8,128)(2,1)}, bf16[4,640,256]{2,1,0:T(8,128)(2,1)}, u32[]{:S(2)}, u32[]{:S(2)}) collective-permute-start(bf16[4,640,256]{2,1,0:T(8,128)(2,1)} %pad_maximum_fusion.my_five), channel_id=1, source_target_pairs={{0,16},{16,0},{1,17},{17,1},{2,18},{18,2},{3,19},{19,3},{4,20},{20... | collective-permute-start | bytes 3932168 | tf_op jit(solution)/shard_map/ppermute | solution.py:286
  71.0 9.0 %collective-permute-start.5 = (bf16[128,512]{1,0:T(8,128)(2,1)S(1)}, bf16[128,512]{1,0:T(8,128)(2,1)S(1)}, u32[]{:S(2)}, u32[]{:S(2)}) collective-permute-start(bf16[128,512]{1,0:T(8,128)(2,1)S(1)} %bitcast.134), channel_id=1, source_target_pairs={{128,0},{256,128},{384,256},{129,1},{257,129},{385,257},{130,2},{2... | collective-permute-start | bytes 393224 | tf_op jit(solution)/shard_map/ppermute | solution.py:288
  95.6 1.1 copy-start.1
  96.7 21.3 %copy-start.2 = (bf16[4,640,256]{2,1,0:T(8,128)(2,1)S(1)}, bf16[4,640,256]{2,1,0:T(8,128)(2,1)}, u32[]{:S(2)}) copy-start(bf16[4,640,256]{2,1,0:T(8,128)(2,1)} %copy-done.1) | copy-start | bytes 3932164
  96.7 21.3 %collective-permute-start.7 = (bf16[4,640,256]{2,1,0:T(8,128)(2,1)}, bf16[4,640,256]{2,1,0:T(8,128)(2,1)S(1)}, u32[]{:S(2)}, u32[]{:S(2)}) collective-permute-start(bf16[4,640,256]{2,1,0:T(8,128)(2,1)} %get-tuple-element.32), channel_id=1, source_target_pairs={{0,16},{16,0},{1,17},{17,1},{2,18},{18,2},{3,19},{19,3},{4,20},{20... | collective-permute-start | bytes 3932168 | tf_op jit(solution)/shard_map/ppermute | solution.py:311
  98.7 6.2 %collective-permute-start.6 = (bf16[128,256]{1,0:T(8,128)(2,1)S(1)}, bf16[128,256]{1,0:T(8,128)(2,1)S(1)}, u32[]{:S(2)}, u32[]{:S(2)}) collective-permute-start(bf16[128,256]{1,0:T(8,128)(2,1)S(1)} %get-tuple-element.27), channel_id=1, source_target_pairs={{0,128},{128,256},{256,384},{1,129},{129,257},{257,385},{2,130},{1... | collective-permute-start | bytes 196616 | tf_op jit(solution)/shard_map/ppermute | solution.py:300
  105.6 40.3 %all-to-all-start.2 = ((bf16[16,32,256]{2,1,0:T(8,128)(2,1)}), bf16[16,32,256]{2,1,0:T(8,128)(2,1)S(1)}, u32[]{:S(2)}, u32[]{:S(2)}) async-start(bf16[16,32,256]{2,1,0:T(8,128)(2,1)} %bitcast.19), calls=%async_computation.2 | async-start | bytes 524288 | tf_op jit(solution)/shard_map/all_to_all | solution.py:315
  118.3 15.6 %collective-permute-start.8 = (bf16[640,256]{1,0:T(8,128)(2,1)S(1)}, bf16[640,256]{1,0:T(8,128)(2,1)S(1)}, u32[]{:S(2)}, u32[]{:S(2)}) collective-permute-start(bf16[640,256]{1,0:T(8,128)(2,1)S(1)} %get-tuple-element.40), channel_id=1, source_target_pairs={{0,4},{4,8},{8,12},{12,0},{1,5},{5,9},{9,13},{13,1},{2,6},{6,10},{... | collective-permute-start | bytes 983048 | tf_op jit(solution)/shard_map/ppermute | solution.py:321
  125.8 13.0 %collective-permute-start.10 = (bf16[640,256]{1,0:T(8,128)(2,1)S(1)}, bf16[640,256]{1,0:T(8,128)(2,1)S(1)}, u32[]{:S(2)}, u32[]{:S(2)}) collective-permute-start(bf16[640,256]{1,0:T(8,128)(2,1)S(1)} %get-tuple-element.41), channel_id=1, source_target_pairs={{0,12},{4,0},{8,4},{12,8},{1,13},{5,1},{9,5},{13,9},{2,14},{6,2},{... | collective-permute-start | bytes 983048 | tf_op jit(solution)/shard_map/ppermute | solution.py:321
  127.7 11.0 %collective-permute-start.9 = (bf16[640,256]{1,0:T(8,128)(2,1)S(1)}, bf16[640,256]{1,0:T(8,128)(2,1)S(1)}, u32[]{:S(2)}, u32[]{:S(2)}) collective-permute-start(bf16[640,256]{1,0:T(8,128)(2,1)S(1)} %get-tuple-element.42), channel_id=1, source_target_pairs={{0,8},{4,12},{8,0},{12,4},{1,9},{5,13},{9,1},{13,5},{2,10},{6,14},... | collective-permute-start | bytes 983048 | tf_op jit(solution)/shard_map/ppermute | solution.py:321
  138.9 6.2 %collective-permute-start.11 = (bf16[128,256]{1,0:T(8,128)(2,1)S(1)}, bf16[128,256]{1,0:T(8,128)(2,1)S(1)}, u32[]{:S(2)}, u32[]{:S(2)}) collective-permute-start(bf16[128,256]{1,0:T(8,128)(2,1)S(1)} %slice.138), channel_id=1, source_target_pairs={{0,128},{128,256},{256,384},{144,16},{272,144},{400,272},{1,129},{... | collective-permute-start | bytes 196616 | tf_op jit(solution)/shard_map/ppermute | solution.py:322
  145.9 26.7 %all-to-all-start.3 = ((bf16[16,32,256]{2,1,0:T(8,128)(2,1)}), bf16[16,32,256]{2,1,0:T(8,128)(2,1)S(1)}, u32[]{:S(2)}, u32[]{:S(2)}) async-start(bf16[16,32,256]{2,1,0:T(8,128)(2,1)} %bitcast.25), calls=%async_computation.3 | async-start | bytes 524288 | tf_op jit(solution)/shard_map/all_to_all | solution.py:328

commit v6 on v5

--- a/solution.py
+++ b/solution.py
@@ -40,12 +40,10 @@
 
 def by_two(low, stop, step, carry):
     pairs = (stop - low) // 2
-
-    def both(i, carry):
-        return step(low + 2 * i + 1, step(low + 2 * i, carry))
-
-    carry = lax.fori_loop(0, pairs, both, carry)
-    return lax.fori_loop(low + 2 * pairs, stop, step, carry)
+    carry = lax.fori_loop(
+        0, pairs, lambda i, held: step((low + 2 * i, low + 2 * i + 1), held), carry
+    )
+    return lax.fori_loop(low + 2 * pairs, stop, lambda i, held: step((i,), held), carry)
 
 
 def slot_of(run, side):
@@ -87,22 +85,23 @@
     grad_t = grad.T
     query_code = query_code_ref[run : run + 1, :]
 
-    def forward(block, carry):
+    def forward(blocks, carry):
         total, weighted = carry
-        raw = jnp.dot(keys[block], query_t, preferred_element_type=f32)
-        ratio = jnp.tanh(raw * (SCORE_SCALE / SOFT_CAP))
-        expo = jnp.exp2(ratio * (SOFT_CAP * LOG2_E))
-        gap = query_code - key_code_ref[pl.ds(pl.multiple_of(block * KB, KB), KB), :]
-        seen = (gap >= 0) & (gap < 8 * WINDOW) & ((gap & 7) != 1)
-        expo = jnp.concatenate(
-            [jnp.where(seen, expo[:, :RUN], 0.0), jnp.where(seen, expo[:, RUN:], 0.0)], axis=1
-        )
-        ratios[block - low] = ratio
-        expos[block - low] = expo
-        total = total + jnp.sum(expo, axis=0, keepdims=True)
-        weighted = weighted + jnp.dot(
-            values_t[block], expo.astype(b16), preferred_element_type=f32
-        )
+        raws = [jnp.dot(keys[block], query_t, preferred_element_type=f32) for block in blocks]
+        for block, raw in zip(blocks, raws):
+            ratio = jnp.tanh(raw * (SCORE_SCALE / SOFT_CAP))
+            expo = jnp.exp2(ratio * (SOFT_CAP * LOG2_E))
+            gap = query_code - key_code_ref[pl.ds(pl.multiple_of(block * KB, KB), KB), :]
+            seen = ((gap & -(8 * WINDOW)) == 0) & ((gap & 7) != 1)
+            expo = jnp.concatenate(
+                [jnp.where(seen, expo[:, :RUN], 0.0), jnp.where(seen, expo[:, RUN:], 0.0)], axis=1
+            )
+            ratios[block - low] = ratio
+            expos[block - low] = expo
+            total = total + jnp.sum(expo, axis=0, keepdims=True)
+            weighted = weighted + jnp.dot(
+                values_t[block], expo.astype(b16), preferred_element_type=f32
+            )
         return total, weighted
 
     total, weighted = by_two(
@@ -112,16 +111,18 @@
     scale = jnp.where(total > 0.0, 1.0 / total, 0.0)
     delta = jnp.sum(grad_t.astype(f32) * weighted, axis=0, keepdims=True) * scale
 
-    def backward(block, dq_t):
-        ratio = ratios[block - low]
-        prob = expos[block - low] * scale
-        dprob = jnp.dot(values[block], grad_t, preferred_element_type=f32)
-        dscore = prob * (dprob - delta) * ((1.0 - ratio * ratio) * SCORE_SCALE)
-        dscore = dscore.astype(b16)
-        dq_t = dq_t + jnp.dot(keys_t[block], dscore, preferred_element_type=f32)
-        dk = jnp.dot(dscore, query, preferred_element_type=f32)
-        dv = jnp.dot(prob.astype(b16), grad, preferred_element_type=f32)
-        sums[block] = sums[block] + jnp.concatenate([dk, dv], axis=1)
+    def backward(blocks, dq_t):
+        dprobs = [jnp.dot(values[block], grad_t, preferred_element_type=f32) for block in blocks]
+        pairs = []
+        for block, dprob in zip(blocks, dprobs):
+            ratio = ratios[block - low]
+            prob = expos[block - low] * scale
+            dscore = prob * (dprob - delta) * ((1.0 - ratio * ratio) * SCORE_SCALE)
+            pairs.append((block, prob.astype(b16), dscore.astype(b16)))
+        for block, prob, dscore in pairs:
+            dq_t = dq_t + jnp.dot(keys_t[block], dscore, preferred_element_type=f32)
+            sums[block, :, :HEAD_DIM] += jnp.dot(dscore, query, preferred_element_type=f32)
+            sums[block, :, HEAD_DIM:] += jnp.dot(prob, grad, preferred_element_type=f32)
         return dq_t
 
     dq_t = by_two(low, high + 1, backward, jnp.zeros((HEAD_DIM, 2 * RUN), f32))
@@ -291,11 +292,11 @@
     shape = jax.ShapeDtypeStruct
     dq_first, first_sums = call_runs(
         attend_first,
-        (shape((HALF * RUN, 256), b16), shape(sums_shape, f32)), (*common, qg), (), 12,
+        (shape((HALF * RUN, 256), b16), shape(sums_shape, f32)), (*common, qg), (), 16,
     )
     dq_tail, tail_sums = call_runs(
         attend_tail,
-        (shape((RUN, 256), b16), shape(sums_shape, f32)), (*common, tail), (), 12,
+        (shape((RUN, 256), b16), shape(sums_shape, f32)), (*common, tail), (), 16,
     )
     dq_tail = lax.ppermute(dq_tail, ("x", "core"), [(b, a) for a, b in tails])
     dq_last, mine, other = call_runs(
@@ -305,7 +306,7 @@
             shape((Y, RUNS * RUN, 256), b16),
             shape((Y, RUNS * RUN, 256), b16),
         ),
-        (*common, qg, first_sums, tail_sums), (pltpu.VMEM(sums_shape, f32),), 18,
+        (*common, qg, first_sums, tail_sums), (pltpu.VMEM(sums_shape, f32),), 22,
     )
 
     other = lax.ppermute(other, "core", ring(CORE, 1))

time: 175 us -> 173 us (0.989)
  Pallas kernels: 22 us -> 19.9 us
    pallas_call x3, Pallas kernels: 19.1 us -> 17.1 us  [call_runs(): pl.pallas_call(kernel, out_shape=out_shape, in_specs=[pl.BlockSpec(memory...]
where the time goes in v6:
time: 173 us; the launch traced here: 172 us
  starting transfers between devices  81.3 us (47%)
  waiting for transfers between devices  56.4 us (33%)
  Pallas kernels  19.9 us (12%)
  other arithmetic  6.67 us (4%)
  local copies, waits for them, and re-layouts  6.59 us (4%)
    pallas_call x3, Pallas kernels, call_runs(): pl.pallas_call(kernel, out_shape=out_shape, in_specs=[pl.BlockSpec(memory...  17.1 us
    all_to_all x1, starting transfers between devices, local(): kv = lax.all_to_all(kv, z, split_axis=0, concat_axis=0, tiled=True)  15.2 us
    all_to_all x1, waiting for transfers between devices, local(): dkv = lax.all_to_all(dkv, z, split_axis=0, concat_axis=0, tiled=True)  13.9 us
    all_to_all x1, waiting for transfers between devices, local(): kv = lax.all_to_all(kv, z, split_axis=0, concat_axis=0, tiled=True)  13.7 us
    ppermute x3, starting transfers between devices, local(): total = total + lax.ppermute(sent[dy - 1], 'y', ring(Y, dy)).astype(f32)  12.8 us
    all_to_all x1, starting transfers between devices, local(): dq = lax.all_to_all(dq, z, split_axis=0, concat_axis=0, tiled=True)  12.3 us
    all_to_all x1, starting transfers between devices, local(): dkv = lax.all_to_all(dkv, z, split_axis=0, concat_axis=0, tiled=True)  12 us
    ppermute x3, starting transfers between devices, local(): lax.ppermute(five, 'y', ring(Y, -dy))  10 us
  transfers between devices with their start and end apart: 16, of which 12 were waited for; matrix products, arithmetic and copies ran while one was open for 5% of the time, Pallas kernels for 4%

profile of v6, /device:TPU:42, one launch (start us, length us, event | category | flops | bytes accessed | tf_op | source)
XLA Modules:
  0.0 171.9 jit_solution(6066926186786635356)
XLA Ops:
  1.5 1.0 bitcast_bitcast_fusion.2
  3.3 15.2 %all-to-all-start = ((bf16[16,32,256]{2,1,0:T(8,128)(2,1)}), bf16[16,32,256]{2,1,0:T(8,128)(2,1)S(1)}, u32[]{:S(2)}, u32[]{:S(2)}) async-start(bf16[16,32,256]{2,1,0:T(8,128)(2,1)} %pad_maximum_fusion.3), calls=%async_computation | async-start | bytes 524288 | tf_op jit(solution)/shard_map/all_to_all | solution.py:275
  22.7 13.7 %all-to-all-done = bf16[16,32,256]{2,1,0:T(8,128)(2,1)S(1)} async-done(((bf16[16,32,256]{2,1,0:T(8,128)(2,1)}), bf16[16,32,256]{2,1,0:T(8,128)(2,1)S(1)}, u32[]{:S(2)}, u32[]{:S(2)}) %all-to-all-start) | async-done | bytes 262176 | tf_op jit(solution)/shard_map/all_to_all | solution.py:275
  36.4 6.2 %all-to-all-start.1 = ((bf16[16,32,512]{2,1,0:T(8,128)(2,1)}), bf16[16,32,512]{2,1,0:T(8,128)(2,1)S(1)}, u32[]{:S(2)}, u32[]{:S(2)}) async-start(bf16[16,32,512]{2,1,0:T(8,128)(2,1)} %pad_maximum_fusion.1), calls=%async_computation.1 | async-start | bytes 1048576 | tf_op jit(solution)/shard_map/all_to_all | solution.py:279
  42.7 2.4 %collective-permute-start = (bf16[128,256]{1,0:T(8,128)(2,1)S(1)}, bf16[128,256]{1,0:T(8,128)(2,1)S(1)}, u32[]{:S(2)}, u32[]{:S(2)}) collective-permute-start(bf16[128,256]{1,0:T(8,128)(2,1)S(1)} %constant_dynamic-slice_fusion), channel_id=1, source_target_pairs={{128,0},{256,128},{384,256},{16,144},{144,272},{272,400},{129,1},{... | collective-permute-start | bytes 196616 | tf_op jit(solution)/shard_map/ppermute | solution.py:283
  45.1 3.7 %collective-permute-done = bf16[128,256]{1,0:T(8,128)(2,1)S(1)} collective-permute-done((bf16[128,256]{1,0:T(8,128)(2,1)S(1)}, bf16[128,256]{1,0:T(8,128)(2,1)S(1)}, u32[]{:S(2)}, u32[]{:S(2)}) %collective-permute-start) | collective-permute-done | bytes 65568 | tf_op jit(solution)/shard_map/ppermute | solution.py:283
  48.9 4.2 %collective-permute-start.2 = (bf16[640,256]{1,0:T(8,128)(2,1)S(1)}, bf16[640,256]{1,0:T(8,128)(2,1)S(1)}, u32[]{:S(2)}, u32[]{:S(2)}) collective-permute-start(bf16[640,256]{1,0:T(8,128)(2,1)S(1)} %get-tuple-element.44), channel_id=1, source_target_pairs={{0,8},{4,12},{8,0},{12,4},{1,9},{5,13},{9,1},{13,5},{2,10},{6,14},... | collective-permute-start | bytes 983048 | tf_op jit(solution)/shard_map/ppermute | solution.py:285
  53.1 3.3 %collective-permute-start.1 = (bf16[640,256]{1,0:T(8,128)(2,1)S(1)}, bf16[640,256]{1,0:T(8,128)(2,1)S(1)}, u32[]{:S(2)}, u32[]{:S(2)}) collective-permute-start(bf16[640,256]{1,0:T(8,128)(2,1)S(1)} %get-tuple-element.44), channel_id=1, source_target_pairs={{0,12},{4,0},{8,4},{12,8},{1,13},{5,1},{9,5},{13,9},{2,14},{6,2},{... | collective-permute-start | bytes 983048 | tf_op jit(solution)/shard_map/ppermute | solution.py:285
  56.3 2.6 %collective-permute-start.3 = (bf16[640,256]{1,0:T(8,128)(2,1)S(1)}, bf16[640,256]{1,0:T(8,128)(2,1)S(1)}, u32[]{:S(2)}, u32[]{:S(2)}) collective-permute-start(bf16[640,256]{1,0:T(8,128)(2,1)S(1)} %get-tuple-element.44), channel_id=1, source_target_pairs={{0,4},{4,8},{8,12},{12,0},{1,5},{5,9},{9,13},{13,1},{2,6},{6,10},{... | collective-permute-start | bytes 983048 | tf_op jit(solution)/shard_map/ppermute | solution.py:285
  58.9 3.9 %collective-permute-done.2 = bf16[640,256]{1,0:T(8,128)(2,1)S(1)} collective-permute-done((bf16[640,256]{1,0:T(8,128)(2,1)S(1)}, bf16[640,256]{1,0:T(8,128)(2,1)S(1)}, u32[]{:S(2)}, u32[]{:S(2)}) %collective-permute-start.2) | collective-permute-done | bytes 327712 | tf_op jit(solution)/shard_map/ppermute | solution.py:285
  62.9 4.1 %collective-permute-done.1 = bf16[640,256]{1,0:T(8,128)(2,1)S(1)} collective-permute-done((bf16[640,256]{1,0:T(8,128)(2,1)S(1)}, bf16[640,256]{1,0:T(8,128)(2,1)S(1)}, u32[]{:S(2)}, u32[]{:S(2)}) %collective-permute-start.1) | collective-permute-done | bytes 327712 | tf_op jit(solution)/shard_map/ppermute | solution.py:285
  67.1 1.2 pad_maximum_fusion.my_five
  68.3 1.9 %collective-permute-start.4 = (bf16[4,640,256]{2,1,0:T(8,128)(2,1)}, bf16[4,640,256]{2,1,0:T(8,128)(2,1)}, u32[]{:S(2)}, u32[]{:S(2)}) collective-permute-start(bf16[4,640,256]{2,1,0:T(8,128)(2,1)} %pad_maximum_fusion.my_five), channel_id=1, source_target_pairs={{0,16},{16,0},{1,17},{17,1},{2,18},{18,2},{3,19},{19,3},{4,20},{20... | collective-permute-start | bytes 3932168 | tf_op jit(solution)/shard_map/ppermute | solution.py:287
  71.0 2.4 %collective-permute-start.5 = (bf16[128,512]{1,0:T(8,128)(2,1)S(1)}, bf16[128,512]{1,0:T(8,128)(2,1)S(1)}, u32[]{:S(2)}, u32[]{:S(2)}) collective-permute-start(bf16[128,512]{1,0:T(8,128)(2,1)S(1)} %bitcast.134), channel_id=1, source_target_pairs={{128,0},{256,128},{384,256},{129,1},{257,129},{385,257},{130,2},{2... | collective-permute-start | bytes 393224 | tf_op jit(solution)/shard_map/ppermute | solution.py:289
  73.6 2.9 %arrange.1 = (bf16[20,256,128]{2,1,0:T(8,128)(2,1)S(1)}, bf16[20,256,128]{2,1,0:T(8,128)(2,1)S(1)}, bf16[20,128,256]{2,1,0:T(8,128)(2,1)S(1)}, bf16[20,128,256]{2,1,0:T(8,128)(2,1)S(1)}) custom-call(s32[12]{0:T(128)S(1)} %pad_add_fusion.where_ref, bf16[4,640,256]{2,1,0:T(8,128)(2,1)} %pad_maximum_fusion.my_five, ...), custom_call_target="tpu_custom_call" | custom-call | tf_op jit(solution)/shard_map/arrange/pallas_call | solution.py:202
  76.5 3.2 %shard_map.76 = (bf16[256,256]{1,0:T(8,128)(2,1)S(1)}, f32[20,256,256]{2,1,0:T(8,128)S(1)}) custom-call(s32[12]{0:T(128)S(1)} %pad_add_fusion.where_ref, s32[5,128]{1,0:T(8,128)S(1)} %get-tuple-element.19.query_code_ref, s32[5120,128]{1,0:T(8,128)S(1)} %broadcast_in_dim.98.key_code_ref, bf16[20,256,128]{2,1,0:T(8,128)(2,1)S(1)} %get-tuple-element.21.keys, ...), custom_call_target="tpu_custom_call" | custom-call | tf_op jit(solution)/shard_map/pallas_call | solution.py:214
  79.7 5.2 %shard_map.77 = (bf16[128,256]{1,0:T(8,128)(2,1)S(1)}, f32[20,256,256]{2,1,0:T(8,128)S(1)}) custom-call(s32[12]{0:T(128)S(1)} %pad_add_fusion.where_ref, s32[5,128]{1,0:T(8,128)S(1)} %get-tuple-element.19.query_code_ref, s32[5120,128]{1,0:T(8,128)S(1)} %broadcast_in_dim.98.key_code_ref, bf16[20,256,128]{2,1,0:T(8,128)(2,1)S(1)} %get-tuple-element.21.keys, ...), custom_call_target="tpu_custom_call" | custom-call | tf_op jit(solution)/shard_map/pallas_call | solution.py:214
  84.9 8.7 %shard_map.78 = (bf16[256,256]{1,0:T(8,128)(2,1)S(1)}, bf16[4,640,256]{2,1,0:T(8,128)(2,1)S(1)}, bf16[4,640,256]{2,1,0:T(8,128)(2,1)}) custom-call(s32[12]{0:T(128)S(1)} %pad_add_fusion.where_ref, s32[5,128]{1,0:T(8,128)S(1)} %get-tuple-element.19.query_code_ref, s32[5120,128]{1,0:T(8,128)S(1)} %broadcast_in_dim.98.key_code_ref, ...), custom_call_target="tpu_custom_call" | custom-call | tf_op jit(solution)/shard_map/pallas_call | solution.py:214
  93.6 1.1 copy-done.1
  94.6 2.0 %collective-permute-start.7 = (bf16[4,640,256]{2,1,0:T(8,128)(2,1)}, bf16[4,640,256]{2,1,0:T(8,128)(2,1)S(1)}, u32[]{:S(2)}, u32[]{:S(2)}) collective-permute-start(bf16[4,640,256]{2,1,0:T(8,128)(2,1)} %get-tuple-element.32), channel_id=1, source_target_pairs={{0,16},{16,0},{1,17},{17,1},{2,18},{18,2},{3,19},{19,3},{4,20},{20... | collective-permute-start | bytes 3932168 | tf_op jit(solution)/shard_map/ppermute | solution.py:312
  96.7 1.9 %collective-permute-start.6 = (bf16[128,256]{1,0:T(8,128)(2,1)S(1)}, bf16[128,256]{1,0:T(8,128)(2,1)S(1)}, u32[]{:S(2)}, u32[]{:S(2)}) collective-permute-start(bf16[128,256]{1,0:T(8,128)(2,1)S(1)} %get-tuple-element.27), channel_id=1, source_target_pairs={{0,128},{128,256},{256,384},{1,129},{129,257},{257,385},{2,130},{1... | collective-permute-start | bytes 196616 | tf_op jit(solution)/shard_map/ppermute | solution.py:301
  98.6 4.2 %collective-permute-done.6 = bf16[128,256]{1,0:T(8,128)(2,1)S(1)} collective-permute-done((bf16[128,256]{1,0:T(8,128)(2,1)S(1)}, bf16[128,256]{1,0:T(8,128)(2,1)S(1)}, u32[]{:S(2)}, u32[]{:S(2)}) %collective-permute-start.6) | collective-permute-done | bytes 65568 | tf_op jit(solution)/shard_map/ppermute | solution.py:301
  103.6 12.3 %all-to-all-start.2 = ((bf16[16,32,256]{2,1,0:T(8,128)(2,1)}), bf16[16,32,256]{2,1,0:T(8,128)(2,1)S(1)}, u32[]{:S(2)}, u32[]{:S(2)}) async-start(bf16[16,32,256]{2,1,0:T(8,128)(2,1)} %bitcast.19), calls=%async_computation.2 | async-start | bytes 524288 | tf_op jit(solution)/shard_map/all_to_all | solution.py:316
  116.2 7.5 %collective-permute-start.8 = (bf16[640,256]{1,0:T(8,128)(2,1)S(1)}, bf16[640,256]{1,0:T(8,128)(2,1)S(1)}, u32[]{:S(2)}, u32[]{:S(2)}) collective-permute-start(bf16[640,256]{1,0:T(8,128)(2,1)S(1)} %get-tuple-element.40), channel_id=1, source_target_pairs={{0,4},{4,8},{8,12},{12,0},{1,5},{5,9},{9,13},{13,1},{2,6},{6,10},{... | collective-permute-start | bytes 983048 | tf_op jit(solution)/shard_map/ppermute | solution.py:322
  123.8 1.9 %collective-permute-start.10 = (bf16[640,256]{1,0:T(8,128)(2,1)S(1)}, bf16[640,256]{1,0:T(8,128)(2,1)S(1)}, u32[]{:S(2)}, u32[]{:S(2)}) collective-permute-start(bf16[640,256]{1,0:T(8,128)(2,1)S(1)} %get-tuple-element.41), channel_id=1, source_target_pairs={{0,12},{4,0},{8,4},{12,8},{1,13},{5,1},{9,5},{13,9},{2,14},{6,2},{... | collective-permute-start | bytes 983048 | tf_op jit(solution)/shard_map/ppermute | solution.py:322
  125.7 3.4 %collective-permute-start.9 = (bf16[640,256]{1,0:T(8,128)(2,1)S(1)}, bf16[640,256]{1,0:T(8,128)(2,1)S(1)}, u32[]{:S(2)}, u32[]{:S(2)}) collective-permute-start(bf16[640,256]{1,0:T(8,128)(2,1)S(1)} %get-tuple-element.42), channel_id=1, source_target_pairs={{0,8},{4,12},{8,0},{12,4},{1,9},{5,13},{9,1},{13,5},{2,10},{6,14},... | collective-permute-start | bytes 983048 | tf_op jit(solution)/shard_map/ppermute | solution.py:322
  129.1 2.8 %collective-permute-done.8 = bf16[640,256]{1,0:T(8,128)(2,1)S(1)} collective-permute-done((bf16[640,256]{1,0:T(8,128)(2,1)S(1)}, bf16[640,256]{1,0:T(8,128)(2,1)S(1)}, u32[]{:S(2)}, u32[]{:S(2)}) %collective-permute-start.8) | collective-permute-done | bytes 327712 | tf_op jit(solution)/shard_map/ppermute | solution.py:322
  131.8 4.9 %collective-permute-done.10 = bf16[640,256]{1,0:T(8,128)(2,1)S(1)} collective-permute-done((bf16[640,256]{1,0:T(8,128)(2,1)S(1)}, bf16[640,256]{1,0:T(8,128)(2,1)S(1)}, u32[]{:S(2)}, u32[]{:S(2)}) %collective-permute-start.10) | collective-permute-done | bytes 327712 | tf_op jit(solution)/shard_map/ppermute | solution.py:322
  136.9 1.9 %collective-permute-start.11 = (bf16[128,256]{1,0:T(8,128)(2,1)S(1)}, bf16[128,256]{1,0:T(8,128)(2,1)S(1)}, u32[]{:S(2)}, u32[]{:S(2)}) collective-permute-start(bf16[128,256]{1,0:T(8,128)(2,1)S(1)} %slice.138), channel_id=1, source_target_pairs={{0,128},{128,256},{256,384},{144,16},{272,144},{400,272},{1,129},{... | collective-permute-start | bytes 196616 | tf_op jit(solution)/shard_map/ppermute | solution.py:323
  138.9 4.2 %collective-permute-done.11 = bf16[128,256]{1,0:T(8,128)(2,1)S(1)} collective-permute-done((bf16[128,256]{1,0:T(8,128)(2,1)S(1)}, bf16[128,256]{1,0:T(8,128)(2,1)S(1)}, u32[]{:S(2)}, u32[]{:S(2)}) %collective-permute-start.11) | collective-permute-done | bytes 65568 | tf_op jit(solution)/shard_map/ppermute | solution.py:323
  143.8 12.0 %all-to-all-start.3 = ((bf16[16,32,256]{2,1,0:T(8,128)(2,1)}), bf16[16,32,256]{2,1,0:T(8,128)(2,1)S(1)}, u32[]{:S(2)}, u32[]{:S(2)}) async-start(bf16[16,32,256]{2,1,0:T(8,128)(2,1)} %bitcast.25), calls=%async_computation.3 | async-start | bytes 524288 | tf_op jit(solution)/shard_map/all_to_all | solution.py:329
  156.6 13.9 %all-to-all-done.3 = bf16[16,32,256]{2,1,0:T(8,128)(2,1)S(1)} async-done(((bf16[16,32,256]{2,1,0:T(8,128)(2,1)}), bf16[16,32,256]{2,1,0:T(8,128)(2,1)S(1)}, u32[]{:S(2)}, u32[]{:S(2)}) %all-to-all-start.3) | async-done | bytes 262176 | tf_op jit(solution)/shard_map/all_to_all | solution.py:329
  (60 shorter events, 11.0 us)
Async XLA Ops:
  0.6 0.9 copy-start
  0.6 17.8 %copy-start.5 = (s32[8,4]{0,1:T(4,128)S(1)}, s32[8,4]{0,1:T(4,128)}, u32[]{:S(2)}) copy-start(s32[8,4]{0,1:T(4,128)} %param.9) | copy-start | bytes 388
  0.7 20.2 %copy-start.3 = (bf16[32,4096]{1,0:T(8,128)(2,1)S(1)}, bf16[32,4096]{1,0:T(8,128)(2,1)}, u32[]{:S(2)}) copy-start(bf16[32,4096]{1,0:T(8,128)(2,1)} %param.8) | copy-start | bytes 786436
  1.5 19.3 %copy-start.4 = (bf16[32,4096]{1,0:T(8,128)(2,1)S(1)}, bf16[32,4096]{1,0:T(8,128)(2,1)}, u32[]{:S(2)}) copy-start(bf16[32,4096]{1,0:T(8,128)(2,1)} %param.5) | copy-start | bytes 786436
  3.3 33.1 %all-to-all-start = ((bf16[16,32,256]{2,1,0:T(8,128)(2,1)}), bf16[16,32,256]{2,1,0:T(8,128)(2,1)S(1)}, u32[]{:S(2)}, u32[]{:S(2)}) async-start(bf16[16,32,256]{2,1,0:T(8,128)(2,1)} %pad_maximum_fusion.3), calls=%async_computation | async-start | bytes 524288 | tf_op jit(solution)/shard_map/all_to_all | solution.py:275
  36.4 34.6 %all-to-all-start.1 = ((bf16[16,32,512]{2,1,0:T(8,128)(2,1)}), bf16[16,32,512]{2,1,0:T(8,128)(2,1)S(1)}, u32[]{:S(2)}, u32[]{:S(2)}) async-start(bf16[16,32,512]{2,1,0:T(8,128)(2,1)} %pad_maximum_fusion.1), calls=%async_computation.1 | async-start | bytes 1048576 | tf_op jit(solution)/shard_map/all_to_all | solution.py:279
  42.7 6.2 %collective-permute-start = (bf16[128,256]{1,0:T(8,128)(2,1)S(1)}, bf16[128,256]{1,0:T(8,128)(2,1)S(1)}, u32[]{:S(2)}, u32[]{:S(2)}) collective-permute-start(bf16[128,256]{1,0:T(8,128)(2,1)S(1)} %constant_dynamic-slice_fusion), channel_id=1, source_target_pairs={{128,0},{256,128},{384,256},{16,144},{144,272},{272,400},{129,1},{... | collective-permute-start | bytes 196616 | tf_op jit(solution)/shard_map/ppermute | solution.py:283
  48.9 14.0 %collective-permute-start.2 = (bf16[640,256]{1,0:T(8,128)(2,1)S(1)}, bf16[640,256]{1,0:T(8,128)(2,1)S(1)}, u32[]{:S(2)}, u32[]{:S(2)}) collective-permute-start(bf16[640,256]{1,0:T(8,128)(2,1)S(1)} %get-tuple-element.44), channel_id=1, source_target_pairs={{0,8},{4,12},{8,0},{12,4},{1,9},{5,13},{9,1},{13,5},{2,10},{6,14},... | collective-permute-start | bytes 983048 | tf_op jit(solution)/shard_map/ppermute | solution.py:285
  53.1 13.9 %collective-permute-start.1 = (bf16[640,256]{1,0:T(8,128)(2,1)S(1)}, bf16[640,256]{1,0:T(8,128)(2,1)S(1)}, u32[]{:S(2)}, u32[]{:S(2)}) collective-permute-start(bf16[640,256]{1,0:T(8,128)(2,1)S(1)} %get-tuple-element.44), channel_id=1, source_target_pairs={{0,12},{4,0},{8,4},{12,8},{1,13},{5,1},{9,5},{13,9},{2,14},{6,2},{... | collective-permute-start | bytes 983048 | tf_op jit(solution)/shard_map/ppermute | solution.py:285
  56.3 10.7 %collective-permute-start.3 = (bf16[640,256]{1,0:T(8,128)(2,1)S(1)}, bf16[640,256]{1,0:T(8,128)(2,1)S(1)}, u32[]{:S(2)}, u32[]{:S(2)}) collective-permute-start(bf16[640,256]{1,0:T(8,128)(2,1)S(1)} %get-tuple-element.44), channel_id=1, source_target_pairs={{0,4},{4,8},{8,12},{12,0},{1,5},{5,9},{9,13},{13,1},{2,6},{6,10},{... | collective-permute-start | bytes 983048 | tf_op jit(solution)/shard_map/ppermute | solution.py:285
  68.3 5.3 %collective-permute-start.4 = (bf16[4,640,256]{2,1,0:T(8,128)(2,1)}, bf16[4,640,256]{2,1,0:T(8,128)(2,1)}, u32[]{:S(2)}, u32[]{:S(2)}) collective-permute-start(bf16[4,640,256]{2,1,0:T(8,128)(2,1)} %pad_maximum_fusion.my_five), channel_id=1, source_target_pairs={{0,16},{16,0},{1,17},{17,1},{2,18},{18,2},{3,19},{19,3},{4,20},{20... | collective-permute-start | bytes 3932168 | tf_op jit(solution)/shard_map/ppermute | solution.py:287
  71.0 8.6 %collective-permute-start.5 = (bf16[128,512]{1,0:T(8,128)(2,1)S(1)}, bf16[128,512]{1,0:T(8,128)(2,1)S(1)}, u32[]{:S(2)}, u32[]{:S(2)}) collective-permute-start(bf16[128,512]{1,0:T(8,128)(2,1)S(1)} %bitcast.134), channel_id=1, source_target_pairs={{128,0},{256,128},{384,256},{129,1},{257,129},{385,257},{130,2},{2... | collective-permute-start | bytes 393224 | tf_op jit(solution)/shard_map/ppermute | solution.py:289
  93.6 1.1 copy-start.1
  94.6 21.3 %copy-start.2 = (bf16[4,640,256]{2,1,0:T(8,128)(2,1)S(1)}, bf16[4,640,256]{2,1,0:T(8,128)(2,1)}, u32[]{:S(2)}) copy-start(bf16[4,640,256]{2,1,0:T(8,128)(2,1)} %copy-done.1) | copy-start | bytes 3932164
  94.6 21.3 %collective-permute-start.7 = (bf16[4,640,256]{2,1,0:T(8,128)(2,1)}, bf16[4,640,256]{2,1,0:T(8,128)(2,1)S(1)}, u32[]{:S(2)}, u32[]{:S(2)}) collective-permute-start(bf16[4,640,256]{2,1,0:T(8,128)(2,1)} %get-tuple-element.32), channel_id=1, source_target_pairs={{0,16},{16,0},{1,17},{17,1},{2,18},{18,2},{3,19},{19,3},{4,20},{20... | collective-permute-start | bytes 3932168 | tf_op jit(solution)/shard_map/ppermute | solution.py:312
  96.7 6.2 %collective-permute-start.6 = (bf16[128,256]{1,0:T(8,128)(2,1)S(1)}, bf16[128,256]{1,0:T(8,128)(2,1)S(1)}, u32[]{:S(2)}, u32[]{:S(2)}) collective-permute-start(bf16[128,256]{1,0:T(8,128)(2,1)S(1)} %get-tuple-element.27), channel_id=1, source_target_pairs={{0,128},{128,256},{256,384},{1,129},{129,257},{257,385},{2,130},{1... | collective-permute-start | bytes 196616 | tf_op jit(solution)/shard_map/ppermute | solution.py:301
  103.6 40.3 %all-to-all-start.2 = ((bf16[16,32,256]{2,1,0:T(8,128)(2,1)}), bf16[16,32,256]{2,1,0:T(8,128)(2,1)S(1)}, u32[]{:S(2)}, u32[]{:S(2)}) async-start(bf16[16,32,256]{2,1,0:T(8,128)(2,1)} %bitcast.19), calls=%async_computation.2 | async-start | bytes 524288 | tf_op jit(solution)/shard_map/all_to_all | solution.py:316
  116.2 15.6 %collective-permute-start.8 = (bf16[640,256]{1,0:T(8,128)(2,1)S(1)}, bf16[640,256]{1,0:T(8,128)(2,1)S(1)}, u32[]{:S(2)}, u32[]{:S(2)}) collective-permute-start(bf16[640,256]{1,0:T(8,128)(2,1)S(1)} %get-tuple-element.40), channel_id=1, source_target_pairs={{0,4},{4,8},{8,12},{12,0},{1,5},{5,9},{9,13},{13,1},{2,6},{6,10},{... | collective-permute-start | bytes 983048 | tf_op jit(solution)/shard_map/ppermute | solution.py:322
  123.8 13.0 %collective-permute-start.10 = (bf16[640,256]{1,0:T(8,128)(2,1)S(1)}, bf16[640,256]{1,0:T(8,128)(2,1)S(1)}, u32[]{:S(2)}, u32[]{:S(2)}) collective-permute-start(bf16[640,256]{1,0:T(8,128)(2,1)S(1)} %get-tuple-element.41), channel_id=1, source_target_pairs={{0,12},{4,0},{8,4},{12,8},{1,13},{5,1},{9,5},{13,9},{2,14},{6,2},{... | collective-permute-start | bytes 983048 | tf_op jit(solution)/shard_map/ppermute | solution.py:322
  125.7 11.0 %collective-permute-start.9 = (bf16[640,256]{1,0:T(8,128)(2,1)S(1)}, bf16[640,256]{1,0:T(8,128)(2,1)S(1)}, u32[]{:S(2)}, u32[]{:S(2)}) collective-permute-start(bf16[640,256]{1,0:T(8,128)(2,1)S(1)} %get-tuple-element.42), channel_id=1, source_target_pairs={{0,8},{4,12},{8,0},{12,4},{1,9},{5,13},{9,1},{13,5},{2,10},{6,14},... | collective-permute-start | bytes 983048 | tf_op jit(solution)/shard_map/ppermute | solution.py:322
  136.9 6.2 %collective-permute-start.11 = (bf16[128,256]{1,0:T(8,128)(2,1)S(1)}, bf16[128,256]{1,0:T(8,128)(2,1)S(1)}, u32[]{:S(2)}, u32[]{:S(2)}) collective-permute-start(bf16[128,256]{1,0:T(8,128)(2,1)S(1)} %slice.138), channel_id=1, source_target_pairs={{0,128},{128,256},{256,384},{144,16},{272,144},{400,272},{1,129},{... | collective-permute-start | bytes 196616 | tf_op jit(solution)/shard_map/ppermute | solution.py:323
  143.8 26.7 %all-to-all-start.3 = ((bf16[16,32,256]{2,1,0:T(8,128)(2,1)}), bf16[16,32,256]{2,1,0:T(8,128)(2,1)S(1)}, u32[]{:S(2)}, u32[]{:S(2)}) async-start(bf16[16,32,256]{2,1,0:T(8,128)(2,1)} %bitcast.25), calls=%async_computation.3 | async-start | bytes 524288 | tf_op jit(solution)/shard_map/all_to_all | solution.py:329

commit v7 on v6

--- a/solution.py
+++ b/solution.py
@@ -16,7 +16,6 @@
 SLAB = 4096
 RUN = 128
 RUNS = ZH + 1
-HALF = ZH // 2
 SLOTS = 2 * RUNS
 KB = 256
 BLOCKS = SLOTS * 512 // KB
@@ -130,27 +129,7 @@
     dq_ref[out, 128:256] = dq_t[:, RUN:].T.astype(b16)
 
 
-def attend_tail(
-    where_ref, query_code_ref, key_code_ref, keys, values, keys_t, values_t, tail_ref,
-    dq_ref, sums,
-    ratios, expos,
-):
-    refs = (where_ref, query_code_ref, key_code_ref, keys, values, keys_t, values_t)
-    whole = slice(0, RUN)
-    for block in range(BLOCKS):
-        sums[block] = jnp.zeros((KB, 2 * HEAD_DIM), jnp.float32)
-    core = where_ref[2 * RUNS + 1]
-
-    @pl.when(core == 0)
-    def _():
-        one_run(ZH, tail_ref, whole, refs, dq_ref, whole, ratios, expos, sums)
-
-    @pl.when(core != 0)
-    def _():
-        dq_ref[...] = jnp.zeros((RUN, 256), jnp.bfloat16)
-
-
-def attend_first(
+def attend_main(
     where_ref, query_code_ref, key_code_ref, keys, values, keys_t, values_t, qg_ref,
     dq_ref, sums,
     ratios, expos,
@@ -159,14 +138,13 @@
     for block in range(BLOCKS):
         sums[block] = jnp.zeros((KB, 2 * HEAD_DIM), jnp.float32)
 
-    for run in range(HALF):
+    for run in range(ZH):
         rows = slice(run * RUN, (run + 1) * RUN)
         one_run(run, qg_ref, rows, refs, dq_ref, rows, ratios, expos, sums)
 
 
-def attend_last(
-    where_ref, query_code_ref, key_code_ref, keys, values, keys_t, values_t, qg_ref,
-    first_sums, tail_sums,
+def attend_tail(
+    where_ref, query_code_ref, key_code_ref, keys, values, keys_t, values_t, tail_ref, main_sums,
     dq_ref, mine_ref, other_ref,
     ratios, expos, sums,
 ):
@@ -174,13 +152,17 @@
     core = where_ref[2 * RUNS + 1]
     b16 = jnp.bfloat16
     refs = (where_ref, query_code_ref, key_code_ref, keys, values, keys_t, values_t)
+    whole = slice(0, RUN)
     for block in range(BLOCKS):
-        sums[block] = first_sums[block] + tail_sums[block]
-
-    for run in range(HALF, ZH):
-        rows = slice(run * RUN, (run + 1) * RUN)
-        out = slice((run - HALF) * RUN, (run - HALF + 1) * RUN)
-        one_run(run, qg_ref, rows, refs, dq_ref, out, ratios, expos, sums)
+        sums[block] = main_sums[block]
+
+    @pl.when(core == 0)
+    def _():
+        one_run(ZH, tail_ref, whole, refs, dq_ref, whole, ratios, expos, sums)
+
+    @pl.when(core != 0)
+    def _():
+        dq_ref[...] = jnp.zeros((RUN, 256), b16)
 
     for dy in range(Y):
         row = (y + dy) % Y
@@ -290,28 +272,24 @@
     common = (where, query_code, key_code, *arranged)
     sums_shape = (BLOCKS, KB, 2 * HEAD_DIM)
     shape = jax.ShapeDtypeStruct
-    dq_first, first_sums = call_runs(
-        attend_first,
-        (shape((HALF * RUN, 256), b16), shape(sums_shape, f32)), (*common, qg), (), 16,
-    )
-    dq_tail, tail_sums = call_runs(
+    dq, main_sums = call_runs(
+        attend_main,
+        (shape((ZH * RUN, 256), b16), shape(sums_shape, f32)), (*common, qg), (), 16,
+    )
+    dq_tail, mine, other = call_runs(
         attend_tail,
-        (shape((RUN, 256), b16), shape(sums_shape, f32)), (*common, tail), (), 16,
-    )
-    dq_tail = lax.ppermute(dq_tail, ("x", "core"), [(b, a) for a, b in tails])
-    dq_last, mine, other = call_runs(
-        attend_last,
         (
-            shape(((ZH - HALF) * RUN, 256), b16),
+            shape((RUN, 256), b16),
             shape((Y, RUNS * RUN, 256), b16),
             shape((Y, RUNS * RUN, 256), b16),
         ),
-        (*common, qg, first_sums, tail_sums), (pltpu.VMEM(sums_shape, f32),), 22,
+        (*common, tail, main_sums), (pltpu.VMEM(sums_shape, f32),), 22,
     )
 
     other = lax.ppermute(other, "core", ring(CORE, 1))
-    dq_home = (dq_first[:RUN].astype(f32) + dq_tail.astype(f32)).astype(b16)
-    dq = jnp.concatenate([dq_home, dq_first[RUN:], dq_last], axis=0)
+    dq_tail = lax.ppermute(dq_tail, ("x", "core"), [(b, a) for a, b in tails])
+    dq_home = (dq[:RUN].astype(f32) + dq_tail.astype(f32)).astype(b16)
+    dq = jnp.concatenate([dq_home, dq[RUN:]], axis=0)
     dq = dq.reshape(HEADS, tokens, 256)
     dq = lax.all_to_all(dq, z, split_axis=0, concat_axis=0, tiled=True)
     grad_query = jnp.transpose(dq, (1, 0, 2)).reshape(tokens, HEADS * 256)

time: 173 us -> 172 us (level)
    pallas_call x3 -> x2, Pallas kernels: 17.1 us -> 16.1 us  [call_runs(): pl.pallas_call(kernel, out_shape=out_shape, in_specs=[pl.BlockSpec(memory...]
  transfers between devices with their start and end apart: 16 -> 16, of which waited for: 12 -> 12; matrix products, arithmetic and copies ran while one was open for 5% -> 5% of each run, Pallas kernels for 4% -> 7%
where the time goes in v7:
time: 172 us; the launch traced here: 171 us
  starting transfers between devices  81.3 us (47%)
  waiting for transfers between devices  56.4 us (33%)
  Pallas kernels  19 us (11%)
  other arithmetic  6.66 us (4%)
  local copies, waits for them, and re-layouts  6.63 us (4%)
    pallas_call x2, Pallas kernels, call_runs(): pl.pallas_call(kernel, out_shape=out_shape, in_specs=[pl.BlockSpec(memory...  16.1 us
    all_to_all x1, starting transfers between devices, local(): kv = lax.all_to_all(kv, z, split_axis=0, concat_axis=0, tiled=True)  15.2 us
    all_to_all x1, waiting for transfers between devices, local(): dkv = lax.all_to_all(dkv, z, split_axis=0, concat_axis=0, tiled=True)  13.9 us
    all_to_all x1, waiting for transfers between devices, local(): kv = lax.all_to_all(kv, z, split_axis=0, concat_axis=0, tiled=True)  13.6 us
    ppermute x3, starting transfers between devices, local(): total = total + lax.ppermute(sent[dy - 1], 'y', ring(Y, dy)).astype(f32)  12.8 us
    all_to_all x1, starting transfers between devices, local(): dq = lax.all_to_all(dq, z, split_axis=0, concat_axis=0, tiled=True)  12.3 us
    all_to_all x1, starting transfers between devices, local(): dkv = lax.all_to_all(dkv, z, split_axis=0, concat_axis=0, tiled=True)  12 us
    ppermute x3, starting transfers between devices, local(): lax.ppermute(five, 'y', ring(Y, -dy))  10 us
  transfers between devices with their start and end apart: 16, of which 12 were waited for; matrix products, arithmetic and copies ran while one was open for 5% of the time, Pallas kernels for 7%

profile of v7, /device:TPU:42, one launch (start us, length us, event | category | flops | bytes accessed | tf_op | source)
XLA Modules:
  0.0 170.9 jit_solution(2137916369959947872)
XLA Ops:
  0.7 0.9 copy-done
  1.5 1.0 bitcast_bitcast_fusion.2
  3.3 15.2 %all-to-all-start = ((bf16[16,32,256]{2,1,0:T(8,128)(2,1)}), bf16[16,32,256]{2,1,0:T(8,128)(2,1)S(1)}, u32[]{:S(2)}, u32[]{:S(2)}) async-start(bf16[16,32,256]{2,1,0:T(8,128)(2,1)} %pad_maximum_fusion.3), calls=%async_computation | async-start | bytes 524288 | tf_op jit(solution)/shard_map/all_to_all | solution.py:257
  22.8 13.6 %all-to-all-done = bf16[16,32,256]{2,1,0:T(8,128)(2,1)S(1)} async-done(((bf16[16,32,256]{2,1,0:T(8,128)(2,1)}), bf16[16,32,256]{2,1,0:T(8,128)(2,1)S(1)}, u32[]{:S(2)}, u32[]{:S(2)}) %all-to-all-start) | async-done | bytes 262176 | tf_op jit(solution)/shard_map/all_to_all | solution.py:257
  36.4 6.2 %all-to-all-start.1 = ((bf16[16,32,512]{2,1,0:T(8,128)(2,1)}), bf16[16,32,512]{2,1,0:T(8,128)(2,1)S(1)}, u32[]{:S(2)}, u32[]{:S(2)}) async-start(bf16[16,32,512]{2,1,0:T(8,128)(2,1)} %pad_maximum_fusion.1), calls=%async_computation.1 | async-start | bytes 1048576 | tf_op jit(solution)/shard_map/all_to_all | solution.py:261
  42.7 2.4 %collective-permute-start = (bf16[128,256]{1,0:T(8,128)(2,1)S(1)}, bf16[128,256]{1,0:T(8,128)(2,1)S(1)}, u32[]{:S(2)}, u32[]{:S(2)}) collective-permute-start(bf16[128,256]{1,0:T(8,128)(2,1)S(1)} %constant_dynamic-slice_fusion), channel_id=1, source_target_pairs={{128,0},{256,128},{384,256},{16,144},{144,272},{272,400},{129,1},{... | collective-permute-start | bytes 196616 | tf_op jit(solution)/shard_map/ppermute | solution.py:265
  45.1 3.7 %collective-permute-done = bf16[128,256]{1,0:T(8,128)(2,1)S(1)} collective-permute-done((bf16[128,256]{1,0:T(8,128)(2,1)S(1)}, bf16[128,256]{1,0:T(8,128)(2,1)S(1)}, u32[]{:S(2)}, u32[]{:S(2)}) %collective-permute-start) | collective-permute-done | bytes 65568 | tf_op jit(solution)/shard_map/ppermute | solution.py:265
  48.9 4.2 %collective-permute-start.2 = (bf16[640,256]{1,0:T(8,128)(2,1)S(1)}, bf16[640,256]{1,0:T(8,128)(2,1)S(1)}, u32[]{:S(2)}, u32[]{:S(2)}) collective-permute-start(bf16[640,256]{1,0:T(8,128)(2,1)S(1)} %get-tuple-element.40), channel_id=1, source_target_pairs={{0,8},{4,12},{8,0},{12,4},{1,9},{5,13},{9,1},{13,5},{2,10},{6,14},... | collective-permute-start | bytes 983048 | tf_op jit(solution)/shard_map/ppermute | solution.py:267
  53.1 3.3 %collective-permute-start.1 = (bf16[640,256]{1,0:T(8,128)(2,1)S(1)}, bf16[640,256]{1,0:T(8,128)(2,1)S(1)}, u32[]{:S(2)}, u32[]{:S(2)}) collective-permute-start(bf16[640,256]{1,0:T(8,128)(2,1)S(1)} %get-tuple-element.40), channel_id=1, source_target_pairs={{0,12},{4,0},{8,4},{12,8},{1,13},{5,1},{9,5},{13,9},{2,14},{6,2},{... | collective-permute-start | bytes 983048 | tf_op jit(solution)/shard_map/ppermute | solution.py:267
  56.3 2.6 %collective-permute-start.3 = (bf16[640,256]{1,0:T(8,128)(2,1)S(1)}, bf16[640,256]{1,0:T(8,128)(2,1)S(1)}, u32[]{:S(2)}, u32[]{:S(2)}) collective-permute-start(bf16[640,256]{1,0:T(8,128)(2,1)S(1)} %get-tuple-element.40), channel_id=1, source_target_pairs={{0,4},{4,8},{8,12},{12,0},{1,5},{5,9},{9,13},{13,1},{2,6},{6,10},{... | collective-permute-start | bytes 983048 | tf_op jit(solution)/shard_map/ppermute | solution.py:267
  58.9 3.9 %collective-permute-done.2 = bf16[640,256]{1,0:T(8,128)(2,1)S(1)} collective-permute-done((bf16[640,256]{1,0:T(8,128)(2,1)S(1)}, bf16[640,256]{1,0:T(8,128)(2,1)S(1)}, u32[]{:S(2)}, u32[]{:S(2)}) %collective-permute-start.2) | collective-permute-done | bytes 327712 | tf_op jit(solution)/shard_map/ppermute | solution.py:267
  62.9 4.1 %collective-permute-done.1 = bf16[640,256]{1,0:T(8,128)(2,1)S(1)} collective-permute-done((bf16[640,256]{1,0:T(8,128)(2,1)S(1)}, bf16[640,256]{1,0:T(8,128)(2,1)S(1)}, u32[]{:S(2)}, u32[]{:S(2)}) %collective-permute-start.1) | collective-permute-done | bytes 327712 | tf_op jit(solution)/shard_map/ppermute | solution.py:267
  67.1 1.3 pad_maximum_fusion.my_five
  68.3 1.9 %collective-permute-start.4 = (bf16[4,640,256]{2,1,0:T(8,128)(2,1)}, bf16[4,640,256]{2,1,0:T(8,128)(2,1)}, u32[]{:S(2)}, u32[]{:S(2)}) collective-permute-start(bf16[4,640,256]{2,1,0:T(8,128)(2,1)} %pad_maximum_fusion.my_five), channel_id=1, source_target_pairs={{0,16},{16,0},{1,17},{17,1},{2,18},{18,2},{3,19},{19,3},{4,20},{20... | collective-permute-start | bytes 3932168 | tf_op jit(solution)/shard_map/ppermute | solution.py:269
  71.0 2.4 %collective-permute-start.5 = (bf16[128,512]{1,0:T(8,128)(2,1)S(1)}, bf16[128,512]{1,0:T(8,128)(2,1)S(1)}, u32[]{:S(2)}, u32[]{:S(2)}) collective-permute-start(bf16[128,512]{1,0:T(8,128)(2,1)S(1)} %bitcast.133), channel_id=1, source_target_pairs={{128,0},{256,128},{384,256},{129,1},{257,129},{385,257},{130,2},{2... | collective-permute-start | bytes 393224 | tf_op jit(solution)/shard_map/ppermute | solution.py:271
  73.6 2.9 %arrange.1 = (bf16[20,256,128]{2,1,0:T(8,128)(2,1)S(1)}, bf16[20,256,128]{2,1,0:T(8,128)(2,1)S(1)}, bf16[20,128,256]{2,1,0:T(8,128)(2,1)S(1)}, bf16[20,128,256]{2,1,0:T(8,128)(2,1)S(1)}) custom-call(s32[12]{0:T(128)S(1)} %pad_add_fusion.where_ref, bf16[4,640,256]{2,1,0:T(8,128)(2,1)} %pad_maximum_fusion.my_five, ...), custom_call_target="tpu_custom_call" | custom-call | tf_op jit(solution)/shard_map/arrange/pallas_call | solution.py:184
  76.5 9.6 %shard_map.76 = (bf16[512,256]{1,0:T(8,128)(2,1)S(1)}, f32[20,256,256]{2,1,0:T(8,128)S(1)}) custom-call(s32[12]{0:T(128)S(1)} %pad_add_fusion.where_ref, s32[5,128]{1,0:T(8,128)S(1)} %get-tuple-element.17.query_code_ref, s32[5120,128]{1,0:T(8,128)S(1)} %broadcast_in_dim.98.key_code_ref, bf16[20,256,128]{2,1,0:T(8,128)(2,1)S(1)} %get-tuple-element.19.keys, ...), custom_call_target="tpu_custom_call" | custom-call | tf_op jit(solution)/shard_map/pallas_call | solution.py:196
  86.1 6.5 %shard_map.77 = (bf16[128,256]{1,0:T(8,128)(2,1)S(1)}, bf16[4,640,256]{2,1,0:T(8,128)(2,1)S(1)}, bf16[4,640,256]{2,1,0:T(8,128)(2,1)}) custom-call(s32[12]{0:T(128)S(1)} %pad_add_fusion.where_ref, s32[5,128]{1,0:T(8,128)S(1)} %get-tuple-element.17.query_code_ref, s32[5120,128]{1,0:T(8,128)S(1)} %broadcast_in_dim.98.key_code_ref, ...), custom_call_target="tpu_custom_call" | custom-call | tf_op jit(solution)/shard_map/pallas_call | solution.py:196
  92.6 1.1 copy-done.1
  93.7 2.0 %collective-permute-start.7 = (bf16[4,640,256]{2,1,0:T(8,128)(2,1)}, bf16[4,640,256]{2,1,0:T(8,128)(2,1)S(1)}, u32[]{:S(2)}, u32[]{:S(2)}) collective-permute-start(bf16[4,640,256]{2,1,0:T(8,128)(2,1)} %get-tuple-element.28), channel_id=1, source_target_pairs={{0,16},{16,0},{1,17},{17,1},{2,18},{18,2},{3,19},{19,3},{4,20},{20... | collective-permute-start | bytes 3932168 | tf_op jit(solution)/shard_map/ppermute | solution.py:289
  95.7 1.9 %collective-permute-start.6 = (bf16[128,256]{1,0:T(8,128)(2,1)S(1)}, bf16[128,256]{1,0:T(8,128)(2,1)S(1)}, u32[]{:S(2)}, u32[]{:S(2)}) collective-permute-start(bf16[128,256]{1,0:T(8,128)(2,1)S(1)} %get-tuple-element.26), channel_id=1, source_target_pairs={{0,128},{128,256},{256,384},{1,129},{129,257},{257,385},{2,130},{1... | collective-permute-start | bytes 196616 | tf_op jit(solution)/shard_map/ppermute | solution.py:290
  97.6 4.2 %collective-permute-done.6 = bf16[128,256]{1,0:T(8,128)(2,1)S(1)} collective-permute-done((bf16[128,256]{1,0:T(8,128)(2,1)S(1)}, bf16[128,256]{1,0:T(8,128)(2,1)S(1)}, u32[]{:S(2)}, u32[]{:S(2)}) %collective-permute-start.6) | collective-permute-done | bytes 65568 | tf_op jit(solution)/shard_map/ppermute | solution.py:290
  102.6 12.3 %all-to-all-start.2 = ((bf16[16,32,256]{2,1,0:T(8,128)(2,1)}), bf16[16,32,256]{2,1,0:T(8,128)(2,1)S(1)}, u32[]{:S(2)}, u32[]{:S(2)}) async-start(bf16[16,32,256]{2,1,0:T(8,128)(2,1)} %bitcast.19), calls=%async_computation.2 | async-start | bytes 524288 | tf_op jit(solution)/shard_map/all_to_all | solution.py:294
  115.2 7.5 %collective-permute-start.8 = (bf16[640,256]{1,0:T(8,128)(2,1)S(1)}, bf16[640,256]{1,0:T(8,128)(2,1)S(1)}, u32[]{:S(2)}, u32[]{:S(2)}) collective-permute-start(bf16[640,256]{1,0:T(8,128)(2,1)S(1)} %get-tuple-element.36), channel_id=1, source_target_pairs={{0,4},{4,8},{8,12},{12,0},{1,5},{5,9},{9,13},{13,1},{2,6},{6,10},{... | collective-permute-start | bytes 983048 | tf_op jit(solution)/shard_map/ppermute | solution.py:300
  122.8 1.9 %collective-permute-start.10 = (bf16[640,256]{1,0:T(8,128)(2,1)S(1)}, bf16[640,256]{1,0:T(8,128)(2,1)S(1)}, u32[]{:S(2)}, u32[]{:S(2)}) collective-permute-start(bf16[640,256]{1,0:T(8,128)(2,1)S(1)} %get-tuple-element.37), channel_id=1, source_target_pairs={{0,12},{4,0},{8,4},{12,8},{1,13},{5,1},{9,5},{13,9},{2,14},{6,2},{... | collective-permute-start | bytes 983048 | tf_op jit(solution)/shard_map/ppermute | solution.py:300
  124.7 3.4 %collective-permute-start.9 = (bf16[640,256]{1,0:T(8,128)(2,1)S(1)}, bf16[640,256]{1,0:T(8,128)(2,1)S(1)}, u32[]{:S(2)}, u32[]{:S(2)}) collective-permute-start(bf16[640,256]{1,0:T(8,128)(2,1)S(1)} %get-tuple-element.38), channel_id=1, source_target_pairs={{0,8},{4,12},{8,0},{12,4},{1,9},{5,13},{9,1},{13,5},{2,10},{6,14},... | collective-permute-start | bytes 983048 | tf_op jit(solution)/shard_map/ppermute | solution.py:300
  128.1 2.8 %collective-permute-done.8 = bf16[640,256]{1,0:T(8,128)(2,1)S(1)} collective-permute-done((bf16[640,256]{1,0:T(8,128)(2,1)S(1)}, bf16[640,256]{1,0:T(8,128)(2,1)S(1)}, u32[]{:S(2)}, u32[]{:S(2)}) %collective-permute-start.8) | collective-permute-done | bytes 327712 | tf_op jit(solution)/shard_map/ppermute | solution.py:300
  130.9 4.9 %collective-permute-done.10 = bf16[640,256]{1,0:T(8,128)(2,1)S(1)} collective-permute-done((bf16[640,256]{1,0:T(8,128)(2,1)S(1)}, bf16[640,256]{1,0:T(8,128)(2,1)S(1)}, u32[]{:S(2)}, u32[]{:S(2)}) %collective-permute-start.10) | collective-permute-done | bytes 327712 | tf_op jit(solution)/shard_map/ppermute | solution.py:300
  136.0 1.9 %collective-permute-start.11 = (bf16[128,256]{1,0:T(8,128)(2,1)S(1)}, bf16[128,256]{1,0:T(8,128)(2,1)S(1)}, u32[]{:S(2)}, u32[]{:S(2)}) collective-permute-start(bf16[128,256]{1,0:T(8,128)(2,1)S(1)} %slice.138), channel_id=1, source_target_pairs={{0,128},{128,256},{256,384},{144,16},{272,144},{400,272},{1,129},{... | collective-permute-start | bytes 196616 | tf_op jit(solution)/shard_map/ppermute | solution.py:301
  137.9 4.2 %collective-permute-done.11 = bf16[128,256]{1,0:T(8,128)(2,1)S(1)} collective-permute-done((bf16[128,256]{1,0:T(8,128)(2,1)S(1)}, bf16[128,256]{1,0:T(8,128)(2,1)S(1)}, u32[]{:S(2)}, u32[]{:S(2)}) %collective-permute-start.11) | collective-permute-done | bytes 65568 | tf_op jit(solution)/shard_map/ppermute | solution.py:301
  142.9 12.0 %all-to-all-start.3 = ((bf16[16,32,256]{2,1,0:T(8,128)(2,1)}), bf16[16,32,256]{2,1,0:T(8,128)(2,1)S(1)}, u32[]{:S(2)}, u32[]{:S(2)}) async-start(bf16[16,32,256]{2,1,0:T(8,128)(2,1)} %bitcast.25), calls=%async_computation.3 | async-start | bytes 524288 | tf_op jit(solution)/shard_map/all_to_all | solution.py:307
  155.6 13.9 %all-to-all-done.3 = bf16[16,32,256]{2,1,0:T(8,128)(2,1)S(1)} async-done(((bf16[16,32,256]{2,1,0:T(8,128)(2,1)}), bf16[16,32,256]{2,1,0:T(8,128)(2,1)S(1)}, u32[]{:S(2)}, u32[]{:S(2)}) %all-to-all-start.3) | async-done | bytes 262176 | tf_op jit(solution)/shard_map/all_to_all | solution.py:307
  (59 shorter events, 10.1 us)
Async XLA Ops:
  0.6 0.9 copy-start
  0.6 17.8 %copy-start.5 = (s32[8,4]{0,1:T(4,128)S(1)}, s32[8,4]{0,1:T(4,128)}, u32[]{:S(2)}) copy-start(s32[8,4]{0,1:T(4,128)} %param.9) | copy-start | bytes 388
  0.7 20.2 %copy-start.3 = (bf16[32,4096]{1,0:T(8,128)(2,1)S(1)}, bf16[32,4096]{1,0:T(8,128)(2,1)}, u32[]{:S(2)}) copy-start(bf16[32,4096]{1,0:T(8,128)(2,1)} %param.8) | copy-start | bytes 786436
  1.5 19.4 %copy-start.4 = (bf16[32,4096]{1,0:T(8,128)(2,1)S(1)}, bf16[32,4096]{1,0:T(8,128)(2,1)}, u32[]{:S(2)}) copy-start(bf16[32,4096]{1,0:T(8,128)(2,1)} %param.5) | copy-start | bytes 786436
  3.3 33.1 %all-to-all-start = ((bf16[16,32,256]{2,1,0:T(8,128)(2,1)}), bf16[16,32,256]{2,1,0:T(8,128)(2,1)S(1)}, u32[]{:S(2)}, u32[]{:S(2)}) async-start(bf16[16,32,256]{2,1,0:T(8,128)(2,1)} %pad_maximum_fusion.3), calls=%async_computation | async-start | bytes 524288 | tf_op jit(solution)/shard_map/all_to_all | solution.py:257
  36.4 34.6 %all-to-all-start.1 = ((bf16[16,32,512]{2,1,0:T(8,128)(2,1)}), bf16[16,32,512]{2,1,0:T(8,128)(2,1)S(1)}, u32[]{:S(2)}, u32[]{:S(2)}) async-start(bf16[16,32,512]{2,1,0:T(8,128)(2,1)} %pad_maximum_fusion.1), calls=%async_computation.1 | async-start | bytes 1048576 | tf_op jit(solution)/shard_map/all_to_all | solution.py:261
  42.7 6.2 %collective-permute-start = (bf16[128,256]{1,0:T(8,128)(2,1)S(1)}, bf16[128,256]{1,0:T(8,128)(2,1)S(1)}, u32[]{:S(2)}, u32[]{:S(2)}) collective-permute-start(bf16[128,256]{1,0:T(8,128)(2,1)S(1)} %constant_dynamic-slice_fusion), channel_id=1, source_target_pairs={{128,0},{256,128},{384,256},{16,144},{144,272},{272,400},{129,1},{... | collective-permute-start | bytes 196616 | tf_op jit(solution)/shard_map/ppermute | solution.py:265
  48.9 14.0 %collective-permute-start.2 = (bf16[640,256]{1,0:T(8,128)(2,1)S(1)}, bf16[640,256]{1,0:T(8,128)(2,1)S(1)}, u32[]{:S(2)}, u32[]{:S(2)}) collective-permute-start(bf16[640,256]{1,0:T(8,128)(2,1)S(1)} %get-tuple-element.40), channel_id=1, source_target_pairs={{0,8},{4,12},{8,0},{12,4},{1,9},{5,13},{9,1},{13,5},{2,10},{6,14},... | collective-permute-start | bytes 983048 | tf_op jit(solution)/shard_map/ppermute | solution.py:267
  53.1 13.9 %collective-permute-start.1 = (bf16[640,256]{1,0:T(8,128)(2,1)S(1)}, bf16[640,256]{1,0:T(8,128)(2,1)S(1)}, u32[]{:S(2)}, u32[]{:S(2)}) collective-permute-start(bf16[640,256]{1,0:T(8,128)(2,1)S(1)} %get-tuple-element.40), channel_id=1, source_target_pairs={{0,12},{4,0},{8,4},{12,8},{1,13},{5,1},{9,5},{13,9},{2,14},{6,2},{... | collective-permute-start | bytes 983048 | tf_op jit(solution)/shard_map/ppermute | solution.py:267
  56.3 10.7 %collective-permute-start.3 = (bf16[640,256]{1,0:T(8,128)(2,1)S(1)}, bf16[640,256]{1,0:T(8,128)(2,1)S(1)}, u32[]{:S(2)}, u32[]{:S(2)}) collective-permute-start(bf16[640,256]{1,0:T(8,128)(2,1)S(1)} %get-tuple-element.40), channel_id=1, source_target_pairs={{0,4},{4,8},{8,12},{12,0},{1,5},{5,9},{9,13},{13,1},{2,6},{6,10},{... | collective-permute-start | bytes 983048 | tf_op jit(solution)/shard_map/ppermute | solution.py:267
  68.3 5.3 %collective-permute-start.4 = (bf16[4,640,256]{2,1,0:T(8,128)(2,1)}, bf16[4,640,256]{2,1,0:T(8,128)(2,1)}, u32[]{:S(2)}, u32[]{:S(2)}) collective-permute-start(bf16[4,640,256]{2,1,0:T(8,128)(2,1)} %pad_maximum_fusion.my_five), channel_id=1, source_target_pairs={{0,16},{16,0},{1,17},{17,1},{2,18},{18,2},{3,19},{19,3},{4,20},{20... | collective-permute-start | bytes 3932168 | tf_op jit(solution)/shard_map/ppermute | solution.py:269
  71.0 15.0 %collective-permute-start.5 = (bf16[128,512]{1,0:T(8,128)(2,1)S(1)}, bf16[128,512]{1,0:T(8,128)(2,1)S(1)}, u32[]{:S(2)}, u32[]{:S(2)}) collective-permute-start(bf16[128,512]{1,0:T(8,128)(2,1)S(1)} %bitcast.133), channel_id=1, source_target_pairs={{128,0},{256,128},{384,256},{129,1},{257,129},{385,257},{130,2},{2... | collective-permute-start | bytes 393224 | tf_op jit(solution)/shard_map/ppermute | solution.py:271
  92.6 1.1 copy-start.1
  93.6 21.3 %copy-start.2 = (bf16[4,640,256]{2,1,0:T(8,128)(2,1)S(1)}, bf16[4,640,256]{2,1,0:T(8,128)(2,1)}, u32[]{:S(2)}) copy-start(bf16[4,640,256]{2,1,0:T(8,128)(2,1)} %copy-done.1) | copy-start | bytes 3932164
  93.7 21.3 %collective-permute-start.7 = (bf16[4,640,256]{2,1,0:T(8,128)(2,1)}, bf16[4,640,256]{2,1,0:T(8,128)(2,1)S(1)}, u32[]{:S(2)}, u32[]{:S(2)}) collective-permute-start(bf16[4,640,256]{2,1,0:T(8,128)(2,1)} %get-tuple-element.28), channel_id=1, source_target_pairs={{0,16},{16,0},{1,17},{17,1},{2,18},{18,2},{3,19},{19,3},{4,20},{20... | collective-permute-start | bytes 3932168 | tf_op jit(solution)/shard_map/ppermute | solution.py:289
  95.7 6.2 %collective-permute-start.6 = (bf16[128,256]{1,0:T(8,128)(2,1)S(1)}, bf16[128,256]{1,0:T(8,128)(2,1)S(1)}, u32[]{:S(2)}, u32[]{:S(2)}) collective-permute-start(bf16[128,256]{1,0:T(8,128)(2,1)S(1)} %get-tuple-element.26), channel_id=1, source_target_pairs={{0,128},{128,256},{256,384},{1,129},{129,257},{257,385},{2,130},{1... | collective-permute-start | bytes 196616 | tf_op jit(solution)/shard_map/ppermute | solution.py:290
  102.6 40.3 %all-to-all-start.2 = ((bf16[16,32,256]{2,1,0:T(8,128)(2,1)}), bf16[16,32,256]{2,1,0:T(8,128)(2,1)S(1)}, u32[]{:S(2)}, u32[]{:S(2)}) async-start(bf16[16,32,256]{2,1,0:T(8,128)(2,1)} %bitcast.19), calls=%async_computation.2 | async-start | bytes 524288 | tf_op jit(solution)/shard_map/all_to_all | solution.py:294
  115.2 15.6 %collective-permute-start.8 = (bf16[640,256]{1,0:T(8,128)(2,1)S(1)}, bf16[640,256]{1,0:T(8,128)(2,1)S(1)}, u32[]{:S(2)}, u32[]{:S(2)}) collective-permute-start(bf16[640,256]{1,0:T(8,128)(2,1)S(1)} %get-tuple-element.36), channel_id=1, source_target_pairs={{0,4},{4,8},{8,12},{12,0},{1,5},{5,9},{9,13},{13,1},{2,6},{6,10},{... | collective-permute-start | bytes 983048 | tf_op jit(solution)/shard_map/ppermute | solution.py:300
  122.8 13.0 %collective-permute-start.10 = (bf16[640,256]{1,0:T(8,128)(2,1)S(1)}, bf16[640,256]{1,0:T(8,128)(2,1)S(1)}, u32[]{:S(2)}, u32[]{:S(2)}) collective-permute-start(bf16[640,256]{1,0:T(8,128)(2,1)S(1)} %get-tuple-element.37), channel_id=1, source_target_pairs={{0,12},{4,0},{8,4},{12,8},{1,13},{5,1},{9,5},{13,9},{2,14},{6,2},{... | collective-permute-start | bytes 983048 | tf_op jit(solution)/shard_map/ppermute | solution.py:300
  124.7 11.0 %collective-permute-start.9 = (bf16[640,256]{1,0:T(8,128)(2,1)S(1)}, bf16[640,256]{1,0:T(8,128)(2,1)S(1)}, u32[]{:S(2)}, u32[]{:S(2)}) collective-permute-start(bf16[640,256]{1,0:T(8,128)(2,1)S(1)} %get-tuple-element.38), channel_id=1, source_target_pairs={{0,8},{4,12},{8,0},{12,4},{1,9},{5,13},{9,1},{13,5},{2,10},{6,14},... | collective-permute-start | bytes 983048 | tf_op jit(solution)/shard_map/ppermute | solution.py:300
  136.0 6.2 %collective-permute-start.11 = (bf16[128,256]{1,0:T(8,128)(2,1)S(1)}, bf16[128,256]{1,0:T(8,128)(2,1)S(1)}, u32[]{:S(2)}, u32[]{:S(2)}) collective-permute-start(bf16[128,256]{1,0:T(8,128)(2,1)S(1)} %slice.138), channel_id=1, source_target_pairs={{0,128},{128,256},{256,384},{144,16},{272,144},{400,272},{1,129},{... | collective-permute-start | bytes 196616 | tf_op jit(solution)/shard_map/ppermute | solution.py:301
  142.9 26.7 %all-to-all-start.3 = ((bf16[16,32,256]{2,1,0:T(8,128)(2,1)}), bf16[16,32,256]{2,1,0:T(8,128)(2,1)S(1)}, u32[]{:S(2)}, u32[]{:S(2)}) async-start(bf16[16,32,256]{2,1,0:T(8,128)(2,1)} %bitcast.25), calls=%async_computation.3 | async-start | bytes 524288 | tf_op jit(solution)/shard_map/all_to_all | solution.py:307
